TPU v7x, 256 devices: a whole 4x4x8 slice. The times are simulated.
256 devices in a mesh: ctx: 32 (over x, z), tp: 8 (over y, core).
Axes of the slice: x: 4, y: 4, z: 8, core: 2. Of those that a mesh axis runs over, the one named last changes fastest.
Arguments:
- x_inputs: bfloat16 [16384, 8192], P('ctx', 'tp'), may hold values from -6 to 6
- state_maps: bfloat16 [16384, 2048], P('ctx', 'tp'), may hold values from -6 to 6
- z_gate: bfloat16 [16384, 8192], P('ctx', 'tp'), may hold values from -6 to 6
- step_raw: float32 [16384, 128], P('ctx', 'tp'), may hold values from -3 to 3
- step_bias: float32 [128], P('tp'), may hold values from -0.5 to 0.5
- decay_log: float32 [128], P('tp'), may hold values from -20 to -2
- skip_gain: float32 [128], P('tp'), may hold values from 0.5 to 1.5
- x_filter: bfloat16 [4, 8192], P(None, 'tp'), may hold values from -3 to 3
- state_filter: bfloat16 [4, 2048], P(None, 'tp'), may hold values from -3 to 3
- norm_gain: float32 [8192], P('tp'), may hold values from 0.1 to 1.9
- out_weight: bfloat16 [8192, 4096], P('tp'), may hold values from -0.0625 to 0.0625
Outputs:
- mixed: bfloat16 [16384, 4096], P(('ctx', 'tp'))
All inputs are finite; a program needn't handle non-finite values.
Results may differ from a plain program's by a relative error of at most 0.017.
Values may be sent and summed in bfloat16 or wider, within the bound.
No kernel may reach another device: no remote copies, remote signals or barrier semaphores. Data moves between devices by JAX's collectives and lax.ppermute only.
A program may use at most 128 MiB of HBM per device.

v0:
```python
import jax
import jax.numpy as jnp
from jax import lax
from jax.sharding import PartitionSpec as P


def shifted(value, axis, steps):
    count = lax.axis_size(axis)
    leading, last = (max(0, -steps), min(count, count - steps))
    return lax.ppermute(value, axis, [(source, source + steps) for source in range(leading, last)])


def causal_conv(padded, filters, length):
    total = jnp.zeros((length, padded.shape[1]), jnp.float32)
    for offset in range(filters.shape[0]):
        total = total + filters[offset].astype(jnp.float32) * padded[
            offset : offset + length
        ].astype(jnp.float32)
    return total


def block_scan(values, b_rows, c_rows, log_decay, step_size, span):
    length, head_count, head_dim = values.shape
    state_size = b_rows.shape[1]
    pieces = length // span
    inputs = (
        values.reshape(pieces, span, head_count, head_dim),
        b_rows.reshape(pieces, span, state_size),
        c_rows.reshape(pieces, span, state_size),
        log_decay.reshape(pieces, span, head_count),
        step_size.reshape(pieces, span, head_count),
    )
    row_ids = lax.broadcasted_iota(jnp.int32, (span, span), 0)
    col_ids = lax.broadcasted_iota(jnp.int32, (span, span), 1)
    causal = (row_ids >= col_ids)[None]

    def advance(carried, piece):
        piece_x, piece_b, piece_c, piece_rate, piece_step = piece
        cumulative = jnp.cumsum(piece_rate, axis=0)
        by_head = cumulative.T
        spread = by_head[:, :, None] - by_head[:, None, :]
        decay = jnp.where(causal, jnp.exp(-jnp.where(causal, spread, 0.0)), 0.0)
        scores = jnp.dot(piece_c, piece_b.T, preferred_element_type=jnp.float32)
        weights = (decay * scores[None] * piece_step.T[:, None, :]).astype(jnp.bfloat16)
        output = jnp.einsum("hts,shp->thp", weights, piece_x, preferred_element_type=jnp.float32)
        rounded = carried.astype(jnp.bfloat16)
        output = (
            output
            + jnp.einsum("tn,hpn->thp", piece_c, rounded, preferred_element_type=jnp.float32)
            * jnp.exp(-cumulative)[:, :, None]
        )
        tail = jnp.exp(-(cumulative[-1][None, :] - cumulative)) * piece_step
        weighted = (tail[:, :, None] * piece_x.astype(jnp.float32)).astype(jnp.bfloat16)
        fresh = jnp.exp(-cumulative[-1])[:, None, None] * carried
        fresh = fresh + jnp.einsum(
            "shp,sn->hpn", weighted, piece_b, preferred_element_type=jnp.float32
        )
        return (fresh, output)

    start_state = jnp.zeros((head_count, head_dim, state_size), jnp.float32)
    final_state, outputs = lax.scan(advance, start_state, inputs)
    return (outputs.reshape(length, head_count, head_dim), final_state)


def on_device(
    x_inputs,
    state_maps,
    z_gate,
    step_raw,
    step_bias,
    decay_log,
    skip_gain,
    x_filter,
    state_filter,
    norm_gain,
    out_weight,
):
    length = x_inputs.shape[0]
    leading = x_filter.shape[0] - 1
    channels = x_inputs.shape[1]
    head_count = step_raw.shape[1]
    head_dim = channels // head_count
    state_size = state_maps.shape[1] // 2
    prev_x, prev_maps = shifted(
        (x_inputs[length - leading :], state_maps[length - leading :]), "ctx", 1
    )
    x_conv = jax.nn.silu(
        causal_conv(jnp.concatenate([prev_x, x_inputs], 0), x_filter, length)
    ).astype(jnp.bfloat16)
    bc_conv = jax.nn.silu(
        causal_conv(jnp.concatenate([prev_maps, state_maps], 0), state_filter, length)
    ).astype(jnp.bfloat16)
    step_size = jax.nn.softplus(step_raw + step_bias)
    log_decay = step_size * jnp.exp(decay_log)
    values = x_conv.reshape(length, head_count, head_dim)
    b_rows = bc_conv[:, :state_size]
    c_rows = bc_conv[:, state_size:]
    local_out, local_state = block_scan(
        values, b_rows, c_rows, log_decay, step_size, min(length, 512)
    )
    block_decay = jnp.exp(-jnp.sum(log_decay, axis=0))
    block_count = lax.axis_size("ctx")

    def relay_turn(index, carry_pair):
        incoming = shifted(carry_pair[1], "ctx", 1)
        return (incoming, block_decay[:, None, None] * incoming + local_state)

    carried, _ = lax.fori_loop(
        0, block_count - 1, relay_turn, (jnp.zeros_like(local_state), local_state)
    )
    cumulative = jnp.cumsum(log_decay, axis=0)
    rounded = carried.astype(jnp.bfloat16)
    output = (
        local_out
        + jnp.einsum("tn,hpn->thp", c_rows, rounded, preferred_element_type=jnp.float32)
        * jnp.exp(-cumulative)[:, :, None]
    )
    output = output + skip_gain[None, :, None] * values.astype(jnp.float32)
    gated = output.reshape(length, channels) * jax.nn.silu(z_gate.astype(jnp.float32))
    scale = lax.rsqrt(jnp.mean(gated * gated, axis=-1, keepdims=True) + 1e-05)
    normed = (gated * scale * norm_gain).astype(jnp.bfloat16)
    return lax.psum_scatter(
        jnp.dot(normed, out_weight, preferred_element_type=jnp.float32).astype(jnp.bfloat16),
        "tp",
        scatter_dimension=0,
        tiled=True,
    )


def solution(mesh):
    return jax.shard_map(
        on_device,
        mesh=mesh,
        in_specs=(
            P("ctx", "tp"),
            P("ctx", "tp"),
            P("ctx", "tp"),
            P("ctx", "tp"),
            P("tp"),
            P("tp"),
            P("tp"),
            P(None, "tp"),
            P(None, "tp"),
            P("tp"),
            P("tp", None),
        ),
        out_specs=P(("ctx", "tp"), None),
        check_vma=False,
    )
```

profile of v0, /device:TPU:2, one launch (start us, length us, event | category | flops | bytes accessed | tf_op | source)
XLA Modules:
  0.0 615.8 jit_solution(4022369503231797724)
XLA Ops:
  34.9 515.5 %while.2 = (s32[]{:T(128)}, f32[16,64,128]{2,1,0:T(8,128)}, f32[16,64,128]{2,1,0:T(8,128)}, f32[16]{0:T(128)S(1)}, f32[16,64,128]{2,1,0:T(8,128)S(1)}, /*index=5*/s32[]{:T(128)}) while((s32[]{:T(128)}, f32[16,64,128]{2,1,0:T(8,128)}, f32[16,64,128]{2,1,0:T(8,128)}, f32[16]{0:T(128)S(1)}, f32[16,64,128]{2,1,0:T(8,128)S(1)}, ...), condition=%wide.region_4.5_spmd, body=%wide.region_3.4_spmd.sunk | while | flops 262146 | bytes 5767369 | solution.py:108
  38.7 13.5 %collective-permute-done = f32[16,64,128]{2,1,0:T(8,128)S(1)} collective-permute-done((f32[16,64,128]{2,1,0:T(8,128)}, f32[16,64,128]{2,1,0:T(8,128)S(1)}, u32[]{:S(2)}, u32[]{:S(2)}) %collective-permute-start) | collective-permute-done | bytes 524320 | tf_op jit(solution)/shard_map/while/body/eval_jaxpr/ppermute | solution.py:10
  55.6 13.9 %collective-permute-done = f32[16,64,128]{2,1,0:T(8,128)S(1)} collective-permute-done((f32[16,64,128]{2,1,0:T(8,128)}, f32[16,64,128]{2,1,0:T(8,128)S(1)}, u32[]{:S(2)}, u32[]{:S(2)}) %collective-permute-start) | collective-permute-done | bytes 524320 | tf_op jit(solution)/shard_map/while/body/eval_jaxpr/ppermute | solution.py:10
  72.4 13.5 %collective-permute-done = f32[16,64,128]{2,1,0:T(8,128)S(1)} collective-permute-done((f32[16,64,128]{2,1,0:T(8,128)}, f32[16,64,128]{2,1,0:T(8,128)S(1)}, u32[]{:S(2)}, u32[]{:S(2)}) %collective-permute-start) | collective-permute-done | bytes 524320 | tf_op jit(solution)/shard_map/while/body/eval_jaxpr/ppermute | solution.py:10
  88.8 12.6 %collective-permute-done = f32[16,64,128]{2,1,0:T(8,128)S(1)} collective-permute-done((f32[16,64,128]{2,1,0:T(8,128)}, f32[16,64,128]{2,1,0:T(8,128)S(1)}, u32[]{:S(2)}, u32[]{:S(2)}) %collective-permute-start) | collective-permute-done | bytes 524320 | tf_op jit(solution)/shard_map/while/body/eval_jaxpr/ppermute | solution.py:10
  104.3 11.7 %collective-permute-done = f32[16,64,128]{2,1,0:T(8,128)S(1)} collective-permute-done((f32[16,64,128]{2,1,0:T(8,128)}, f32[16,64,128]{2,1,0:T(8,128)S(1)}, u32[]{:S(2)}, u32[]{:S(2)}) %collective-permute-start) | collective-permute-done | bytes 524320 | tf_op jit(solution)/shard_map/while/body/eval_jaxpr/ppermute | solution.py:10
  118.9 11.5 %collective-permute-done = f32[16,64,128]{2,1,0:T(8,128)S(1)} collective-permute-done((f32[16,64,128]{2,1,0:T(8,128)}, f32[16,64,128]{2,1,0:T(8,128)S(1)}, u32[]{:S(2)}, u32[]{:S(2)}) %collective-permute-start) | collective-permute-done | bytes 524320 | tf_op jit(solution)/shard_map/while/body/eval_jaxpr/ppermute | solution.py:10
  133.2 11.5 %collective-permute-done = f32[16,64,128]{2,1,0:T(8,128)S(1)} collective-permute-done((f32[16,64,128]{2,1,0:T(8,128)}, f32[16,64,128]{2,1,0:T(8,128)S(1)}, u32[]{:S(2)}, u32[]{:S(2)}) %collective-permute-start) | collective-permute-done | bytes 524320 | tf_op jit(solution)/shard_map/while/body/eval_jaxpr/ppermute | solution.py:10
  147.6 12.4 %collective-permute-done = f32[16,64,128]{2,1,0:T(8,128)S(1)} collective-permute-done((f32[16,64,128]{2,1,0:T(8,128)}, f32[16,64,128]{2,1,0:T(8,128)S(1)}, u32[]{:S(2)}, u32[]{:S(2)}) %collective-permute-start) | collective-permute-done | bytes 524320 | tf_op jit(solution)/shard_map/while/body/eval_jaxpr/ppermute | solution.py:10
  162.9 13.5 %collective-permute-done = f32[16,64,128]{2,1,0:T(8,128)S(1)} collective-permute-done((f32[16,64,128]{2,1,0:T(8,128)}, f32[16,64,128]{2,1,0:T(8,128)S(1)}, u32[]{:S(2)}, u32[]{:S(2)}) %collective-permute-start) | collective-permute-done | bytes 524320 | tf_op jit(solution)/shard_map/while/body/eval_jaxpr/ppermute | solution.py:10
  179.3 14.6 %collective-permute-done = f32[16,64,128]{2,1,0:T(8,128)S(1)} collective-permute-done((f32[16,64,128]{2,1,0:T(8,128)}, f32[16,64,128]{2,1,0:T(8,128)S(1)}, u32[]{:S(2)}, u32[]{:S(2)}) %collective-permute-start) | collective-permute-done | bytes 524320 | tf_op jit(solution)/shard_map/while/body/eval_jaxpr/ppermute | solution.py:10
  196.7 15.7 %collective-permute-done = f32[16,64,128]{2,1,0:T(8,128)S(1)} collective-permute-done((f32[16,64,128]{2,1,0:T(8,128)}, f32[16,64,128]{2,1,0:T(8,128)S(1)}, u32[]{:S(2)}, u32[]{:S(2)}) %collective-permute-start) | collective-permute-done | bytes 524320 | tf_op jit(solution)/shard_map/while/body/eval_jaxpr/ppermute | solution.py:10
  215.3 16.8 %collective-permute-done = f32[16,64,128]{2,1,0:T(8,128)S(1)} collective-permute-done((f32[16,64,128]{2,1,0:T(8,128)}, f32[16,64,128]{2,1,0:T(8,128)S(1)}, u32[]{:S(2)}, u32[]{:S(2)}) %collective-permute-start) | collective-permute-done | bytes 524320 | tf_op jit(solution)/shard_map/while/body/eval_jaxpr/ppermute | solution.py:10
  235.0 16.2 %collective-permute-done = f32[16,64,128]{2,1,0:T(8,128)S(1)} collective-permute-done((f32[16,64,128]{2,1,0:T(8,128)}, f32[16,64,128]{2,1,0:T(8,128)S(1)}, u32[]{:S(2)}, u32[]{:S(2)}) %collective-permute-start) | collective-permute-done | bytes 524320 | tf_op jit(solution)/shard_map/while/body/eval_jaxpr/ppermute | solution.py:10
  254.1 15.4 %collective-permute-done = f32[16,64,128]{2,1,0:T(8,128)S(1)} collective-permute-done((f32[16,64,128]{2,1,0:T(8,128)}, f32[16,64,128]{2,1,0:T(8,128)S(1)}, u32[]{:S(2)}, u32[]{:S(2)}) %collective-permute-start) | collective-permute-done | bytes 524320 | tf_op jit(solution)/shard_map/while/body/eval_jaxpr/ppermute | solution.py:10
  272.4 14.5 %collective-permute-done = f32[16,64,128]{2,1,0:T(8,128)S(1)} collective-permute-done((f32[16,64,128]{2,1,0:T(8,128)}, f32[16,64,128]{2,1,0:T(8,128)S(1)}, u32[]{:S(2)}, u32[]{:S(2)}) %collective-permute-start) | collective-permute-done | bytes 524320 | tf_op jit(solution)/shard_map/while/body/eval_jaxpr/ppermute | solution.py:10
  289.8 13.6 %collective-permute-done = f32[16,64,128]{2,1,0:T(8,128)S(1)} collective-permute-done((f32[16,64,128]{2,1,0:T(8,128)}, f32[16,64,128]{2,1,0:T(8,128)S(1)}, u32[]{:S(2)}, u32[]{:S(2)}) %collective-permute-start) | collective-permute-done | bytes 524320 | tf_op jit(solution)/shard_map/while/body/eval_jaxpr/ppermute | solution.py:10
  306.2 12.6 %collective-permute-done = f32[16,64,128]{2,1,0:T(8,128)S(1)} collective-permute-done((f32[16,64,128]{2,1,0:T(8,128)}, f32[16,64,128]{2,1,0:T(8,128)S(1)}, u32[]{:S(2)}, u32[]{:S(2)}) %collective-permute-start) | collective-permute-done | bytes 524320 | tf_op jit(solution)/shard_map/while/body/eval_jaxpr/ppermute | solution.py:10
  321.7 11.7 %collective-permute-done = f32[16,64,128]{2,1,0:T(8,128)S(1)} collective-permute-done((f32[16,64,128]{2,1,0:T(8,128)}, f32[16,64,128]{2,1,0:T(8,128)S(1)}, u32[]{:S(2)}, u32[]{:S(2)}) %collective-permute-start) | collective-permute-done | bytes 524320 | tf_op jit(solution)/shard_map/while/body/eval_jaxpr/ppermute | solution.py:10
  336.3 11.5 %collective-permute-done = f32[16,64,128]{2,1,0:T(8,128)S(1)} collective-permute-done((f32[16,64,128]{2,1,0:T(8,128)}, f32[16,64,128]{2,1,0:T(8,128)S(1)}, u32[]{:S(2)}, u32[]{:S(2)}) %collective-permute-start) | collective-permute-done | bytes 524320 | tf_op jit(solution)/shard_map/while/body/eval_jaxpr/ppermute | solution.py:10
  350.6 11.5 %collective-permute-done = f32[16,64,128]{2,1,0:T(8,128)S(1)} collective-permute-done((f32[16,64,128]{2,1,0:T(8,128)}, f32[16,64,128]{2,1,0:T(8,128)S(1)}, u32[]{:S(2)}, u32[]{:S(2)}) %collective-permute-start) | collective-permute-done | bytes 524320 | tf_op jit(solution)/shard_map/while/body/eval_jaxpr/ppermute | solution.py:10
  365.0 12.4 %collective-permute-done = f32[16,64,128]{2,1,0:T(8,128)S(1)} collective-permute-done((f32[16,64,128]{2,1,0:T(8,128)}, f32[16,64,128]{2,1,0:T(8,128)S(1)}, u32[]{:S(2)}, u32[]{:S(2)}) %collective-permute-start) | collective-permute-done | bytes 524320 | tf_op jit(solution)/shard_map/while/body/eval_jaxpr/ppermute | solution.py:10
  380.3 13.5 %collective-permute-done = f32[16,64,128]{2,1,0:T(8,128)S(1)} collective-permute-done((f32[16,64,128]{2,1,0:T(8,128)}, f32[16,64,128]{2,1,0:T(8,128)S(1)}, u32[]{:S(2)}, u32[]{:S(2)}) %collective-permute-start) | collective-permute-done | bytes 524320 | tf_op jit(solution)/shard_map/while/body/eval_jaxpr/ppermute | solution.py:10
  396.7 14.6 %collective-permute-done = f32[16,64,128]{2,1,0:T(8,128)S(1)} collective-permute-done((f32[16,64,128]{2,1,0:T(8,128)}, f32[16,64,128]{2,1,0:T(8,128)S(1)}, u32[]{:S(2)}, u32[]{:S(2)}) %collective-permute-start) | collective-permute-done | bytes 524320 | tf_op jit(solution)/shard_map/while/body/eval_jaxpr/ppermute | solution.py:10
  414.1 15.7 %collective-permute-done = f32[16,64,128]{2,1,0:T(8,128)S(1)} collective-permute-done((f32[16,64,128]{2,1,0:T(8,128)}, f32[16,64,128]{2,1,0:T(8,128)S(1)}, u32[]{:S(2)}, u32[]{:S(2)}) %collective-permute-start) | collective-permute-done | bytes 524320 | tf_op jit(solution)/shard_map/while/body/eval_jaxpr/ppermute | solution.py:10
  432.7 16.8 %collective-permute-done = f32[16,64,128]{2,1,0:T(8,128)S(1)} collective-permute-done((f32[16,64,128]{2,1,0:T(8,128)}, f32[16,64,128]{2,1,0:T(8,128)S(1)}, u32[]{:S(2)}, u32[]{:S(2)}) %collective-permute-start) | collective-permute-done | bytes 524320 | tf_op jit(solution)/shard_map/while/body/eval_jaxpr/ppermute | solution.py:10
  452.4 16.2 %collective-permute-done = f32[16,64,128]{2,1,0:T(8,128)S(1)} collective-permute-done((f32[16,64,128]{2,1,0:T(8,128)}, f32[16,64,128]{2,1,0:T(8,128)S(1)}, u32[]{:S(2)}, u32[]{:S(2)}) %collective-permute-start) | collective-permute-done | bytes 524320 | tf_op jit(solution)/shard_map/while/body/eval_jaxpr/ppermute | solution.py:10
  471.5 15.4 %collective-permute-done = f32[16,64,128]{2,1,0:T(8,128)S(1)} collective-permute-done((f32[16,64,128]{2,1,0:T(8,128)}, f32[16,64,128]{2,1,0:T(8,128)S(1)}, u32[]{:S(2)}, u32[]{:S(2)}) %collective-permute-start) | collective-permute-done | bytes 524320 | tf_op jit(solution)/shard_map/while/body/eval_jaxpr/ppermute | solution.py:10
  489.8 14.5 %collective-permute-done = f32[16,64,128]{2,1,0:T(8,128)S(1)} collective-permute-done((f32[16,64,128]{2,1,0:T(8,128)}, f32[16,64,128]{2,1,0:T(8,128)S(1)}, u32[]{:S(2)}, u32[]{:S(2)}) %collective-permute-start) | collective-permute-done | bytes 524320 | tf_op jit(solution)/shard_map/while/body/eval_jaxpr/ppermute | solution.py:10
  507.1 13.6 %collective-permute-done = f32[16,64,128]{2,1,0:T(8,128)S(1)} collective-permute-done((f32[16,64,128]{2,1,0:T(8,128)}, f32[16,64,128]{2,1,0:T(8,128)S(1)}, u32[]{:S(2)}, u32[]{:S(2)}) %collective-permute-start) | collective-permute-done | bytes 524320 | tf_op jit(solution)/shard_map/while/body/eval_jaxpr/ppermute | solution.py:10
  523.5 11.5 %collective-permute-done = f32[16,64,128]{2,1,0:T(8,128)S(1)} collective-permute-done((f32[16,64,128]{2,1,0:T(8,128)}, f32[16,64,128]{2,1,0:T(8,128)S(1)}, u32[]{:S(2)}, u32[]{:S(2)}) %collective-permute-start) | collective-permute-done | bytes 524320 | tf_op jit(solution)/shard_map/while/body/eval_jaxpr/ppermute | solution.py:10
  572.0 36.9 %reduce-scatter.2.cloned.1.call-done = bf16[64,4096]{1,0:T(8,128)(2,1)} async-done(((bf16[512,4096]{1,0:T(8,128)(2,1)}), bf16[64,4096]{1,0:T(8,128)(2,1)}) %reduce-scatter.2.cloned.1.call-update) | async-done | bytes 524304 | tf_op jit(solution)/shard_map/reduce_scatter | solution.py:122
  (180 shorter events, 152.8 us)
Async XLA Ops:
  6.5 602.4 %reduce-scatter.2.cloned.1.call-start = ((), (), s32[]{:S(2)}) async-start(), calls=%async_computation.1 | async-start | bytes 4718592 | tf_op jit(solution)/shard_map/reduce_scatter | solution.py:122
  7.2 16.1 %collective-permute-start.2 = (bf16[3,256]{1,0:T(4,128)(2,1)S(1)}, bf16[3,256]{1,0:T(4,128)(2,1)S(1)}, u32[]{:S(2)}, u32[]{:S(2)}) collective-permute-start(bf16[3,256]{1,0:T(4,128)(2,1)S(1)} %slice.78), channel_id=1, source_target_pairs={{0,8},{8,16},{16,24},{24,32},{32,40},{40,48},{48,56},{56,64},{64,7... | collective-permute-start | bytes 4616 | tf_op jit(solution)/shard_map/ppermute | solution.py:10
  11.8 14.9 %collective-permute-start.1 = (bf16[3,1024]{1,0:T(4,128)(2,1)S(1)}, bf16[3,1024]{1,0:T(4,128)(2,1)S(1)}, u32[]{:S(2)}, u32[]{:S(2)}) collective-permute-start(bf16[3,1024]{1,0:T(4,128)(2,1)S(1)} %slice.68), channel_id=1, source_target_pairs={{0,8},{8,16},{16,24},{24,32},{32,40},{40,48},{48,56},{56,64},{64,7... | collective-permute-start | bytes 18440 | tf_op jit(solution)/shard_map/ppermute | solution.py:10
  34.9 17.3 %collective-permute-start = (f32[16,64,128]{2,1,0:T(8,128)}, f32[16,64,128]{2,1,0:T(8,128)S(1)}, u32[]{:S(2)}, u32[]{:S(2)}) collective-permute-start(f32[16,64,128]{2,1,0:T(8,128)} %get-tuple-element.121), channel_id=1, source_target_pairs={{0,8},{8,16},{16,24},{24,32},{32,40},{40,48},{48,56},{56,64},{64,7... | collective-permute-start | bytes 1572872 | tf_op jit(solution)/shard_map/while/body/eval_jaxpr/ppermute | solution.py:10
  53.1 16.4 %collective-permute-start = (f32[16,64,128]{2,1,0:T(8,128)}, f32[16,64,128]{2,1,0:T(8,128)S(1)}, u32[]{:S(2)}, u32[]{:S(2)}) collective-permute-start(f32[16,64,128]{2,1,0:T(8,128)} %get-tuple-element.121), channel_id=1, source_target_pairs={{0,8},{8,16},{16,24},{24,32},{32,40},{40,48},{48,56},{56,64},{64,7... | collective-permute-start | bytes 1572872 | tf_op jit(solution)/shard_map/while/body/eval_jaxpr/ppermute | solution.py:10
  70.5 15.5 %collective-permute-start = (f32[16,64,128]{2,1,0:T(8,128)}, f32[16,64,128]{2,1,0:T(8,128)S(1)}, u32[]{:S(2)}, u32[]{:S(2)}) collective-permute-start(f32[16,64,128]{2,1,0:T(8,128)} %get-tuple-element.121), channel_id=1, source_target_pairs={{0,8},{8,16},{16,24},{24,32},{32,40},{40,48},{48,56},{56,64},{64,7... | collective-permute-start | bytes 1572872 | tf_op jit(solution)/shard_map/while/body/eval_jaxpr/ppermute | solution.py:10
  86.9 14.5 %collective-permute-start = (f32[16,64,128]{2,1,0:T(8,128)}, f32[16,64,128]{2,1,0:T(8,128)S(1)}, u32[]{:S(2)}, u32[]{:S(2)}) collective-permute-start(f32[16,64,128]{2,1,0:T(8,128)} %get-tuple-element.121), channel_id=1, source_target_pairs={{0,8},{8,16},{16,24},{24,32},{32,40},{40,48},{48,56},{56,64},{64,7... | collective-permute-start | bytes 1572872 | tf_op jit(solution)/shard_map/while/body/eval_jaxpr/ppermute | solution.py:10
  102.4 13.6 %collective-permute-start = (f32[16,64,128]{2,1,0:T(8,128)}, f32[16,64,128]{2,1,0:T(8,128)S(1)}, u32[]{:S(2)}, u32[]{:S(2)}) collective-permute-start(f32[16,64,128]{2,1,0:T(8,128)} %get-tuple-element.121), channel_id=1, source_target_pairs={{0,8},{8,16},{16,24},{24,32},{32,40},{40,48},{48,56},{56,64},{64,7... | collective-permute-start | bytes 1572872 | tf_op jit(solution)/shard_map/while/body/eval_jaxpr/ppermute | solution.py:10
  117.0 13.4 %collective-permute-start = (f32[16,64,128]{2,1,0:T(8,128)}, f32[16,64,128]{2,1,0:T(8,128)S(1)}, u32[]{:S(2)}, u32[]{:S(2)}) collective-permute-start(f32[16,64,128]{2,1,0:T(8,128)} %get-tuple-element.121), channel_id=1, source_target_pairs={{0,8},{8,16},{16,24},{24,32},{32,40},{40,48},{48,56},{56,64},{64,7... | collective-permute-start | bytes 1572872 | tf_op jit(solution)/shard_map/while/body/eval_jaxpr/ppermute | solution.py:10
  131.3 13.4 %collective-permute-start = (f32[16,64,128]{2,1,0:T(8,128)}, f32[16,64,128]{2,1,0:T(8,128)S(1)}, u32[]{:S(2)}, u32[]{:S(2)}) collective-permute-start(f32[16,64,128]{2,1,0:T(8,128)} %get-tuple-element.121), channel_id=1, source_target_pairs={{0,8},{8,16},{16,24},{24,32},{32,40},{40,48},{48,56},{56,64},{64,7... | collective-permute-start | bytes 1572872 | tf_op jit(solution)/shard_map/while/body/eval_jaxpr/ppermute | solution.py:10
  145.7 14.3 %collective-permute-start = (f32[16,64,128]{2,1,0:T(8,128)}, f32[16,64,128]{2,1,0:T(8,128)S(1)}, u32[]{:S(2)}, u32[]{:S(2)}) collective-permute-start(f32[16,64,128]{2,1,0:T(8,128)} %get-tuple-element.121), channel_id=1, source_target_pairs={{0,8},{8,16},{16,24},{24,32},{32,40},{40,48},{48,56},{56,64},{64,7... | collective-permute-start | bytes 1572872 | tf_op jit(solution)/shard_map/while/body/eval_jaxpr/ppermute | solution.py:10
  161.0 15.4 %collective-permute-start = (f32[16,64,128]{2,1,0:T(8,128)}, f32[16,64,128]{2,1,0:T(8,128)S(1)}, u32[]{:S(2)}, u32[]{:S(2)}) collective-permute-start(f32[16,64,128]{2,1,0:T(8,128)} %get-tuple-element.121), channel_id=1, source_target_pairs={{0,8},{8,16},{16,24},{24,32},{32,40},{40,48},{48,56},{56,64},{64,7... | collective-permute-start | bytes 1572872 | tf_op jit(solution)/shard_map/while/body/eval_jaxpr/ppermute | solution.py:10
  177.4 16.5 %collective-permute-start = (f32[16,64,128]{2,1,0:T(8,128)}, f32[16,64,128]{2,1,0:T(8,128)S(1)}, u32[]{:S(2)}, u32[]{:S(2)}) collective-permute-start(f32[16,64,128]{2,1,0:T(8,128)} %get-tuple-element.121), channel_id=1, source_target_pairs={{0,8},{8,16},{16,24},{24,32},{32,40},{40,48},{48,56},{56,64},{64,7... | collective-permute-start | bytes 1572872 | tf_op jit(solution)/shard_map/while/body/eval_jaxpr/ppermute | solution.py:10
  194.8 17.6 %collective-permute-start = (f32[16,64,128]{2,1,0:T(8,128)}, f32[16,64,128]{2,1,0:T(8,128)S(1)}, u32[]{:S(2)}, u32[]{:S(2)}) collective-permute-start(f32[16,64,128]{2,1,0:T(8,128)} %get-tuple-element.121), channel_id=1, source_target_pairs={{0,8},{8,16},{16,24},{24,32},{32,40},{40,48},{48,56},{56,64},{64,7... | collective-permute-start | bytes 1572872 | tf_op jit(solution)/shard_map/while/body/eval_jaxpr/ppermute | solution.py:10
  213.4 18.7 %collective-permute-start = (f32[16,64,128]{2,1,0:T(8,128)}, f32[16,64,128]{2,1,0:T(8,128)S(1)}, u32[]{:S(2)}, u32[]{:S(2)}) collective-permute-start(f32[16,64,128]{2,1,0:T(8,128)} %get-tuple-element.121), channel_id=1, source_target_pairs={{0,8},{8,16},{16,24},{24,32},{32,40},{40,48},{48,56},{56,64},{64,7... | collective-permute-start | bytes 1572872 | tf_op jit(solution)/shard_map/while/body/eval_jaxpr/ppermute | solution.py:10
  233.1 18.1 %collective-permute-start = (f32[16,64,128]{2,1,0:T(8,128)}, f32[16,64,128]{2,1,0:T(8,128)S(1)}, u32[]{:S(2)}, u32[]{:S(2)}) collective-permute-start(f32[16,64,128]{2,1,0:T(8,128)} %get-tuple-element.121), channel_id=1, source_target_pairs={{0,8},{8,16},{16,24},{24,32},{32,40},{40,48},{48,56},{56,64},{64,7... | collective-permute-start | bytes 1572872 | tf_op jit(solution)/shard_map/while/body/eval_jaxpr/ppermute | solution.py:10
  252.2 17.3 %collective-permute-start = (f32[16,64,128]{2,1,0:T(8,128)}, f32[16,64,128]{2,1,0:T(8,128)S(1)}, u32[]{:S(2)}, u32[]{:S(2)}) collective-permute-start(f32[16,64,128]{2,1,0:T(8,128)} %get-tuple-element.121), channel_id=1, source_target_pairs={{0,8},{8,16},{16,24},{24,32},{32,40},{40,48},{48,56},{56,64},{64,7... | collective-permute-start | bytes 1572872 | tf_op jit(solution)/shard_map/while/body/eval_jaxpr/ppermute | solution.py:10
  270.5 16.4 %collective-permute-start = (f32[16,64,128]{2,1,0:T(8,128)}, f32[16,64,128]{2,1,0:T(8,128)S(1)}, u32[]{:S(2)}, u32[]{:S(2)}) collective-permute-start(f32[16,64,128]{2,1,0:T(8,128)} %get-tuple-element.121), channel_id=1, source_target_pairs={{0,8},{8,16},{16,24},{24,32},{32,40},{40,48},{48,56},{56,64},{64,7... | collective-permute-start | bytes 1572872 | tf_op jit(solution)/shard_map/while/body/eval_jaxpr/ppermute | solution.py:10
  287.8 15.5 %collective-permute-start = (f32[16,64,128]{2,1,0:T(8,128)}, f32[16,64,128]{2,1,0:T(8,128)S(1)}, u32[]{:S(2)}, u32[]{:S(2)}) collective-permute-start(f32[16,64,128]{2,1,0:T(8,128)} %get-tuple-element.121), channel_id=1, source_target_pairs={{0,8},{8,16},{16,24},{24,32},{32,40},{40,48},{48,56},{56,64},{64,7... | collective-permute-start | bytes 1572872 | tf_op jit(solution)/shard_map/while/body/eval_jaxpr/ppermute | solution.py:10
  304.3 14.5 %collective-permute-start = (f32[16,64,128]{2,1,0:T(8,128)}, f32[16,64,128]{2,1,0:T(8,128)S(1)}, u32[]{:S(2)}, u32[]{:S(2)}) collective-permute-start(f32[16,64,128]{2,1,0:T(8,128)} %get-tuple-element.121), channel_id=1, source_target_pairs={{0,8},{8,16},{16,24},{24,32},{32,40},{40,48},{48,56},{56,64},{64,7... | collective-permute-start | bytes 1572872 | tf_op jit(solution)/shard_map/while/body/eval_jaxpr/ppermute | solution.py:10
  319.8 13.6 %collective-permute-start = (f32[16,64,128]{2,1,0:T(8,128)}, f32[16,64,128]{2,1,0:T(8,128)S(1)}, u32[]{:S(2)}, u32[]{:S(2)}) collective-permute-start(f32[16,64,128]{2,1,0:T(8,128)} %get-tuple-element.121), channel_id=1, source_target_pairs={{0,8},{8,16},{16,24},{24,32},{32,40},{40,48},{48,56},{56,64},{64,7... | collective-permute-start | bytes 1572872 | tf_op jit(solution)/shard_map/while/body/eval_jaxpr/ppermute | solution.py:10
  348.7 13.4 %collective-permute-start = (f32[16,64,128]{2,1,0:T(8,128)}, f32[16,64,128]{2,1,0:T(8,128)S(1)}, u32[]{:S(2)}, u32[]{:S(2)}) collective-permute-start(f32[16,64,128]{2,1,0:T(8,128)} %get-tuple-element.121), channel_id=1, source_target_pairs={{0,8},{8,16},{16,24},{24,32},{32,40},{40,48},{48,56},{56,64},{64,7... | collective-permute-start | bytes 1572872 | tf_op jit(solution)/shard_map/while/body/eval_jaxpr/ppermute | solution.py:10
  363.1 14.3 %collective-permute-start = (f32[16,64,128]{2,1,0:T(8,128)}, f32[16,64,128]{2,1,0:T(8,128)S(1)}, u32[]{:S(2)}, u32[]{:S(2)}) collective-permute-start(f32[16,64,128]{2,1,0:T(8,128)} %get-tuple-element.121), channel_id=1, source_target_pairs={{0,8},{8,16},{16,24},{24,32},{32,40},{40,48},{48,56},{56,64},{64,7... | collective-permute-start | bytes 1572872 | tf_op jit(solution)/shard_map/while/body/eval_jaxpr/ppermute | solution.py:10
  378.4 15.4 %collective-permute-start = (f32[16,64,128]{2,1,0:T(8,128)}, f32[16,64,128]{2,1,0:T(8,128)S(1)}, u32[]{:S(2)}, u32[]{:S(2)}) collective-permute-start(f32[16,64,128]{2,1,0:T(8,128)} %get-tuple-element.121), channel_id=1, source_target_pairs={{0,8},{8,16},{16,24},{24,32},{32,40},{40,48},{48,56},{56,64},{64,7... | collective-permute-start | bytes 1572872 | tf_op jit(solution)/shard_map/while/body/eval_jaxpr/ppermute | solution.py:10
  394.7 16.5 %collective-permute-start = (f32[16,64,128]{2,1,0:T(8,128)}, f32[16,64,128]{2,1,0:T(8,128)S(1)}, u32[]{:S(2)}, u32[]{:S(2)}) collective-permute-start(f32[16,64,128]{2,1,0:T(8,128)} %get-tuple-element.121), channel_id=1, source_target_pairs={{0,8},{8,16},{16,24},{24,32},{32,40},{40,48},{48,56},{56,64},{64,7... | collective-permute-start | bytes 1572872 | tf_op jit(solution)/shard_map/while/body/eval_jaxpr/ppermute | solution.py:10
  412.2 17.6 %collective-permute-start = (f32[16,64,128]{2,1,0:T(8,128)}, f32[16,64,128]{2,1,0:T(8,128)S(1)}, u32[]{:S(2)}, u32[]{:S(2)}) collective-permute-start(f32[16,64,128]{2,1,0:T(8,128)} %get-tuple-element.121), channel_id=1, source_target_pairs={{0,8},{8,16},{16,24},{24,32},{32,40},{40,48},{48,56},{56,64},{64,7... | collective-permute-start | bytes 1572872 | tf_op jit(solution)/shard_map/while/body/eval_jaxpr/ppermute | solution.py:10
  430.8 18.7 %collective-permute-start = (f32[16,64,128]{2,1,0:T(8,128)}, f32[16,64,128]{2,1,0:T(8,128)S(1)}, u32[]{:S(2)}, u32[]{:S(2)}) collective-permute-start(f32[16,64,128]{2,1,0:T(8,128)} %get-tuple-element.121), channel_id=1, source_target_pairs={{0,8},{8,16},{16,24},{24,32},{32,40},{40,48},{48,56},{56,64},{64,7... | collective-permute-start | bytes 1572872 | tf_op jit(solution)/shard_map/while/body/eval_jaxpr/ppermute | solution.py:10
  450.4 18.1 %collective-permute-start = (f32[16,64,128]{2,1,0:T(8,128)}, f32[16,64,128]{2,1,0:T(8,128)S(1)}, u32[]{:S(2)}, u32[]{:S(2)}) collective-permute-start(f32[16,64,128]{2,1,0:T(8,128)} %get-tuple-element.121), channel_id=1, source_target_pairs={{0,8},{8,16},{16,24},{24,32},{32,40},{40,48},{48,56},{56,64},{64,7... | collective-permute-start | bytes 1572872 | tf_op jit(solution)/shard_map/while/body/eval_jaxpr/ppermute | solution.py:10
  469.6 17.3 %collective-permute-start = (f32[16,64,128]{2,1,0:T(8,128)}, f32[16,64,128]{2,1,0:T(8,128)S(1)}, u32[]{:S(2)}, u32[]{:S(2)}) collective-permute-start(f32[16,64,128]{2,1,0:T(8,128)} %get-tuple-element.121), channel_id=1, source_target_pairs={{0,8},{8,16},{16,24},{24,32},{32,40},{40,48},{48,56},{56,64},{64,7... | collective-permute-start | bytes 1572872 | tf_op jit(solution)/shard_map/while/body/eval_jaxpr/ppermute | solution.py:10
  487.8 16.4 %collective-permute-start = (f32[16,64,128]{2,1,0:T(8,128)}, f32[16,64,128]{2,1,0:T(8,128)S(1)}, u32[]{:S(2)}, u32[]{:S(2)}) collective-permute-start(f32[16,64,128]{2,1,0:T(8,128)} %get-tuple-element.121), channel_id=1, source_target_pairs={{0,8},{8,16},{16,24},{24,32},{32,40},{40,48},{48,56},{56,64},{64,7... | collective-permute-start | bytes 1572872 | tf_op jit(solution)/shard_map/while/body/eval_jaxpr/ppermute | solution.py:10
  505.2 15.5 %collective-permute-start = (f32[16,64,128]{2,1,0:T(8,128)}, f32[16,64,128]{2,1,0:T(8,128)S(1)}, u32[]{:S(2)}, u32[]{:S(2)}) collective-permute-start(f32[16,64,128]{2,1,0:T(8,128)} %get-tuple-element.121), channel_id=1, source_target_pairs={{0,8},{8,16},{16,24},{24,32},{32,40},{40,48},{48,56},{56,64},{64,7... | collective-permute-start | bytes 1572872 | tf_op jit(solution)/shard_map/while/body/eval_jaxpr/ppermute | solution.py:10
  521.6 13.4 %collective-permute-start = (f32[16,64,128]{2,1,0:T(8,128)}, f32[16,64,128]{2,1,0:T(8,128)S(1)}, u32[]{:S(2)}, u32[]{:S(2)}) collective-permute-start(f32[16,64,128]{2,1,0:T(8,128)} %get-tuple-element.121), channel_id=1, source_target_pairs={{0,8},{8,16},{16,24},{24,32},{32,40},{40,48},{48,56},{56,64},{64,7... | collective-permute-start | bytes 1572872 | tf_op jit(solution)/shard_map/while/body/eval_jaxpr/ppermute | solution.py:10
  (42 other events, 72.0 us)
Sparse Core Ops, SparseCore 0:
  572.1 36.7 reduce-scatter.1
where the time goes:
time: 617 us; the launch traced here: 616 us
  waiting for transfers between devices  461 us (75%)
  starting transfers between devices  69.2 us (11%)
  other arithmetic  42.6 us (7%)
  matrix products  22.2 us (4%)
  between operations  13.5 us (2%)
  local copies, waits for them, and re-layouts  7.38 us (1%)
    ppermute x33, waiting for transfers between devices, shifted(): lax.ppermute(value, axis, [(source, source + steps) for source in range(l...  424 us
    ppermute x33, starting transfers between devices, shifted(): lax.ppermute(value, axis, [(source, source + steps) for source in range(l...  69.2 us
    reduce_scatter x1, waiting for transfers between devices, on_device(): lax.psum_scatter(jnp.dot(normed, out_weight, preferred_element_type=jnp.f...  36.9 us
    add x31, other arithmetic, relay_turn(): return (incoming, block_decay[:, None, None] * incoming + local_state)  29.8 us
  transfers between devices with their start and end apart: 34, of which 32 were waited for; matrix products, arithmetic and copies ran while one was open for 2% of the time, Pallas kernels for 0%

commit v1 on v0

--- a/solution.py
+++ b/solution.py
@@ -98,18 +98,23 @@
     local_out, local_state = block_scan(
         values, b_rows, c_rows, log_decay, step_size, min(length, 512)
     )
-    block_decay = jnp.exp(-jnp.sum(log_decay, axis=0))
     block_count = lax.axis_size("ctx")
+    block_total = jnp.sum(log_decay, axis=0)
+    totals = lax.all_gather(block_total, "ctx", axis=0)
+    slices = local_state.reshape(block_count, -1, state_size).astype(jnp.bfloat16)
+    slices = lax.all_to_all(slices, "ctx", 0, 0, tiled=True).astype(jnp.float32)
+    own = lax.axis_index("ctx") * head_count // block_count
+    decays = jnp.exp(-lax.dynamic_slice_in_dim(totals, own, 1, axis=1))[:, 0]
+    running = jnp.zeros_like(slices[0])
+    entering = []
+    for block in range(block_count):
+        entering.append(running.astype(jnp.bfloat16))
+        running = decays[block] * running + slices[block]
+    carried = lax.all_to_all(jnp.stack(entering), "ctx", 0, 0, tiled=True)
+    carried = carried.reshape(head_count, head_dim, state_size)
 
-    def relay_turn(index, carry_pair):
-        incoming = shifted(carry_pair[1], "ctx", 1)
-        return (incoming, block_decay[:, None, None] * incoming + local_state)
-
-    carried, _ = lax.fori_loop(
-        0, block_count - 1, relay_turn, (jnp.zeros_like(local_state), local_state)
-    )
     cumulative = jnp.cumsum(log_decay, axis=0)
-    rounded = carried.astype(jnp.bfloat16)
+    rounded = carried
     output = (
         local_out
         + jnp.einsum("tn,hpn->thp", c_rows, rounded, preferred_element_type=jnp.float32)

time: 617 us -> 331 us (0.54)
  waiting for transfers between devices: 461 us -> 52.6 us
  blocking collectives: 0 us -> 129 us
  starting transfers between devices: 69.2 us -> 29.9 us
  other arithmetic: 42.6 us -> 72.1 us
    ppermute x33 -> x2, waiting for transfers between devices: 424 us -> 0.01 us  [shifted(): lax.ppermute(value, axis, [(source, source + steps) for source in range(l...]
    unnamed x0 -> x1, blocking collectives: none -> 129 us
    ppermute x33 -> x2, starting transfers between devices: 69.2 us -> 7.63 us  [shifted(): lax.ppermute(value, axis, [(source, source + steps) for source in range(l...]
    unnamed x0 -> x30, other arithmetic: none -> 58.6 us
    add x31 -> x0, other arithmetic: 29.8 us -> none  [relay_turn(): return (incoming, block_decay[:, None, None] * incoming + local_state)]
    all_to_all x0 -> x2, starting transfers between devices: none -> 22.1 us  [the longest x1 16.2 us: on_device(): slices = lax.all_to_all(slices, 'ctx', 0, 0, tiled=True).astype(jnp.float32)]
    all_to_all x0 -> x2, waiting for transfers between devices: none -> 14.9 us  [the longest x1 8.7 us: on_device(): carried = lax.all_to_all(jnp.stack(entering), 'ctx', 0, 0, tiled=True)]
  transfers between devices with their start and end apart: 34 -> 5, of which waited for: 32 -> 3; matrix products, arithmetic and copies ran while one was open for 2% -> 4% of each run, Pallas kernels for 0% -> 0%
where the time goes in v1:
time: 331 us; the launch traced here: 327 us
  blocking collectives  129 us (39%)
  other arithmetic  72.1 us (22%)
  waiting for transfers between devices  52.6 us (16%)
  starting transfers between devices  29.9 us (9%)
  matrix products  20.4 us (6%)
  between operations  15 us (5%)
  local copies, waits for them, and re-layouts  8.5 us (3%)
    unnamed x1, blocking collectives  129 us
    unnamed x30, other arithmetic  58.6 us
    reduce_scatter x1, waiting for transfers between devices, on_device(): lax.psum_scatter(jnp.dot(normed, out_weight, preferred_element_type=jnp.f...  37.7 us
    all_to_all x1, starting transfers between devices, on_device(): slices = lax.all_to_all(slices, 'ctx', 0, 0, tiled=True).astype(jnp.float32)  16.2 us
    dot_general x1, matrix products, on_device(): jnp.dot(normed, out_weight, preferred_element_type=jnp.float32)  10 us
    all_to_all x1, waiting for transfers between devices, on_device(): carried = lax.all_to_all(jnp.stack(entering), 'ctx', 0, 0, tiled=True)  8.7 us
    ppermute x2, starting transfers between devices, shifted(): lax.ppermute(value, axis, [(source, source + steps) for source in range(l...  7.63 us
    dot_general x1, matrix products, advance(): jnp.einsum('hts,shp->thp', weights, piece_x, preferred_element_type=jnp.f...  6.99 us
  transfers between devices with their start and end apart: 5, of which 3 were waited for; matrix products, arithmetic and copies ran while one was open for 4% of the time, Pallas kernels for 0%

profile of v1, /device:TPU:2, one launch (start us, length us, event | category | flops | bytes accessed | tf_op | source)
XLA Modules:
  0.0 327.1 jit_solution(4887845754108709007)
XLA Ops:
  7.2 3.8 %collective-permute-start.1 = (bf16[3,256]{1,0:T(4,128)(2,1)S(1)}, bf16[3,256]{1,0:T(4,128)(2,1)S(1)}, u32[]{:S(2)}, u32[]{:S(2)}) collective-permute-start(bf16[3,256]{1,0:T(4,128)(2,1)S(1)} %slice.295), channel_id=1, source_target_pairs={{0,8},{8,16},{16,24},{24,32},{32,40},{40,48},{48,56},{56,64},{64,7... | collective-permute-start | bytes 4616 | tf_op jit(solution)/shard_map/ppermute | solution.py:10
  11.8 3.8 %collective-permute-start = (bf16[3,1024]{1,0:T(4,128)(2,1)S(1)}, bf16[3,1024]{1,0:T(4,128)(2,1)S(1)}, u32[]{:S(2)}, u32[]{:S(2)}) collective-permute-start(bf16[3,1024]{1,0:T(4,128)(2,1)S(1)} %slice.285), channel_id=1, source_target_pairs={{0,8},{8,16},{16,24},{24,32},{32,40},{40,48},{48,56},{56,64},{64,7... | collective-permute-start | bytes 18440 | tf_op jit(solution)/shard_map/ppermute | solution.py:10
  23.7 128.6 %all-reduce.1 = f32[32,16]{1,0:T(8,128)S(1)} all-reduce(f32[32,16]{1,0:T(8,128)S(1)} %reshape.166), channel_id=2, replica_groups=mesh['ctx'=32,'tp'=8] {'ctx'}, use_global_device_ids=true, to_apply=%add | all-reduce | flops 512 | bytes 4096
  154.1 3.4 %multiply_convert_fusion.3 = bf16[512,1024]{1,0:T(8,128)(2,1)S(1)} fusion(bf16[512,1024]{1,0:T(8,128)(2,1)} %param.11, bf16[3,1024]{1,0:T(4,128)(2,1)S(1)} %collective-permute-done, f32[1024]{0:T(1024)S(1)} %bitcast.91, f32[1024]{0:T(1024)S(1)} %bitcast.92, f32[1024]{0:T(1024)S(1)} %bitcast.90, f32[1024]{0:T(1024)S(1)} %bitcast.89), kind=kLoop, calls=%fused_computation.18 | loop fusion | flops 13107200 | bytes 2119680 | tf_op jit(solution)/shard_map/convert_element_type | solution.py:89
  159.2 16.2 %all-to-all-start = ((bf16[32,32,128]{2,1,0:T(8,128)(2,1)}), bf16[32,32,128]{2,1,0:T(8,128)(2,1)S(1)}, u32[]{:S(2)}, u32[]{:S(2)}) async-start(bf16[32,32,128]{2,1,0:T(8,128)(2,1)} %bitcast.17), calls=%async_computation | async-start | bytes 524288 | tf_op jit(solution)/shard_map/all_to_all | solution.py:105
  178.9 6.2 %all-to-all-done = bf16[32,32,128]{2,1,0:T(8,128)(2,1)S(1)} async-done(((bf16[32,32,128]{2,1,0:T(8,128)(2,1)}), bf16[32,32,128]{2,1,0:T(8,128)(2,1)S(1)}, u32[]{:S(2)}, u32[]{:S(2)}) %all-to-all-start) | async-done | bytes 262176 | tf_op jit(solution)/shard_map/all_to_all | solution.py:105
  188.3 1.9 constant_dynamic-update-slice_fusion.27
  191.5 1.9 constant_dynamic-update-slice_fusion.25
  200.7 2.5 constant_dynamic-update-slice_fusion.19
  203.2 1.9 constant_dynamic-update-slice_fusion.18
  205.1 2.6 constant_dynamic-update-slice_fusion.17
  207.7 1.9 constant_dynamic-update-slice_fusion.16
  209.6 2.6 constant_dynamic-update-slice_fusion.15
  214.0 2.6 constant_dynamic-update-slice_fusion.13
  216.6 1.9 constant_dynamic-update-slice_fusion.12
  218.5 2.6 constant_dynamic-update-slice_fusion.11
  221.1 1.9 constant_dynamic-update-slice_fusion.10
  223.0 2.6 constant_dynamic-update-slice_fusion.9
  225.6 1.9 constant_dynamic-update-slice_fusion.8
  227.6 2.6 constant_dynamic-update-slice_fusion.7
  232.0 2.6 constant_dynamic-update-slice_fusion.5
  234.6 1.9 constant_dynamic-update-slice_fusion.4
  236.5 2.6 constant_dynamic-update-slice_fusion.3
  239.1 2.0 constant_dynamic-update-slice_fusion.2
  241.1 2.6 constant_dynamic-update-slice_fusion.1
  243.7 1.9 constant_dynamic-update-slice_fusion
  245.6 5.9 %all-to-all-start.1 = ((bf16[32,32,128]{2,1,0:T(8,128)(2,1)}), bf16[32,32,128]{2,1,0:T(8,128)(2,1)}, u32[]{:S(2)}, u32[]{:S(2)}) async-start(bf16[32,32,128]{2,1,0:T(8,128)(2,1)} %constant_dynamic-update-slice_fusion), calls=%async_computation.1 | async-start | bytes 524288 | tf_op jit(solution)/shard_map/all_to_all | solution.py:113
  252.5 8.7 %all-to-all-done.1 = bf16[32,32,128]{2,1,0:T(8,128)(2,1)} async-done(((bf16[32,32,128]{2,1,0:T(8,128)(2,1)}), bf16[32,32,128]{2,1,0:T(8,128)(2,1)}, u32[]{:S(2)}, u32[]{:S(2)}) %all-to-all-start.1) | async-done | bytes 262176 | tf_op jit(solution)/shard_map/all_to_all | solution.py:113
  262.7 7.0 %fusion.3 = f32[512,16,64]{0,2,1:T(8,128)} fusion(bf16[512,16,64]{0,2,1:T(8,128)(2,1)S(1)} %bitcast.87, f32[512,16,64]{0,2,1:T(8,128)S(1)} %fusion.19, f32[512,16,64]{0,2,1:T(8,128)S(1)} %fusion.21, f32[16,512]{1,0:T(8,128)S(1)} %get-tuple-element.64, f32[512,512]{1,0:T(8,128)S(1)} %fusion.25, f32[16,512]{1,0:T(8,128)S(1)} %get-tuple-element.67, ...), kind=kOutput, calls=%fused_computation.9 | convolution fusion | flops 569901056 | bytes 8749120 | tf_op jit(solution)/shard_map/while/body/eval_jaxpr/hts,shp->thp/dot_general | solution.py:45
  269.7 2.0 copy.18
  272.5 10.0 %convolution_convert_fusion = bf16[512,4096]{1,0:T(8,128)(2,1)} fusion(bf16[1024,4096]{1,0:T(8,128)(2,1)} %param.21, f32[1024]{0:T(1024)S(1)} %copy-done.5, f32[512]{0:T(512)S(1)} %add_rsqrt_fusion, f32[512,1024]{1,0:T(8,128)S(1)} %copy.18, bf16[512,1024]{1,0:T(8,128)(2,1)S(1)} %copy-done.3), kind=kOutput, calls=%fused_computation.3 | convolution fusion | flops 4301783040 | bytes 15734784 | tf_op jit(solution)/shard_map/dot_general | solution.py:128
  282.5 37.7 %reduce-scatter.2.cloned.1.call-done = bf16[64,4096]{1,0:T(8,128)(2,1)} async-done(((bf16[512,4096]{1,0:T(8,128)(2,1)}), bf16[64,4096]{1,0:T(8,128)(2,1)}) %reduce-scatter.2.cloned.1.call-update) | async-done | bytes 524304 | tf_op jit(solution)/shard_map/reduce_scatter | solution.py:127
  (62 shorter events, 33.7 us)
Async XLA Ops:
  7.2 145.1 %collective-permute-start.1 = (bf16[3,256]{1,0:T(4,128)(2,1)S(1)}, bf16[3,256]{1,0:T(4,128)(2,1)S(1)}, u32[]{:S(2)}, u32[]{:S(2)}) collective-permute-start(bf16[3,256]{1,0:T(4,128)(2,1)S(1)} %slice.295), channel_id=1, source_target_pairs={{0,8},{8,16},{16,24},{24,32},{32,40},{40,48},{48,56},{56,64},{64,7... | collective-permute-start | bytes 4616 | tf_op jit(solution)/shard_map/ppermute | solution.py:10
  11.8 142.3 %collective-permute-start = (bf16[3,1024]{1,0:T(4,128)(2,1)S(1)}, bf16[3,1024]{1,0:T(4,128)(2,1)S(1)}, u32[]{:S(2)}, u32[]{:S(2)}) collective-permute-start(bf16[3,1024]{1,0:T(4,128)(2,1)S(1)} %slice.285), channel_id=1, source_target_pairs={{0,8},{8,16},{16,24},{24,32},{32,40},{40,48},{48,56},{56,64},{64,7... | collective-permute-start | bytes 18440 | tf_op jit(solution)/shard_map/ppermute | solution.py:10
  158.1 42.6 %copy-start.1 = (bf16[512,1024]{0,1:T(8,128)(2,1)}, bf16[512,1024]{0,1:T(8,128)(2,1)S(1)}, u32[]{:S(2)}) copy-start(bf16[512,1024]{0,1:T(8,128)(2,1)S(1)} %copy.15) | copy-start | bytes 3145732
  159.2 25.9 %all-to-all-start = ((bf16[32,32,128]{2,1,0:T(8,128)(2,1)}), bf16[32,32,128]{2,1,0:T(8,128)(2,1)S(1)}, u32[]{:S(2)}, u32[]{:S(2)}) async-start(bf16[32,32,128]{2,1,0:T(8,128)(2,1)} %bitcast.17), calls=%async_computation | async-start | bytes 524288 | tf_op jit(solution)/shard_map/all_to_all | solution.py:105
  185.1 15.6 %copy-start = (f32[32,32,128]{2,1,0:T(8,128)}, f32[32,32,128]{2,1,0:T(8,128)S(1)}, u32[]{:S(2)}) copy-start(f32[32,32,128]{2,1,0:T(8,128)S(1)} %convert_element_type.219) | copy-start | bytes 1572868
  245.6 15.6 %all-to-all-start.1 = ((bf16[32,32,128]{2,1,0:T(8,128)(2,1)}), bf16[32,32,128]{2,1,0:T(8,128)(2,1)}, u32[]{:S(2)}, u32[]{:S(2)}) async-start(bf16[32,32,128]{2,1,0:T(8,128)(2,1)} %constant_dynamic-update-slice_fusion), calls=%async_computation.1 | async-start | bytes 524288 | tf_op jit(solution)/shard_map/all_to_all | solution.py:113
  251.5 68.7 %reduce-scatter.2.cloned.1.call-start = ((), (), s32[]{:S(2)}) async-start(), calls=%async_computation.3 | async-start | bytes 4718592 | tf_op jit(solution)/shard_map/reduce_scatter | solution.py:127
  252.1 10.6 %copy-start.6 = (f32[16]{0:T(128)S(1)}, f32[16]{0:T(128)}, u32[]{:S(2)}) copy-start(f32[16]{0:T(128)} %param.17) | copy-start | bytes 196
  261.2 1.5 copy-start.2
  261.2 1.5 copy-start.4
  269.7 2.0 copy-start.3
  271.7 0.7 copy-start.5
Sparse Core Ops, SparseCore 0:
  282.6 37.5 reduce-scatter.1

commit v2 on v0

v2 whole, which is shorter than its diff:
```python
import functools

import jax
import jax.numpy as jnp
from jax import lax
from jax.experimental import pallas as pl
from jax.experimental.pallas import tpu as pltpu
from jax.sharding import PartitionSpec as P

BF16 = jnp.bfloat16
F32 = jnp.float32
VMEM_LIMIT = 40 * 1024 * 1024


def params(**more):
    return pltpu.CompilerParams(vmem_limit_bytes=VMEM_LIMIT, **more)


def shifted(value, axis, steps):
    count = lax.axis_size(axis)
    leading, last = (max(0, -steps), min(count, count - steps))
    return lax.ppermute(value, axis, [(source, source + steps) for source in range(leading, last)])


def three_parts(value):
    high = value.astype(BF16)
    rest = value - high.astype(F32)
    middle = rest.astype(BF16)
    low = (rest - middle.astype(F32)).astype(BF16)
    return high, middle, low


def packed_parts(value):
    high, middle, low = three_parts(value)
    wide = [high.astype(F32), middle.astype(F32), low.astype(F32)]
    return jnp.concatenate(wide, axis=1).astype(BF16)


def head_selector(first_head, heads, head_dim, width):
    rows = lax.broadcasted_iota(jnp.int32, (3 * heads, width), 0)
    lanes = lax.broadcasted_iota(jnp.int32, (3 * heads, width), 1)
    return (rows % heads == first_head + lanes // head_dim).astype(F32).astype(BF16)


def silu(value):
    return value / (1.0 + jnp.exp(-value))


def conv_rows(padded, taps, start, rows):
    count = taps.shape[0]
    total = None
    for offset in range(count):
        first = 8 - (count - 1) + offset + start
        term = taps[offset : offset + 1] * padded[pl.ds(first, rows), :]
        total = term if total is None else total + term
    return total


def state_kernel(
    heads,
    head_dim,
    x_ref,
    halo_ref,
    x_taps_ref,
    maps_ref,
    maps_halo_ref,
    maps_taps_ref,
    raw_ref,
    bias_ref,
    decay_ref,
    conv_ref,
    maps_conv_ref,
    step_ref,
    total_ref,
    sent_ref,
    padded,
    tail_parts,
    end_parts,
    weighted,
):
    column = pl.program_id(0)
    length, width = x_ref.shape
    leading = halo_ref.shape[0]
    tile = 64
    state = maps_ref.shape[1] // 2

    def fill(source, halo):
        padded[pl.ds(8 - leading, leading), :] = halo[...].astype(F32)
        for start in range(0, length, tile):
            padded[pl.ds(8 + start, tile), :] = source[pl.ds(start, tile), :].astype(F32)

    @pl.when(column == 0)
    def _():
        step = jnp.log1p(jnp.exp(raw_ref[...] + bias_ref[...]))
        step_ref[...] = step
        rate = step * jnp.exp(decay_ref[...])
        piece = 128
        upper = lax.broadcasted_iota(jnp.int32, (piece, piece), 0)
        lower = lax.broadcasted_iota(jnp.int32, (piece, piece), 1)
        triangle = (upper >= lower).astype(F32).astype(BF16)
        before = jnp.zeros((1, heads), F32)
        for start in range(0, length, piece):
            parts = three_parts(rate[start : start + piece])
            sums = [jnp.dot(triangle, part, preferred_element_type=F32) for part in parts]
            block = sums[0] + (sums[1] + sums[2]) + before
            total_ref[pl.ds(start, piece), :] = block
            before = block[piece - 1 : piece]
        end = before
        tail_parts[...] = packed_parts(jnp.exp(total_ref[...] - end) * step)
        end_parts[...] = packed_parts(jnp.broadcast_to(jnp.exp(-end), (8, heads)))
        fill(maps_ref, maps_halo_ref)
        taps = maps_taps_ref[...].astype(F32)
        for start in range(0, length, tile):
            rows = silu(conv_rows(padded, taps, start, tile))
            maps_conv_ref[pl.ds(start, tile), :] = rows.astype(BF16)

    fill(x_ref, halo_ref)
    taps = x_taps_ref[...].astype(F32)
    selector = head_selector(column * (width // head_dim), heads, head_dim, width)
    for start in range(0, length, tile):
        rows = silu(conv_rows(padded, taps, start, tile)).astype(BF16)
        conv_ref[pl.ds(start, tile), :] = rows
        tail = jnp.dot(
            tail_parts[pl.ds(start, tile), :], selector, preferred_element_type=F32
        )
        weighted[pl.ds(start, tile), :] = (tail * rows.astype(F32)).astype(BF16)
    reached = lax.dot_general(
        maps_conv_ref[:, :state],
        weighted[...],
        (((0,), (0,)), ((), ())),
        preferred_element_type=F32,
    )
    factor = jnp.dot(end_parts[...], selector, preferred_element_type=F32)
    high, middle, low = [part.astype(F32) for part in three_parts(factor)]
    ids = lax.broadcasted_iota(jnp.int32, factor.shape, 0)
    extra = jnp.where(ids == 0, high, jnp.where(ids == 1, middle, jnp.where(ids == 2, low, 0.0)))
    per_column = sent_ref.shape[0] // (width // 128)
    depth = state // per_column
    for piece in range(sent_ref.shape[0]):
        lanes = slice(128 * (piece // per_column), 128 * (piece // per_column) + 128)
        first = depth * (piece % per_column)
        sent_ref[piece] = jnp.concatenate(
            [reached[first : first + depth, lanes], extra[:, lanes]], axis=0
        ).astype(BF16)


def local_states(x, halo, x_taps, maps, maps_taps, raw, bias, decay_log, blocks):
    length, channels = x.shape
    heads = raw.shape[1]
    maps_width = maps.shape[1]
    width = 256
    columns = channels // width
    leading = halo.shape[0]
    taps = x_taps.shape[0]
    state = maps_width // 2
    sent = (blocks, state * channels // (blocks * 128) + 8, 128)
    whole = lambda shape: pl.BlockSpec(shape, lambda i: (0,) * len(shape))
    return pl.pallas_call(
        functools.partial(state_kernel, heads, channels // heads),
        grid=(columns,),
        in_specs=[
            pl.BlockSpec((length, width), lambda i: (0, i)),
            pl.BlockSpec((leading, width), lambda i: (0, i)),
            pl.BlockSpec((taps, width), lambda i: (0, i)),
            whole((length, maps_width)),
            pl.BlockSpec((leading, maps_width), lambda i: (0, channels // maps_width)),
            whole((taps, maps_width)),
            whole((length, heads)),
            whole((1, heads)),
            whole((1, heads)),
        ],
        out_specs=[
            pl.BlockSpec((length, width), lambda i: (0, i)),
            whole((length, maps_width)),
            whole((length, heads)),
            whole((length, heads)),
            pl.BlockSpec((blocks // columns,) + sent[1:], lambda i: (i, 0, 0)),
        ],
        out_shape=[
            jax.ShapeDtypeStruct((length, channels), BF16),
            jax.ShapeDtypeStruct((length, maps_width), BF16),
            jax.ShapeDtypeStruct((length, heads), F32),
            jax.ShapeDtypeStruct((length, heads), F32),
            jax.ShapeDtypeStruct(sent, BF16),
        ],
        scratch_shapes=[
            pltpu.VMEM((length + 8, width), F32),
            pltpu.VMEM((length, 3 * heads), BF16),
            pltpu.VMEM((8, 3 * heads), BF16),
            pltpu.VMEM((length, width), BF16),
        ],
        compiler_params=params(),
        cost_estimate=pl.CostEstimate(
            flops=20_000_000_000, bytes_accessed=4_000_000, transcendentals=0
        ),
        name="local_states",
    )(x, halo, x_taps, maps, halo, maps_taps, raw, bias, decay_log)


def scan_kernel(got_ref, out_ref):
    blocks, rows, lanes = out_ref.shape
    running = jnp.zeros((rows, lanes), F32)
    for block in range(blocks):
        out_ref[block] = running.astype(BF16)
        if block < blocks - 1:
            piece = got_ref[block].astype(F32)
            factor = piece[rows : rows + 1] + (
                piece[rows + 1 : rows + 2] + piece[rows + 2 : rows + 3]
            )
            running = factor * running + piece[:rows]


def scan_blocks(got):
    blocks, rows, lanes = got.shape
    return pl.pallas_call(
        scan_kernel,
        out_shape=jax.ShapeDtypeStruct((blocks, rows - 8, lanes), BF16),
        compiler_params=params(),
        name="scan_blocks",
    )(got)


def local_kernel(
    head_dim, x_ref, maps_ref, z_ref, step_ref, total_ref, skip_ref, shown_ref, passed_ref, scores
):
    pair = pl.program_id(0)
    length, width = x_ref.shape
    state = maps_ref.shape[1] // 2
    per_step = width // head_dim
    tile = 128

    @pl.when(pair == 0)
    def _():
        scores[...] = lax.dot_general(
            maps_ref[:, state:],
            maps_ref[:, :state],
            (((1,), (1,)), ((), ())),
            preferred_element_type=F32,
        )

    later = lax.broadcasted_iota(jnp.int32, (tile, tile), 0)
    earlier = lax.broadcasted_iota(jnp.int32, (tile, tile), 1)
    causal = later >= earlier
    lanes = lax.broadcasted_iota(jnp.int32, (tile, width), 1)
    totals = total_ref[0]
    steps = step_ref[0]
    for start in range(0, length, tile):
        outs = []
        outer = None
        for head in range(per_step):
            columns = jnp.broadcast_to(totals[head : head + 1, start : start + tile], (tile, tile)).T
            weights = []
            for source in range(0, start + tile, tile):
                spread = totals[head : head + 1, source : source + tile] - columns
                if source == start:
                    spread = jnp.where(causal, spread, -1e30)
                part = jnp.exp(spread) * scores[pl.ds(start, tile), pl.ds(source, tile)]
                part = part * steps[head : head + 1, source : source + tile]
                weights.append(part.astype(BF16))
            weights = weights[0] if len(weights) == 1 else jnp.concatenate(weights, axis=1)
            outs.append(
                jnp.dot(
                    weights,
                    x_ref[pl.ds(0, start + tile), pl.ds(head * head_dim, head_dim)],
                    preferred_element_type=F32,
                )
            )
            fade = jnp.exp(-columns)
            outer = fade if outer is None else jnp.where(lanes >= head * head_dim, fade, outer)
        values = x_ref[pl.ds(start, tile), :].astype(F32)
        gate = silu(z_ref[pl.ds(start, tile), :].astype(F32))
        out = jnp.concatenate(outs, axis=1) + skip_ref[...] * values
        shown_ref[pl.ds(start, tile), :] = out * gate
        passed_ref[pl.ds(start, tile), :] = outer * gate


def local_outputs(x_conv, maps_conv, z, step_rows, total_rows, skip, head_dim):
    length, channels = x_conv.shape
    width = 128
    columns = channels // width
    heads = channels // head_dim
    per_step = heads // columns
    maps_width = maps_conv.shape[1]
    step_rows = step_rows.reshape(columns, per_step, length)
    total_rows = total_rows.reshape(columns, per_step, length)
    block = pl.BlockSpec((length, width), lambda i: (0, i))
    row_block = pl.BlockSpec((1, per_step, length), lambda i: (i, 0, 0))
    return pl.pallas_call(
        functools.partial(local_kernel, head_dim),
        grid=(columns,),
        in_specs=[
            block,
            pl.BlockSpec((length, maps_width), lambda i: (0, 0)),
            block,
            row_block,
            row_block,
            pl.BlockSpec((1, width), lambda i: (0, i)),
        ],
        out_specs=[block, block],
        out_shape=[jax.ShapeDtypeStruct((length, channels), F32)] * 2,
        scratch_shapes=[pltpu.VMEM((length, length), F32)],
        compiler_params=params(),
        cost_estimate=pl.CostEstimate(
            flops=8_000_000_000, bytes_accessed=6_000_000, transcendentals=0
        ),
        name="local_outputs",
    )(x_conv, maps_conv, z, step_rows, total_rows, skip)


def norm_kernel(picks, carried_ref, maps_ref, shown_ref, passed_ref, gain_ref, out_ref, entering):
    state, channels = entering.shape
    pieces, depth, lanes = carried_ref.shape
    per_column = state // depth

    @pl.when(pl.program_id(0) == 0)
    def _():
        for piece in range(pieces):
            entering[
                pl.ds(depth * (piece % per_column), depth),
                pl.ds(lanes * (piece // per_column), lanes),
            ] = carried_ref[piece]

    carry = jnp.dot(maps_ref[...], entering[...], preferred_element_type=F32)
    gated = shown_ref[...] + carry * passed_ref[...]
    scale = lax.rsqrt(jnp.mean(gated * gated, axis=1, keepdims=True) + 1e-05)
    out_ref[...] = (gated * scale * gain_ref[...]).astype(BF16)


def normed_rows(picks, carried, maps_conv, shown, passed, gain, name):
    length, channels = shown.shape
    state = maps_conv.shape[1] // 2
    count = picks.shape[0]
    rows = length // (2 * count)
    picked = pl.BlockSpec((rows, channels), lambda i, picks: (picks[i], 0))
    return pl.pallas_call(
        norm_kernel,
        grid_spec=pltpu.PrefetchScalarGridSpec(
            num_scalar_prefetch=1,
            grid=(count,),
            in_specs=[
                pl.BlockSpec(carried.shape, lambda i, picks: (0, 0, 0)),
                pl.BlockSpec((rows, state), lambda i, picks: (picks[i], 1)),
                picked,
                picked,
                pl.BlockSpec((1, channels), lambda i, picks: (0, 0)),
            ],
            out_specs=pl.BlockSpec((rows, channels), lambda i, picks: (i, 0)),
            scratch_shapes=[pltpu.VMEM((state, channels), BF16)],
        ),
        out_shape=jax.ShapeDtypeStruct((rows * count, channels), BF16),
        compiler_params=params(),
        cost_estimate=pl.CostEstimate(
            flops=1_000_000_000, bytes_accessed=3_000_000, transcendentals=0
        ),
        name=name,
    )(picks, carried, maps_conv, shown, passed, gain)


def project_kernel(own_ref, other_ref, own_weight_ref, other_weight_ref, *out_refs):
    product = jnp.dot(own_ref[...], own_weight_ref[...], preferred_element_type=F32)
    product = product + jnp.dot(
        other_ref[...], other_weight_ref[...], preferred_element_type=F32
    )
    rows = out_refs[0].shape[0]
    for index, out_ref in enumerate(out_refs):
        out_ref[...] = product[rows * index : rows * (index + 1)].astype(out_ref.dtype)


def project(own, other, own_weight, other_weight, part, parts, name):
    count, depth = own.shape
    columns = own_weight.shape[1] // parts
    rows = count // 4
    width = 512
    tiles = columns // width
    source = pl.BlockSpec((count, depth), lambda i: (0, 0))
    weight = pl.BlockSpec((depth, width), lambda i: (0, part * tiles + i))
    return pl.pallas_call(
        project_kernel,
        grid=(tiles,),
        in_specs=[source, source, weight, weight],
        out_specs=[pl.BlockSpec((rows, width), lambda i: (0, i))] * 4,
        out_shape=[jax.ShapeDtypeStruct((rows, columns), BF16)] * 4,
        compiler_params=params(),
        cost_estimate=pl.CostEstimate(
            flops=4 * count * depth * columns, bytes_accessed=9_000_000, transcendentals=0
        ),
        name=name,
    )(own, other, own_weight, other_weight)


def on_device(
    x_inputs,
    state_maps,
    z_gate,
    step_raw,
    step_bias,
    decay_log,
    skip_gain,
    x_filter,
    state_filter,
    norm_gain,
    out_weight,
):
    length, channels = x_inputs.shape
    leading = x_filter.shape[0] - 1
    heads = step_raw.shape[1]
    head_dim = channels // heads
    blocks = lax.axis_size("ctx")
    members = lax.axis_size("tp")
    ring = members // 2
    place = lax.axis_index("tp")
    across, core = place // 2, place % 2

    def core_swap(value):
        return lax.ppermute(value, "tp", [(i, i ^ 1) for i in range(members)])

    def along(value, steps):
        pairs = [
            (2 * y + c, 2 * ((y + steps) % ring) + c) for y in range(ring) for c in range(2)
        ]
        return lax.ppermute(value, "tp", pairs)

    ends = jnp.concatenate([x_inputs[length - leading :], state_maps[length - leading :]], axis=1)
    halo = shifted(ends, "ctx", 1)
    other_weight = core_swap(out_weight)
    x_conv, maps_conv, step, total, sent = local_states(
        x_inputs,
        halo,
        x_filter,
        state_maps,
        state_filter,
        step_raw,
        step_bias[None],
        decay_log[None],
        blocks,
    )
    got = lax.all_to_all(sent, "ctx", 0, 0, tiled=True)
    shown, passed = local_outputs(
        x_conv,
        maps_conv,
        z_gate,
        step.T,
        total.T,
        jnp.repeat(skip_gain, head_dim)[None],
        head_dim,
    )
    entering = scan_blocks(got)
    carried = lax.all_to_all(entering, "ctx", 0, 0, tiled=True)

    turns = (across + jnp.array([2, 1, 3, 0], jnp.int32)) % ring
    gain = norm_gain[None]
    give = normed_rows(2 * turns + 1 - core, carried, maps_conv, shown, passed, gain, "give_rows")
    taken = core_swap(give)
    keep = normed_rows(2 * turns + core, carried, maps_conv, shown, passed, gain, "keep_rows")
    far_a, up_a, down_a, own_a = project(keep, taken, out_weight, other_weight, 0, 2, "left_half")
    far_b, up_b, down_b, own_b = project(keep, taken, out_weight, other_weight, 1, 2, "right_half")

    def added(*values):
        return functools.reduce(lambda a, b: a + b, [v.astype(F32) for v in values]).astype(BF16)

    relay_a = along(far_a, 1)
    from_above_a = along(down_a, -1)
    relay_b = along(far_b, -1)
    from_below_b = along(up_b, 1)
    from_below_a = along(added(up_a, relay_a), 1)
    from_above_b = along(added(down_b, relay_b), -1)
    return jnp.concatenate(
        [added(own_a, from_above_a, from_below_a), added(own_b, from_above_b, from_below_b)], axis=1
    )


def solution(mesh):
    return jax.shard_map(
        on_device,
        mesh=mesh,
        in_specs=(
            P("ctx", "tp"),
            P("ctx", "tp"),
            P("ctx", "tp"),
            P("ctx", "tp"),
            P("tp"),
            P("tp"),
            P("tp"),
            P(None, "tp"),
            P(None, "tp"),
            P("tp"),
            P("tp", None),
        ),
        out_specs=P(("ctx", "tp"), None),
        check_vma=False,
    )
```

time: 617 us -> 100 us (0.16)
  waiting for transfers between devices: 461 us -> 26.9 us
  other arithmetic: 42.6 us -> 1.18 us
  starting transfers between devices: 69.2 us -> 27.8 us
  Pallas kernels: 0 us -> 26.2 us
  matrix products: 22.2 us -> 0 us
  between operations: 13.5 us -> 0.22 us
  local copies, waits for them, and re-layouts: 7.38 us -> 16.4 us
    ppermute x33 -> x1, waiting for transfers between devices: 424 us -> 4.66 us  [shifted(): lax.ppermute(value, axis, [(source, source + steps) for source in range(l...]
    ppermute x33 -> x1, starting transfers between devices: 69.2 us -> 3.83 us  [shifted(): lax.ppermute(value, axis, [(source, source + steps) for source in range(l...]
    reduce_scatter x1 -> x0, waiting for transfers between devices: 36.9 us -> none  [on_device(): lax.psum_scatter(jnp.dot(normed, out_weight, preferred_element_type=jnp.f...]
    add x31 -> x1, other arithmetic: 29.8 us -> 0.01 us  [on_device(): 2 * turns + core]
    pallas_call x0 -> x7, Pallas kernels: none -> 26.2 us  [the longest x2 9.97 us: project(): pl.pallas_call(project_kernel, grid=(tiles,), in_specs=[source, source, w...]
    dot_general x6 -> x0, matrix products: 22.2 us -> none  [the longest x1 10 us: on_device(): jnp.dot(normed, out_weight, preferred_element_type=jnp.float32)]
    all_to_all x0 -> x2, starting transfers between devices: none -> 15 us  [the longest x1 9.01 us: on_device(): got = lax.all_to_all(sent, 'ctx', 0, 0, tiled=True)]
    unnamed x19 -> x31, local copies, waits for them, and re-layouts: 1.49 us -> 14.5 us
  transfers between devices with their start and end apart: 34 -> 11, of which waited for: 32 -> 4; matrix products, arithmetic and copies ran while one was open for 2% -> 3% of each run, Pallas kernels for 0% -> 22%
where the time goes in v2:
time: 100 us; the launch traced here: 98.6 us
  starting transfers between devices  27.8 us (28%)
  waiting for transfers between devices  26.9 us (27%)
  Pallas kernels  26.2 us (26%)
  local copies, waits for them, and re-layouts  16.4 us (16%)
  other arithmetic  1.18 us (1%)
    unnamed x31, local copies, waits for them, and re-layouts  14.5 us
    all_to_all x1, waiting for transfers between devices, on_device(): got = lax.all_to_all(sent, 'ctx', 0, 0, tiled=True)  11.3 us
    ppermute x6, waiting for transfers between devices, along(): return lax.ppermute(value, 'tp', pairs)  10.9 us
    pallas_call x2, Pallas kernels, project(): pl.pallas_call(project_kernel, grid=(tiles,), in_specs=[source, source, w...  9.97 us
    all_to_all x1, starting transfers between devices, on_device(): got = lax.all_to_all(sent, 'ctx', 0, 0, tiled=True)  9.01 us
    ppermute x6, starting transfers between devices, along(): return lax.ppermute(value, 'tp', pairs)  8.8 us
    pallas_call x1, Pallas kernels, local_outputs(): pl.pallas_call(functools.partial(local_kernel, head_dim), grid=(columns,)...  6.48 us
    all_to_all x1, starting transfers between devices, on_device(): carried = lax.all_to_all(entering, 'ctx', 0, 0, tiled=True)  6.02 us
  transfers between devices with their start and end apart: 11, of which 4 were waited for; matrix products, arithmetic and copies ran while one was open for 3% of the time, Pallas kernels for 22%

profile of v2, /device:TPU:2, one launch (start us, length us, event | category | flops | bytes accessed | tf_op | source)
XLA Modules:
  0.0 98.6 jit_solution(6289591032866842776)
XLA Ops:
  0.0 0.7 slice.6
  0.7 0.7 slice.7
  1.4 3.8 %collective-permute-start = (bf16[3,1280]{1,0:T(4,128)(2,1)S(1)}, bf16[3,1280]{1,0:T(4,128)(2,1)S(1)}, u32[]{:S(2)}, u32[]{:S(2)}) collective-permute-start(bf16[3,1280]{1,0:T(4,128)(2,1)S(1)} %pad_maximum_fusion.1), channel_id=1, source_target_pairs={{0,8},{8,16},{16,24},{24,32},{32,40},{40,48},{48,56},{56,64},{64,7... | collective-permute-start | bytes 23048 | tf_op jit(solution)/shard_map/ppermute | solution.py:22
  5.3 0.9 copy.13.raw_ref
  6.2 4.7 %collective-permute-done.halo_ref.maps_halo_ref = bf16[3,1280]{1,0:T(4,128)(2,1)S(1)} collective-permute-done((bf16[3,1280]{1,0:T(4,128)(2,1)S(1)}, bf16[3,1280]{1,0:T(4,128)(2,1)S(1)}, u32[]{:S(2)}, u32[]{:S(2)}) %collective-permute-start) | collective-permute-done | bytes 7712 | tf_op jit(solution)/shard_map/ppermute | solution.py:22
  10.8 1.2 %copy-done.4 = bf16[512,1024]{1,0:T(8,128)(2,1)S(1)} copy-done((bf16[512,1024]{1,0:T(8,128)(2,1)S(1)}, bf16[512,1024]{1,0:T(8,128)(2,1)}, u32[]{:S(2)}) %copy-start.4) | copy-done | bytes 1048600
  12.0 0.9 copy-done.5
  13.0 0.7 copy-done.7
  13.7 0.7 copy-done.8
  14.4 0.7 copy-done.9
  15.7 5.2 %local_states.1 = (bf16[512,1024]{1,0:T(8,128)(2,1)S(1)}, bf16[512,256]{1,0:T(8,128)(2,1)S(1)}, f32[512,16]{1,0:T(8,128)S(1)}, f32[512,16]{1,0:T(8,128)S(1)}, bf16[32,40,128]{2,1,0:T(8,128)(2,1)}) custom-call(bf16[512,1024]{1,0:T(8,128)(2,1)S(1)} %copy-done.4, bf16[3,1280]{1,0:T(4,128)(2,1)S(1)} %collective-permute-done.halo_ref.maps_halo_ref, ...), custom_call_target="tpu_custom_call" | custom-call | flops 20000000000 | bytes 4000000 | tf_op jit(solution)/shard_map/local_states/pallas_call | solution.py:158
  20.9 9.0 %all-to-all-start = ((bf16[32,40,128]{2,1,0:T(8,128)(2,1)}), bf16[32,40,128]{2,1,0:T(8,128)(2,1)S(1)}, u32[]{:S(2)}, u32[]{:S(2)}) async-start(bf16[32,40,128]{2,1,0:T(8,128)(2,1)} %get-tuple-element.20), calls=%async_computation | async-start | bytes 655360 | tf_op jit(solution)/shard_map/all_to_all | solution.py:437
  30.4 11.3 %all-to-all-done.got_ref = bf16[32,40,128]{2,1,0:T(8,128)(2,1)S(1)} async-done(((bf16[32,40,128]{2,1,0:T(8,128)(2,1)}), bf16[32,40,128]{2,1,0:T(8,128)(2,1)S(1)}, u32[]{:S(2)}, u32[]{:S(2)}) %all-to-all-start) | async-done | bytes 327712 | tf_op jit(solution)/shard_map/all_to_all | solution.py:437
  41.7 0.8 scan_blocks.1
  42.5 6.0 %all-to-all-start.1 = ((bf16[32,32,128]{2,1,0:T(8,128)(2,1)}), bf16[32,32,128]{2,1,0:T(8,128)(2,1)S(1)}, u32[]{:S(2)}, u32[]{:S(2)}) async-start(bf16[32,32,128]{2,1,0:T(8,128)(2,1)} %scan_blocks.1), calls=%async_computation.1 | async-start | bytes 524288 | tf_op jit(solution)/shard_map/all_to_all | solution.py:448
  48.5 1.2 %copy-done.6 = bf16[512,1024]{1,0:T(8,128)(2,1)S(1)} copy-done((bf16[512,1024]{1,0:T(8,128)(2,1)S(1)}, bf16[512,1024]{1,0:T(8,128)(2,1)}, u32[]{:S(2)}) %copy-start.6) | copy-done | bytes 1048600
  49.8 1.2 %copy-done.12 = bf16[512,1024]{1,0:T(8,128)(2,1)S(1)} copy-done((bf16[512,1024]{1,0:T(8,128)(2,1)S(1)}, bf16[512,1024]{1,0:T(8,128)(2,1)}, u32[]{:S(2)}) %copy-start.12) | copy-done | bytes 1048600
  51.0 6.5 %local_outputs.1 = (f32[512,1024]{1,0:T(8,128)S(1)}, f32[512,1024]{1,0:T(8,128)S(1)}) custom-call(bf16[512,1024]{1,0:T(8,128)(2,1)S(1)} %copy-done.12, bf16[512,256]{1,0:T(8,128)(2,1)S(1)} %get-tuple-element.21.maps_ref, bf16[512,1024]{1,0:T(8,128)(2,1)S(1)} %copy-done.6, f32[8,2,512]{2,1,0:T(2,128)S(1)} %reshape.6.step_ref, ...), custom_call_target="tpu_custom_call" | custom-call | flops 8000000000 | bytes 6000000 | tf_op jit(solution)/shard_map/local_outputs/pallas_call | solution.py:288
  57.5 1.4 %copy-done.1 = f32[512,1024]{1,0:T(8,128)} copy-done((f32[512,1024]{1,0:T(8,128)}, f32[512,1024]{1,0:T(8,128)S(1)}, u32[]{:S(2)}) %copy-start.1) | copy-done | bytes 2097176
  58.8 1.6 %copy-done.2 = f32[512,1024]{1,0:T(8,128)S(1)} copy-done((f32[512,1024]{1,0:T(8,128)S(1)}, f32[512,1024]{1,0:T(8,128)}, u32[]{:S(2)}) %copy-start.2) | copy-done | bytes 2097176
  60.4 1.9 %give_rows.1 = bf16[256,1024]{1,0:T(8,128)(2,1)S(1)} custom-call(s32[4]{0:T(128)S(1)} %get-tuple-element.35.picks, bf16[32,32,128]{2,1,0:T(8,128)(2,1)S(1)} %all-to-all-done.1.carried_ref, bf16[512,256]{1,0:T(8,128)(2,1)S(1)} %get-tuple-element.21.maps_ref, f32[512,1024]{1,0:T(8,128)S(1)} %get-tuple-element.25.shown_ref, f32[512,1024]{1,0:T(8,128)S(1)} %copy-done.2, ...), custom_call_target="tpu_custom_call" | custom-call | flops 1000000000 | bytes 3000000 | tf_op jit(solution)/shard_map/give_rows/pallas_call | solution.py:335
  62.4 1.9 %keep_rows.1.own_ref = bf16[256,1024]{1,0:T(8,128)(2,1)S(1)} custom-call(s32[4]{0:T(128)S(1)} %broadcast_add_fusion.picks, bf16[32,32,128]{2,1,0:T(8,128)(2,1)S(1)} %all-to-all-done.1.carried_ref, bf16[512,256]{1,0:T(8,128)(2,1)S(1)} %get-tuple-element.21.maps_ref, f32[512,1024]{1,0:T(8,128)S(1)} %get-tuple-element.25.shown_ref, f32[512,1024]{1,0:T(8,128)S(1)} %copy-done.2, ...), custom_call_target="tpu_custom_call" | custom-call | flops 1000000000 | bytes 3000000 | tf_op jit(solution)/shard_map/keep_rows/pallas_call | solution.py:335
  64.3 3.4 %copy-done = bf16[1024,4096]{1,0:T(8,128)(2,1)S(1)} copy-done((bf16[1024,4096]{1,0:T(8,128)(2,1)S(1)}, bf16[1024,4096]{1,0:T(8,128)(2,1)}, u32[]{:S(2)}) %copy-start) | copy-done | bytes 8388632
  67.7 5.0 %left_half.1 = (bf16[64,2048]{1,0:T(8,128)(2,1)S(1)}, bf16[64,2048]{1,0:T(8,128)(2,1)S(1)}, bf16[64,2048]{1,0:T(8,128)(2,1)S(1)}, bf16[64,2048]{1,0:T(8,128)(2,1)S(1)}) custom-call(bf16[256,1024]{1,0:T(8,128)(2,1)S(1)} %keep_rows.1.own_ref, bf16[256,1024]{1,0:T(8,128)(2,1)S(1)} %collective-permute-done.1.other_ref, bf16[1024,4096]{1,0:T(8,128)(2,1)S(1)} %copy-done, ...), custom_call_target="tpu_custom_call" | custom-call | flops 2147483648 | bytes 9000000 | tf_op jit(solution)/shard_map/left_half/pallas_call | solution.py:377
  72.7 1.7 %collective-permute-start.4 = (bf16[64,2048]{1,0:T(8,128)(2,1)S(1)}, bf16[64,2048]{1,0:T(8,128)(2,1)S(1)}, u32[]{:S(2)}, u32[]{:S(2)}) collective-permute-start(bf16[64,2048]{1,0:T(8,128)(2,1)S(1)} %get-tuple-element.30), channel_id=1, source_target_pairs={{0,2},{1,3},{2,4},{3,5},{4,6},{5,7},{6,0},{7,1},{8,10},{9,11},{10,... | collective-permute-start | bytes 786440 | tf_op jit(solution)/shard_map/ppermute | solution.py:421
  74.3 1.7 %collective-permute-start.3 = (bf16[64,2048]{1,0:T(8,128)(2,1)S(1)}, bf16[64,2048]{1,0:T(8,128)(2,1)S(1)}, u32[]{:S(2)}, u32[]{:S(2)}) collective-permute-start(bf16[64,2048]{1,0:T(8,128)(2,1)S(1)} %get-tuple-element.28), channel_id=1, source_target_pairs={{0,6},{1,7},{2,0},{3,1},{4,2},{5,3},{6,4},{7,5},{8,14},{9,15},{10,... | collective-permute-start | bytes 786440 | tf_op jit(solution)/shard_map/ppermute | solution.py:421
  76.0 5.0 %right_half.1 = (bf16[64,2048]{1,0:T(8,128)(2,1)S(1)}, bf16[64,2048]{1,0:T(8,128)(2,1)S(1)}, bf16[64,2048]{1,0:T(8,128)(2,1)S(1)}, bf16[64,2048]{1,0:T(8,128)(2,1)S(1)}) custom-call(bf16[256,1024]{1,0:T(8,128)(2,1)S(1)} %keep_rows.1.own_ref, bf16[256,1024]{1,0:T(8,128)(2,1)S(1)} %collective-permute-done.1.other_ref, bf16[1024,4096]{1,0:T(8,128)(2,1)S(1)} %copy-done, ...), custom_call_target="tpu_custom_call" | custom-call | flops 2147483648 | bytes 9000000 | tf_op jit(solution)/shard_map/right_half/pallas_call | solution.py:377
  81.0 1.9 %collective-permute-start.6 = (bf16[64,2048]{1,0:T(8,128)(2,1)S(1)}, bf16[64,2048]{1,0:T(8,128)(2,1)S(1)}, u32[]{:S(2)}, u32[]{:S(2)}) collective-permute-start(bf16[64,2048]{1,0:T(8,128)(2,1)S(1)} %get-tuple-element.33), channel_id=1, source_target_pairs={{0,6},{1,7},{2,0},{3,1},{4,2},{5,3},{6,4},{7,5},{8,14},{9,15},{10,... | collective-permute-start | bytes 786440 | tf_op jit(solution)/shard_map/ppermute | solution.py:421
  83.6 5.7 %collective-permute-done.6 = bf16[64,2048]{1,0:T(8,128)(2,1)S(1)} collective-permute-done((bf16[64,2048]{1,0:T(8,128)(2,1)S(1)}, bf16[64,2048]{1,0:T(8,128)(2,1)S(1)}, u32[]{:S(2)}, u32[]{:S(2)}) %collective-permute-start.6) | collective-permute-done | bytes 262176 | tf_op jit(solution)/shard_map/ppermute | solution.py:421
  89.4 2.9 %collective-permute-start.7 = (bf16[64,2048]{1,0:T(8,128)(2,1)S(1)}, bf16[64,2048]{1,0:T(8,128)(2,1)S(1)}, u32[]{:S(2)}, u32[]{:S(2)}) collective-permute-start(bf16[64,2048]{1,0:T(8,128)(2,1)S(1)} %add_convert_fusion.1), channel_id=1, source_target_pairs={{0,6},{1,7},{2,0},{3,1},{4,2},{5,3},{6,4},{7,5},{8,14},{9,15},{10,... | collective-permute-start | bytes 786440 | tf_op jit(solution)/shard_map/ppermute | solution.py:421
  92.4 5.2 %collective-permute-done.5 = bf16[64,2048]{1,0:T(8,128)(2,1)S(1)} collective-permute-done((bf16[64,2048]{1,0:T(8,128)(2,1)S(1)}, bf16[64,2048]{1,0:T(8,128)(2,1)S(1)}, u32[]{:S(2)}, u32[]{:S(2)}) %collective-permute-start.5) | collective-permute-done | bytes 262176 | tf_op jit(solution)/shard_map/ppermute | solution.py:421
  97.8 0.8 pad_maximum_fusion
  (44 shorter events, 2.2 us)
Async XLA Ops:
  0.0 64.3 %collective-permute-start.2 = (bf16[1024,4096]{1,0:T(8,128)(2,1)}, bf16[1024,4096]{1,0:T(8,128)(2,1)}, u32[]{:S(2)}, u32[]{:S(2)}) collective-permute-start(bf16[1024,4096]{1,0:T(8,128)(2,1)} %own_weight_ref.3), channel_id=1, source_target_pairs={{0,1},{1,0},{2,3},{3,2},{4,5},{5,4},{6,7},{7,6},{8,9},{9,8},{10,11... | collective-permute-start | bytes 25165832 | tf_op jit(solution)/shard_map/ppermute | solution.py:415
  1.4 9.4 %collective-permute-start = (bf16[3,1280]{1,0:T(4,128)(2,1)S(1)}, bf16[3,1280]{1,0:T(4,128)(2,1)S(1)}, u32[]{:S(2)}, u32[]{:S(2)}) collective-permute-start(bf16[3,1280]{1,0:T(4,128)(2,1)S(1)} %pad_maximum_fusion.1), channel_id=1, source_target_pairs={{0,8},{8,16},{16,24},{24,32},{32,40},{40,48},{48,56},{56,64},{64,7... | collective-permute-start | bytes 23048 | tf_op jit(solution)/shard_map/ppermute | solution.py:22
  10.8 1.2 %copy-start.4 = (bf16[512,1024]{1,0:T(8,128)(2,1)S(1)}, bf16[512,1024]{1,0:T(8,128)(2,1)}, u32[]{:S(2)}) copy-start(bf16[512,1024]{1,0:T(8,128)(2,1)} %x_ref.1) | copy-start | bytes 3145732
  12.0 0.9 copy-start.5
  13.0 0.7 copy-start.7
  13.7 0.7 copy-start.8
  14.4 0.7 copy-start.9
  15.0 0.7 copy-start.10
  15.7 14.3 %copy-start.13 = (f32[16]{0:T(128)S(1)}, f32[16]{0:T(128)}, u32[]{:S(2)}) copy-start(f32[16]{0:T(128)} %param.18) | copy-start | bytes 196
  15.7 14.4 %copy-start.14 = (s32[4]{0:T(128)S(1)}, s32[4]{0:T(128)}, u32[]{:S(2)}) copy-start(s32[4]{0:T(128)} %constant.46.clone) | copy-start | bytes 52
  20.9 27.6 %copy-start.11 = (bf16[512,1024]{1,0:T(8,128)(2,1)}, bf16[512,1024]{1,0:T(8,128)(2,1)S(1)}, u32[]{:S(2)}) copy-start(bf16[512,1024]{1,0:T(8,128)(2,1)S(1)} %get-tuple-element.22.x_ref) | copy-start | bytes 3145732
  20.9 20.8 %all-to-all-start = ((bf16[32,40,128]{2,1,0:T(8,128)(2,1)}), bf16[32,40,128]{2,1,0:T(8,128)(2,1)S(1)}, u32[]{:S(2)}, u32[]{:S(2)}) async-start(bf16[32,40,128]{2,1,0:T(8,128)(2,1)} %get-tuple-element.20), calls=%async_computation | async-start | bytes 655360 | tf_op jit(solution)/shard_map/all_to_all | solution.py:437
  42.5 16.4 %all-to-all-start.1 = ((bf16[32,32,128]{2,1,0:T(8,128)(2,1)}), bf16[32,32,128]{2,1,0:T(8,128)(2,1)S(1)}, u32[]{:S(2)}, u32[]{:S(2)}) async-start(bf16[32,32,128]{2,1,0:T(8,128)(2,1)} %scan_blocks.1), calls=%async_computation.1 | async-start | bytes 524288 | tf_op jit(solution)/shard_map/all_to_all | solution.py:448
  48.5 1.2 %copy-start.6 = (bf16[512,1024]{1,0:T(8,128)(2,1)S(1)}, bf16[512,1024]{1,0:T(8,128)(2,1)}, u32[]{:S(2)}) copy-start(bf16[512,1024]{1,0:T(8,128)(2,1)} %z_ref.1) | copy-start | bytes 3145732
  49.8 1.2 %copy-start.12 = (bf16[512,1024]{1,0:T(8,128)(2,1)S(1)}, bf16[512,1024]{1,0:T(8,128)(2,1)}, u32[]{:S(2)}) copy-start(bf16[512,1024]{1,0:T(8,128)(2,1)} %copy-done.11) | copy-start | bytes 3145732
  51.0 7.9 %copy-start.3 = (f32[1024]{0:T(1024)S(1)}, f32[1024]{0:T(1024)}, u32[]{:S(2)}) copy-start(f32[1024]{0:T(1024)} %param.21) | copy-start | bytes 12292
  57.5 1.4 %copy-start.1 = (f32[512,1024]{1,0:T(8,128)}, f32[512,1024]{1,0:T(8,128)S(1)}, u32[]{:S(2)}) copy-start(f32[512,1024]{1,0:T(8,128)S(1)} %get-tuple-element.26.passed_ref) | copy-start | bytes 6291460
  58.8 1.6 %copy-start.2 = (f32[512,1024]{1,0:T(8,128)S(1)}, f32[512,1024]{1,0:T(8,128)}, u32[]{:S(2)}) copy-start(f32[512,1024]{1,0:T(8,128)} %copy-done.1) | copy-start | bytes 6291460
  62.3 2.0 %collective-permute-start.1 = (bf16[256,1024]{1,0:T(8,128)(2,1)S(1)}, bf16[256,1024]{1,0:T(8,128)(2,1)S(1)}, u32[]{:S(2)}, u32[]{:S(2)}) collective-permute-start(bf16[256,1024]{1,0:T(8,128)(2,1)S(1)} %give_rows.1), channel_id=1, source_target_pairs={{0,1},{1,0},{2,3},{3,2},{4,5},{5,4},{6,7},{7,6},{8,9},{9,8},{10,11... | collective-permute-start | bytes 1572872 | tf_op jit(solution)/shard_map/ppermute | solution.py:415
  64.3 3.4 %copy-start = (bf16[1024,4096]{1,0:T(8,128)(2,1)S(1)}, bf16[1024,4096]{1,0:T(8,128)(2,1)}, u32[]{:S(2)}) copy-start(bf16[1024,4096]{1,0:T(8,128)(2,1)} %own_weight_ref.3) | copy-start | bytes 25165828
  72.7 10.4 %collective-permute-start.4 = (bf16[64,2048]{1,0:T(8,128)(2,1)S(1)}, bf16[64,2048]{1,0:T(8,128)(2,1)S(1)}, u32[]{:S(2)}, u32[]{:S(2)}) collective-permute-start(bf16[64,2048]{1,0:T(8,128)(2,1)S(1)} %get-tuple-element.30), channel_id=1, source_target_pairs={{0,2},{1,3},{2,4},{3,5},{4,6},{5,7},{6,0},{7,1},{8,10},{9,11},{10,... | collective-permute-start | bytes 786440 | tf_op jit(solution)/shard_map/ppermute | solution.py:421
  74.3 18.0 %collective-permute-start.3 = (bf16[64,2048]{1,0:T(8,128)(2,1)S(1)}, bf16[64,2048]{1,0:T(8,128)(2,1)S(1)}, u32[]{:S(2)}, u32[]{:S(2)}) collective-permute-start(bf16[64,2048]{1,0:T(8,128)(2,1)S(1)} %get-tuple-element.28), channel_id=1, source_target_pairs={{0,6},{1,7},{2,0},{3,1},{4,2},{5,3},{6,4},{7,5},{8,14},{9,15},{10,... | collective-permute-start | bytes 786440 | tf_op jit(solution)/shard_map/ppermute | solution.py:421
  81.0 8.4 %collective-permute-start.6 = (bf16[64,2048]{1,0:T(8,128)(2,1)S(1)}, bf16[64,2048]{1,0:T(8,128)(2,1)S(1)}, u32[]{:S(2)}, u32[]{:S(2)}) collective-permute-start(bf16[64,2048]{1,0:T(8,128)(2,1)S(1)} %get-tuple-element.33), channel_id=1, source_target_pairs={{0,6},{1,7},{2,0},{3,1},{4,2},{5,3},{6,4},{7,5},{8,14},{9,15},{10,... | collective-permute-start | bytes 786440 | tf_op jit(solution)/shard_map/ppermute | solution.py:421
  82.9 14.8 %collective-permute-start.8 = (bf16[64,2048]{1,0:T(8,128)(2,1)S(1)}, bf16[64,2048]{1,0:T(8,128)(2,1)S(1)}, u32[]{:S(2)}, u32[]{:S(2)}) collective-permute-start(bf16[64,2048]{1,0:T(8,128)(2,1)S(1)} %get-tuple-element.34), channel_id=1, source_target_pairs={{0,2},{1,3},{2,4},{3,5},{4,6},{5,7},{6,0},{7,1},{8,10},{9,11},{10,... | collective-permute-start | bytes 786440 | tf_op jit(solution)/shard_map/ppermute | solution.py:421
  83.2 14.4 %collective-permute-start.5 = (bf16[64,2048]{1,0:T(8,128)(2,1)S(1)}, bf16[64,2048]{1,0:T(8,128)(2,1)S(1)}, u32[]{:S(2)}, u32[]{:S(2)}) collective-permute-start(bf16[64,2048]{1,0:T(8,128)(2,1)S(1)} %add_convert_fusion.3), channel_id=1, source_target_pairs={{0,2},{1,3},{2,4},{3,5},{4,6},{5,7},{6,0},{7,1},{8,10},{9,11},{10,... | collective-permute-start | bytes 786440 | tf_op jit(solution)/shard_map/ppermute | solution.py:421
  89.4 8.3 %collective-permute-start.7 = (bf16[64,2048]{1,0:T(8,128)(2,1)S(1)}, bf16[64,2048]{1,0:T(8,128)(2,1)S(1)}, u32[]{:S(2)}, u32[]{:S(2)}) collective-permute-start(bf16[64,2048]{1,0:T(8,128)(2,1)S(1)} %add_convert_fusion.1), channel_id=1, source_target_pairs={{0,6},{1,7},{2,0},{3,1},{4,2},{5,3},{6,4},{7,5},{8,14},{9,15},{10,... | collective-permute-start | bytes 786440 | tf_op jit(solution)/shard_map/ppermute | solution.py:421

commit v3 on v2

v3 whole, which is shorter than its diff:
```python
import functools

import jax
import jax.numpy as jnp
from jax import lax
from jax.experimental import pallas as pl
from jax.experimental.pallas import tpu as pltpu
from jax.sharding import PartitionSpec as P

BF16 = jnp.bfloat16
F32 = jnp.float32
VMEM_LIMIT = 16 * 1024 * 1024
TURNS = (2, 1, 3, 0)


def far_memory(value):
    return pltpu.with_memory_space_constraint(value, pltpu.HBM)


def params(**more):
    return pltpu.CompilerParams(vmem_limit_bytes=VMEM_LIMIT, **more)


def shifted(value, axis, steps):
    count = lax.axis_size(axis)
    leading, last = (max(0, -steps), min(count, count - steps))
    return lax.ppermute(value, axis, [(source, source + steps) for source in range(leading, last)])


def three_parts(value):
    high = value.astype(BF16)
    rest = value - high.astype(F32)
    middle = rest.astype(BF16)
    low = (rest - middle.astype(F32)).astype(BF16)
    return high, middle, low


def packed_parts(value):
    high, middle, low = three_parts(value)
    wide = [high.astype(F32), middle.astype(F32), low.astype(F32)]
    return jnp.concatenate(wide, axis=0).astype(BF16)


def head_selector(first_head, heads, head_dim, width):
    rows = lax.broadcasted_iota(jnp.int32, (3 * heads, width), 0)
    lanes = lax.broadcasted_iota(jnp.int32, (3 * heads, width), 1)
    return (rows % heads == first_head + lanes // head_dim).astype(F32).astype(BF16)


def spread_heads(parts, selector):
    return lax.dot_general(
        parts, selector, (((0,), (0,)), ((), ())), preferred_element_type=F32
    )


def silu(value):
    return value / (1.0 + jnp.exp(-value))


def conv_rows(padded, taps, start, rows):
    count = taps.shape[0]
    total = None
    for offset in range(count):
        first = 8 - (count - 1) + offset + start
        term = taps[offset : offset + 1] * padded[pl.ds(first, rows), :]
        total = term if total is None else total + term
    return total


def state_kernel(
    heads,
    head_dim,
    held,
    x_ref,
    x_taps_ref,
    maps_ref,
    maps_taps_ref,
    raw_ref,
    bias_ref,
    decay_ref,
    conv_ref,
    maps_conv_ref,
    step_ref,
    total_ref,
    first_tail_ref,
    reached_ref,
    padded,
    tail_parts,
    end_parts,
    weighted,
):
    column = pl.program_id(0)
    length, width = x_ref.shape
    tile = 64
    state = maps_ref.shape[1] // 2

    def fill(source):
        padded[pl.ds(0, 8), :] = jnp.zeros((8, padded.shape[1]), F32)
        for start in range(0, length, tile):
            padded[pl.ds(8 + start, tile), :] = source[pl.ds(start, tile), :].astype(F32)

    @pl.when(column == 0)
    def _():
        row_ids = lax.broadcasted_iota(jnp.int32, (heads, heads), 0)
        col_ids = lax.broadcasted_iota(jnp.int32, (heads, heads), 1)

        def as_column(ref):
            spread = jnp.where(row_ids == col_ids, ref[...], 0.0)
            return jnp.sum(spread, axis=1, keepdims=True)

        step = jnp.log1p(jnp.exp(raw_ref[...] + as_column(bias_ref)))
        step_ref[...] = step
        rate = step * jnp.exp(as_column(decay_ref))
        piece = 128
        source = lax.broadcasted_iota(jnp.int32, (piece, piece), 0)
        target = lax.broadcasted_iota(jnp.int32, (piece, piece), 1)
        triangle = (source <= target).astype(F32).astype(BF16)
        before = jnp.zeros((heads, 1), F32)
        for start in range(0, length, piece):
            parts = three_parts(rate[:, start : start + piece])
            sums = [jnp.dot(part, triangle, preferred_element_type=F32) for part in parts]
            block = sums[0] + (sums[1] + sums[2]) + before
            total_ref[:, pl.ds(start, piece)] = block
            before = block[:, piece - 1 : piece]
        tail_parts[...] = packed_parts(jnp.exp(total_ref[...] - before) * step)
        end_parts[...] = packed_parts(jnp.broadcast_to(jnp.exp(-before), (heads, 128)))
        first_tail_ref[...] = tail_parts[:, :128]
        fill(maps_ref)
        taps = maps_taps_ref[...].astype(F32)
        for start in range(0, length, tile):
            rows = silu(conv_rows(padded, taps, start, tile))
            maps_conv_ref[pl.ds(start, tile), :] = rows.astype(BF16)

    fill(x_ref)
    taps = x_taps_ref[...].astype(F32)
    selector = head_selector(column * (width // head_dim), heads, head_dim, width)
    for start in range(0, length, tile):
        rows = silu(conv_rows(padded, taps, start, tile)).astype(BF16)
        conv_ref[pl.ds(start, tile), :] = rows
        tail = spread_heads(tail_parts[:, start : start + tile], selector)
        scaled = tail * rows.astype(F32)
        if start == 0:
            ids = lax.broadcasted_iota(jnp.int32, scaled.shape, 0)
            scaled = jnp.where(ids >= held, scaled, 0.0)
        weighted[pl.ds(start, tile), :] = scaled.astype(BF16)
    reached = lax.dot_general(
        maps_conv_ref[:, :state],
        weighted[...],
        (((0,), (0,)), ((), ())),
        preferred_element_type=F32,
    )
    factor = spread_heads(end_parts[:, :8], selector)
    high, middle, low = [part.astype(F32) for part in three_parts(factor)]
    ids = lax.broadcasted_iota(jnp.int32, factor.shape, 0)
    extra = jnp.where(ids == 0, high, jnp.where(ids == 1, middle, jnp.where(ids == 2, low, 0.0)))
    per_column = reached_ref.shape[0] // (width // 128)
    depth = state // per_column
    for piece in range(reached_ref.shape[0]):
        lanes = slice(128 * (piece // per_column), 128 * (piece // per_column) + 128)
        first = depth * (piece % per_column)
        reached_ref[piece, pl.ds(0, depth), :] = reached[first : first + depth, lanes]
        reached_ref[piece, pl.ds(depth, 8), :] = extra[:, lanes]


def local_states(x, x_taps, maps, maps_taps, raw, bias, decay_log, blocks, held):
    length, channels = x.shape
    heads = raw.shape[0]
    maps_width = maps.shape[1]
    width = 256
    columns = channels // width
    taps = x_taps.shape[0]
    state = maps_width // 2
    reached = (blocks, state * channels // (blocks * 128) + 8, 128)
    whole = lambda shape: pl.BlockSpec(shape, lambda i: (0,) * len(shape))
    return pl.pallas_call(
        functools.partial(state_kernel, heads, channels // heads, held),
        grid=(columns,),
        in_specs=[
            pl.BlockSpec((length, width), lambda i: (0, i)),
            pl.BlockSpec((taps, width), lambda i: (0, i)),
            whole((length, maps_width)),
            whole((taps, maps_width)),
            whole((heads, length)),
            whole((1, heads)),
            whole((1, heads)),
        ],
        out_specs=[
            pl.BlockSpec((length, width), lambda i: (0, i)),
            whole((length, maps_width)),
            whole((heads, length)),
            whole((heads, length)),
            whole((3 * heads, 128)),
            pl.BlockSpec((blocks // columns,) + reached[1:], lambda i: (i, 0, 0)),
        ],
        out_shape=[
            pltpu.HBM((length, channels), BF16),
            jax.ShapeDtypeStruct((length, maps_width), BF16),
            jax.ShapeDtypeStruct((heads, length), F32),
            jax.ShapeDtypeStruct((heads, length), F32),
            jax.ShapeDtypeStruct((3 * heads, 128), BF16),
            jax.ShapeDtypeStruct(reached, F32),
        ],
        scratch_shapes=[
            pltpu.VMEM((length + 8, width), F32),
            pltpu.VMEM((3 * heads, length), BF16),
            pltpu.VMEM((3 * heads, 128), BF16),
            pltpu.VMEM((length, width), BF16),
        ],
        compiler_params=params(),
        cost_estimate=pl.CostEstimate(
            flops=5_000_000_000, bytes_accessed=4_000_000, transcendentals=0
        ),
        name="local_states",
    )(x, x_taps, maps, maps_taps, raw, bias, decay_log)


def first_rows_kernel(
    head_dim,
    x_ref,
    maps_ref,
    halo_ref,
    x_taps_ref,
    maps_taps_ref,
    first_tail_ref,
    reached_ref,
    conv_in_ref,
    maps_conv_in_ref,
    conv_ref,
    maps_conv_ref,
    sent_ref,
    padded,
):
    held, channels = x_ref.shape
    maps_width = maps_ref.shape[1]
    leading = halo_ref.shape[0]
    state = maps_width // 2
    heads = first_tail_ref.shape[0] // 3
    padded[pl.ds(8 - leading, leading), :] = halo_ref[...].astype(F32)
    padded[pl.ds(8, held), :channels] = x_ref[...].astype(F32)
    padded[pl.ds(8, held), channels:] = maps_ref[...].astype(F32)
    taps = jnp.concatenate([x_taps_ref[...].astype(F32), maps_taps_ref[...].astype(F32)], axis=1)
    rows = silu(conv_rows(padded, taps, 0, held)).astype(BF16)
    conv_ref[...] = rows[:, :channels]
    maps_conv_ref[...] = rows[:, channels:]
    selector = head_selector(0, heads, head_dim, channels)
    tail = spread_heads(first_tail_ref[:, :held], selector)
    weighted = (tail * rows[:, :channels].astype(F32)).astype(BF16)
    more = lax.dot_general(
        rows[:, channels : channels + state],
        weighted,
        (((0,), (0,)), ((), ())),
        preferred_element_type=F32,
    )
    pieces = sent_ref.shape[0]
    per_column = pieces // (channels // 128)
    depth = state // per_column
    for piece in range(pieces):
        lanes = slice(128 * (piece // per_column), 128 * (piece // per_column) + 128)
        first = depth * (piece % per_column)
        sent_ref[piece] = jnp.concatenate(
            [
                reached_ref[piece, pl.ds(0, depth), :] + more[first : first + depth, lanes],
                reached_ref[piece, pl.ds(depth, 8), :],
            ],
            axis=0,
        ).astype(BF16)


def first_rows(x, maps, halo, x_taps, maps_taps, first_tail, reached, conv, maps_conv, held):
    heads = first_tail.shape[0] // 3
    channels, maps_width = x.shape[1], maps.shape[1]
    whole = lambda array: pl.BlockSpec(array.shape, lambda i: (0,) * array.ndim)
    head = lambda array: pl.BlockSpec((held, array.shape[1]), lambda i: (0, 0))
    near = pl.BlockSpec(memory_space=pltpu.VMEM)
    return pl.pallas_call(
        functools.partial(first_rows_kernel, channels // heads),
        grid=(1,),
        in_specs=[
            head(x),
            head(maps),
            near,
            whole(x_taps),
            whole(maps_taps),
            near,
            near,
            head(conv),
            head(maps_conv),
        ],
        out_specs=[head(conv), head(maps_conv), whole(reached)],
        out_shape=[
            pltpu.HBM(conv.shape, BF16),
            jax.ShapeDtypeStruct(maps_conv.shape, BF16),
            jax.ShapeDtypeStruct(reached.shape, BF16),
        ],
        scratch_shapes=[pltpu.VMEM((held + 8, channels + maps_width), F32)],
        input_output_aliases={7: 0, 8: 1},
        compiler_params=params(),
        name="first_rows",
    )(x, maps, halo, x_taps, maps_taps, first_tail, reached, conv, maps_conv)


def scan_kernel(got_ref, out_ref):
    blocks, rows, lanes = out_ref.shape
    running = jnp.zeros((rows, lanes), F32)
    for block in range(blocks):
        out_ref[block] = running.astype(BF16)
        if block < blocks - 1:
            piece = got_ref[block].astype(F32)
            factor = piece[rows : rows + 1] + (
                piece[rows + 1 : rows + 2] + piece[rows + 2 : rows + 3]
            )
            running = factor * running + piece[:rows]


def scan_blocks(got):
    blocks, rows, lanes = got.shape
    return pl.pallas_call(
        scan_kernel,
        out_shape=jax.ShapeDtypeStruct((blocks, rows - 8, lanes), BF16),
        compiler_params=params(),
        name="scan_blocks",
    )(got)


def local_kernel(
    head_dim, x_ref, maps_ref, z_ref, step_ref, total_ref, skip_ref, shown_ref, passed_ref, scores
):
    pair = pl.program_id(0)
    length, width = x_ref.shape
    state = maps_ref.shape[1] // 2
    per_step = width // head_dim
    tile = 128

    @pl.when(pair == 0)
    def _():
        scores[...] = lax.dot_general(
            maps_ref[:, state:],
            maps_ref[:, :state],
            (((1,), (1,)), ((), ())),
            preferred_element_type=F32,
        )

    later = lax.broadcasted_iota(jnp.int32, (tile, tile), 0)
    earlier = lax.broadcasted_iota(jnp.int32, (tile, tile), 1)
    causal = later >= earlier
    lanes = lax.broadcasted_iota(jnp.int32, (tile, width), 1)
    totals = [total_ref[pl.ds(pair * per_step + head, 1), :] for head in range(per_step)]
    steps = [step_ref[pl.ds(pair * per_step + head, 1), :] for head in range(per_step)]
    skip = skip_ref[pair * per_step]
    for head in range(1, per_step):
        skip = jnp.where(lanes >= head * head_dim, skip_ref[pair * per_step + head], skip)
    for start in range(0, length, tile):
        outs = []
        outer = None
        for head in range(per_step):
            columns = jnp.broadcast_to(totals[head][:, start : start + tile], (tile, tile)).T
            weights = []
            for source in range(0, start + tile, tile):
                spread = totals[head][:, source : source + tile] - columns
                if source == start:
                    spread = jnp.where(causal, spread, -1e30)
                part = jnp.exp(spread) * scores[pl.ds(start, tile), pl.ds(source, tile)]
                part = part * steps[head][:, source : source + tile]
                weights.append(part.astype(BF16))
            weights = weights[0] if len(weights) == 1 else jnp.concatenate(weights, axis=1)
            outs.append(
                jnp.dot(
                    weights,
                    x_ref[pl.ds(0, start + tile), pl.ds(head * head_dim, head_dim)],
                    preferred_element_type=F32,
                )
            )
            fade = jnp.exp(-columns)
            outer = fade if outer is None else jnp.where(lanes >= head * head_dim, fade, outer)
        values = x_ref[pl.ds(start, tile), :].astype(F32)
        gate = silu(z_ref[pl.ds(start, tile), :].astype(F32))
        out = jnp.concatenate(outs, axis=1) + skip * values
        shown_ref[pl.ds(start, tile), :] = (out * gate).astype(BF16)
        passed_ref[pl.ds(start, tile), :] = (outer * gate).astype(BF16)


def local_outputs(x_conv, maps_conv, z, step_rows, total_rows, skip, head_dim):
    length, channels = x_conv.shape
    width = 128
    columns = channels // width
    heads = channels // head_dim
    maps_width = maps_conv.shape[1]
    block = pl.BlockSpec((length, width), lambda i: (0, i))
    row_block = pl.BlockSpec((heads, length), lambda i: (0, 0))
    return pl.pallas_call(
        functools.partial(local_kernel, head_dim),
        grid=(columns,),
        in_specs=[
            block,
            pl.BlockSpec((length, maps_width), lambda i: (0, 0)),
            block,
            row_block,
            row_block,
            pl.BlockSpec(memory_space=pltpu.SMEM),
        ],
        out_specs=[block, block],
        out_shape=[jax.ShapeDtypeStruct((length, channels), BF16)] * 2,
        scratch_shapes=[pltpu.VMEM((length, length), F32)],
        compiler_params=params(),
        cost_estimate=pl.CostEstimate(
            flops=8_000_000_000, bytes_accessed=6_000_000, transcendentals=0
        ),
        name="local_outputs",
    )(x_conv, maps_conv, z, step_rows, total_rows, skip)


def fetches(sources, targets, columns, arrived):
    pieces = 4
    copies = []
    for index, (source, target) in enumerate(zip(sources, targets)):
        depth = target.shape[0] // pieces
        for piece in range(pieces):
            rows = pl.ds(piece * depth, depth)
            copies.append(
                pltpu.make_async_copy(
                    source.at[rows, columns],
                    target.at[rows, :],
                    arrived.at[index * pieces + piece],
                )
            )
    return copies


def norm_kernel(other, carried_ref, maps_ref, shown_ref, passed_ref, gain_ref, *rest):
    copies = []
    if other:
        out_ref, entering = rest
    else:
        sources, out_ref, targets, (entering, arrived) = rest[:2], rest[2], rest[3:5], rest[5:]
        copies = fetches(sources, targets, pl.ds(0, targets[0].shape[1]), arrived)
    for copy in copies:
        copy.start()
    state, channels = entering.shape
    pieces, depth, lanes = carried_ref.shape
    per_column = state // depth
    for piece in range(pieces):
        entering[
            pl.ds(depth * (piece % per_column), depth),
            pl.ds(lanes * (piece // per_column), lanes),
        ] = carried_ref[piece]
    ring = len(TURNS)
    size = out_ref.shape[0] // ring
    place = lax.axis_index("tp")
    across, core = place // 2, lax.rem(place, 2)
    if other:
        core = 1 - core
    for turn, ahead in enumerate(TURNS):
        pick = 2 * lax.rem(across + ahead, ring) + core
        rows = pl.ds(pl.multiple_of(pick * size, size), size)
        carry = jnp.dot(maps_ref[rows, state:], entering[...], preferred_element_type=F32)
        gated = shown_ref[rows, :].astype(F32) + carry * passed_ref[rows, :].astype(F32)
        scale = lax.rsqrt(jnp.mean(gated * gated, axis=1, keepdims=True) + 1e-05)
        out_ref[pl.ds(size * turn, size), :] = (gated * scale * gain_ref[...]).astype(BF16)
    for copy in copies:
        copy.wait()


def normed_rows(other, carried, maps_conv, shown, passed, gain, weights, name):
    length, channels = shown.shape
    state = maps_conv.shape[1] // 2
    near = pl.BlockSpec(memory_space=pltpu.VMEM)
    far = pl.BlockSpec(memory_space=pltpu.HBM)
    normed = jax.ShapeDtypeStruct((length // 2, channels), BF16)
    scratch = [pltpu.VMEM((state, channels), BF16)]
    fetched = []
    if not other:
        fetched = [jax.ShapeDtypeStruct((w.shape[0], w.shape[1] // 2), BF16) for w in weights]
        scratch.append(pltpu.SemaphoreType.DMA((8,)))
    return pl.pallas_call(
        functools.partial(norm_kernel, other),
        in_specs=[near] * 5 + [far] * len(weights),
        out_specs=[near] * (1 + len(fetched)),
        scratch_shapes=scratch,
        out_shape=[normed] + fetched,
        compiler_params=params(),
        cost_estimate=pl.CostEstimate(
            flops=1_000_000_000, bytes_accessed=3_000_000, transcendentals=0
        ),
        name=name,
    )(carried, maps_conv, shown, passed, gain, *[far_memory(weight) for weight in weights])


def project_near_kernel(own_ref, other_ref, own_weight_ref, other_weight_ref, *out_refs):
    rows, columns = out_refs[0].shape
    width = 512
    for start in range(0, columns, width):
        lanes = pl.ds(start, width)
        product = jnp.dot(own_ref[...], own_weight_ref[:, lanes], preferred_element_type=F32)
        product = product + jnp.dot(
            other_ref[...], other_weight_ref[:, lanes], preferred_element_type=F32
        )
        for index, out_ref in enumerate(out_refs):
            piece = product[rows * index : rows * (index + 1)]
            out_ref[:, lanes] = piece.astype(out_ref.dtype)


def project_far_kernel(own_ref, other_ref, own_weight_ref, other_weight_ref, *rest):
    out_refs, (own_near, other_near, total, arrived) = rest[:4], rest[4:]
    rows, columns = out_refs[0].shape
    width = 512
    copies = fetches(
        (own_weight_ref, other_weight_ref),
        (own_near, other_near),
        pl.ds(columns, columns),
        arrived,
    )
    half = len(copies) // 2
    for copy in copies:
        copy.start()
    for copy in copies[:half]:
        copy.wait()
    for start in range(0, columns, width):
        lanes = pl.ds(start, width)
        total[:, lanes] = jnp.dot(
            own_ref[...], own_near[:, lanes], preferred_element_type=F32
        )
    for copy in copies[half:]:
        copy.wait()
    for start in range(0, columns, width):
        lanes = pl.ds(start, width)
        product = total[:, lanes] + jnp.dot(
            other_ref[...], other_near[:, lanes], preferred_element_type=F32
        )
        for index, out_ref in enumerate(out_refs):
            piece = product[rows * index : rows * (index + 1)]
            out_ref[:, lanes] = piece.astype(out_ref.dtype)


def project(own, other, own_weight, other_weight, columns, name):
    count, depth = own.shape
    near = pl.BlockSpec(memory_space=pltpu.VMEM)
    far = own_weight.shape[1] > columns
    weight_spec = pl.BlockSpec(memory_space=pltpu.HBM) if far else near
    weights = [own_weight, other_weight]
    return pl.pallas_call(
        project_far_kernel if far else project_near_kernel,
        in_specs=[near, near, weight_spec, weight_spec],
        out_specs=[near] * 4,
        out_shape=[jax.ShapeDtypeStruct((count // 4, columns), BF16)] * 4,
        scratch_shapes=[
            pltpu.VMEM((depth, columns), BF16),
            pltpu.VMEM((depth, columns), BF16),
            pltpu.VMEM((count, columns), F32),
            pltpu.SemaphoreType.DMA((8,)),
        ]
        if far
        else [],
        compiler_params=params(),
        cost_estimate=pl.CostEstimate(
            flops=4 * count * depth * columns, bytes_accessed=9_000_000, transcendentals=0
        ),
        name=name,
    )(own, other, *([far_memory(weight) for weight in weights] if far else weights))


def on_device(
    x_inputs,
    state_maps,
    z_gate,
    step_raw,
    step_bias,
    decay_log,
    skip_gain,
    x_filter,
    state_filter,
    norm_gain,
    out_weight,
):
    length, channels = x_inputs.shape
    leading = x_filter.shape[0] - 1
    heads = step_raw.shape[1]
    head_dim = channels // heads
    blocks = lax.axis_size("ctx")
    members = lax.axis_size("tp")
    ring = members // 2

    def core_swap(value):
        return lax.ppermute(value, "tp", [(i, i ^ 1) for i in range(members)])

    def along(value, steps):
        pairs = [
            (2 * y + c, 2 * ((y + steps) % ring) + c) for y in range(ring) for c in range(2)
        ]
        return lax.ppermute(value, "tp", pairs)

    ends = jnp.concatenate([x_inputs[length - leading :], state_maps[length - leading :]], axis=1)
    halo = shifted(ends, "ctx", 1)
    x_inputs, state_maps = far_memory(x_inputs), far_memory(state_maps)
    x_filter, state_filter = far_memory(x_filter), far_memory(state_filter)
    held = 16
    conv, maps_conv, step, total, first_tail, reached = local_states(
        x_inputs,
        x_filter,
        state_maps,
        state_filter,
        far_memory(step_raw.T),
        far_memory(step_bias[None]),
        far_memory(decay_log[None]),
        blocks,
        held,
    )
    other_weight = core_swap(lax.optimization_barrier((out_weight, halo, first_tail))[0])
    x_conv, maps_conv, sent = first_rows(
        x_inputs,
        state_maps,
        halo,
        x_filter,
        state_filter,
        first_tail,
        reached,
        conv,
        maps_conv,
        held,
    )
    got = lax.all_to_all(sent, "ctx", 0, 0, tiled=True)
    shown, passed = local_outputs(
        x_conv,
        maps_conv,
        far_memory(z_gate),
        step,
        total,
        skip_gain,
        head_dim,
    )
    got, shown, passed = lax.optimization_barrier((got, shown, passed))
    entering = scan_blocks(got)
    carried = lax.all_to_all(entering, "ctx", 0, 0, tiled=True)

    gain = norm_gain[None]
    weights = (out_weight, other_weight)
    (give,) = normed_rows(True, carried, maps_conv, shown, passed, gain, (), "give_rows")
    taken = core_swap(give)
    keep, own_left, other_left = normed_rows(
        False, carried, maps_conv, shown, passed, gain, weights, "keep_rows"
    )
    columns = own_left.shape[1]
    far_a, up_a, down_a, own_a = project(keep, taken, own_left, other_left, columns, "left_half")
    far_b, up_b, down_b, own_b = project(
        keep, taken, out_weight, other_weight, columns, "right_half"
    )

    def added(*values):
        return functools.reduce(lambda a, b: a + b, [v.astype(F32) for v in values]).astype(BF16)

    relay_a = along(far_a, 1)
    from_above_a = along(down_a, -1)
    relay_b = along(far_b, -1)
    from_below_b = along(up_b, 1)
    from_below_a = along(added(up_a, relay_a), 1)
    from_above_b = along(added(down_b, relay_b), -1)
    return jnp.concatenate(
        [added(own_a, from_above_a, from_below_a), added(own_b, from_above_b, from_below_b)], axis=1
    )


def solution(mesh):
    return jax.shard_map(
        on_device,
        mesh=mesh,
        in_specs=(
            P("ctx", "tp"),
            P("ctx", "tp"),
            P("ctx", "tp"),
            P("ctx", "tp"),
            P("tp"),
            P("tp"),
            P("tp"),
            P(None, "tp"),
            P(None, "tp"),
            P("tp"),
            P("tp", None),
        ),
        out_specs=P(("ctx", "tp"), None),
        check_vma=False,
    )
```

time: 100 us -> 88.5 us (0.89)
  blocking collectives: 0 us -> 17.5 us
  local copies, waits for them, and re-layouts: 16.4 us -> 2.64 us
  waiting for transfers between devices: 26.9 us -> 14.4 us
  starting transfers between devices: 27.8 us -> 23.4 us
  Pallas kernels: 26.2 us -> 27.6 us
    all_to_all x0 -> x1, blocking collectives: none -> 17.5 us  [on_device(): carried = lax.all_to_all(entering, 'ctx', 0, 0, tiled=True)]
    unnamed x31 -> x6, local copies, waits for them, and re-layouts: 14.5 us -> 1.23 us
    all_to_all x1, waiting for transfers between devices: 11.3 us -> 3.48 us  [on_device(): got = lax.all_to_all(sent, 'ctx', 0, 0, tiled=True)]
    all_to_all x1 -> x0, starting transfers between devices: 6.02 us -> none  [on_device(): carried = lax.all_to_all(entering, 'ctx', 0, 0, tiled=True)]
    ppermute x1, waiting for transfers between devices: 4.66 us -> 0.01 us  [shifted(): lax.ppermute(value, axis, [(source, source + steps) for source in range(l...]
    all_to_all x1, starting transfers between devices: 9.01 us -> 10.7 us  [on_device(): got = lax.all_to_all(sent, 'ctx', 0, 0, tiled=True)]
    pallas_call x1, Pallas kernels: 6.48 us -> 7.73 us  [local_outputs(): pl.pallas_call(functools.partial(local_kernel, head_dim), grid=(columns,)...]
    pallas_call x5 -> x6, Pallas kernels: 18.9 us -> 19.7 us  [the longest x2 7.08 us: project(): pl.pallas_call(project_far_kernel if far else project_near_kernel, in_spe...]
  transfers between devices with their start and end apart: 11 -> 10, of which waited for: 4 -> 3; matrix products, arithmetic and copies ran while one was open for 3% -> 0% of each run, Pallas kernels for 22% -> 29%
where the time goes in v3:
time: 88.5 us; the launch traced here: 86.9 us
  Pallas kernels  27.6 us (31%)
  starting transfers between devices  23.4 us (26%)
  blocking collectives  17.5 us (20%)
  waiting for transfers between devices  14.4 us (16%)
  local copies, waits for them, and re-layouts  2.64 us (3%)
  other arithmetic  1.17 us (1%)
    all_to_all x1, blocking collectives, on_device(): carried = lax.all_to_all(entering, 'ctx', 0, 0, tiled=True)  17.5 us
    ppermute x6, waiting for transfers between devices, along(): return lax.ppermute(value, 'tp', pairs)  10.9 us
    all_to_all x1, starting transfers between devices, on_device(): got = lax.all_to_all(sent, 'ctx', 0, 0, tiled=True)  10.7 us
    ppermute x6, starting transfers between devices, along(): return lax.ppermute(value, 'tp', pairs)  8.8 us
    pallas_call x1, Pallas kernels, local_outputs(): pl.pallas_call(functools.partial(local_kernel, head_dim), grid=(columns,)...  7.73 us
    pallas_call x2, Pallas kernels, project(): pl.pallas_call(project_far_kernel if far else project_near_kernel, in_spe...  7.08 us
    pallas_call x1, Pallas kernels, local_states(): pl.pallas_call(functools.partial(state_kernel, heads, channels // heads,...  6.37 us
    pallas_call x2, Pallas kernels, normed_rows(): pl.pallas_call(functools.partial(norm_kernel, other), in_specs=[near] * 5...  4.35 us
  transfers between devices with their start and end apart: 10, of which 3 were waited for; matrix products, arithmetic and copies ran while one was open for 0% of the time, Pallas kernels for 29%

profile of v3, /device:TPU:2, one launch (start us, length us, event | category | flops | bytes accessed | tf_op | source)
XLA Modules:
  0.0 86.9 jit_solution(17838437802104059665)
XLA Ops:
  0.0 0.7 slice.6
  0.7 0.7 slice.7
  1.4 3.8 %collective-permute-start = (bf16[3,1280]{1,0:T(4,128)(2,1)S(1)}, bf16[3,1280]{1,0:T(4,128)(2,1)S(1)}, u32[]{:S(2)}, u32[]{:S(2)}) collective-permute-start(bf16[3,1280]{1,0:T(4,128)(2,1)S(1)} %pad_maximum_fusion.1), channel_id=1, source_target_pairs={{0,8},{8,16},{16,24},{24,32},{32,40},{40,48},{48,56},{56,64},{64,7... | collective-permute-start | bytes 23048 | tf_op jit(solution)/shard_map/ppermute | solution.py:27
  5.3 0.0 copy-start.2
  5.3 6.4 %local_states.1 = (bf16[512,1024]{1,0:T(8,128)(2,1)}, bf16[512,256]{1,0:T(8,128)(2,1)S(1)}, f32[16,512]{1,0:T(8,128)S(1)}, f32[16,512]{1,0:T(8,128)S(1)}, bf16[4...) custom-call(bf16[512,1024]{1,0:T(8,128)(2,1)} %x_ref.3, bf16[4,1024]{1,0:T(4,128)(2,1)} %x_taps_ref.3, ...), custom_call_target="tpu_custom_call" | custom-call | flops 5000000000 | bytes 4000000 | tf_op jit(solution)/shard_map/local_states/pallas_call | solution.py:175
  11.6 0.0 collective-permute-done.halo_ref
  11.6 0.0 collective-permute-start.1
  11.7 1.9 %first_rows.1 = (bf16[512,1024]{1,0:T(8,128)(2,1)}, bf16[512,256]{1,0:T(8,128)(2,1)S(1)}, bf16[32,40,128]{2,1,0:T(8,128)(2,1)}) custom-call(bf16[512,1024]{1,0:T(8,128)(2,1)} %x_ref.3, bf16[512,256]{1,0:T(8,128)(2,1)} %maps_ref.3, bf16[3,1280]{1,0:T(4,128)(2,1)S(1)} %collective-permute-done.halo_ref, ...), custom_call_target="tpu_custom_call", output_to_operand_aliasing={{0}: (7, {}), {1}: (8, {})} | custom-call | tf_op jit(solution)/shard_map/first_rows/pallas_call | solution.py:275
  13.6 10.7 %all-to-all-start = ((bf16[32,40,128]{2,1,0:T(8,128)(2,1)}), bf16[32,40,128]{2,1,0:T(8,128)(2,1)S(1)}, u32[]{:S(2)}, u32[]{:S(2)}) async-start(bf16[32,40,128]{2,1,0:T(8,128)(2,1)} %get-tuple-element.35), calls=%async_computation | async-start | bytes 655360 | tf_op jit(solution)/shard_map/all_to_all | solution.py:620
  24.3 1.2 %copy-done = bf16[512,1024]{1,0:T(8,128)(2,1)S(1)} copy-done((bf16[512,1024]{1,0:T(8,128)(2,1)S(1)}, bf16[512,1024]{1,0:T(8,128)(2,1)}, u32[]{:S(2)}) %copy-start) | copy-done | bytes 1048600
  25.6 7.7 %local_outputs.1 = (bf16[512,1024]{1,0:T(8,128)(2,1)S(1)}, bf16[512,1024]{1,0:T(8,128)(2,1)S(1)}) custom-call(bf16[512,1024]{1,0:T(8,128)(2,1)S(1)} %copy-done, bf16[512,256]{1,0:T(8,128)(2,1)S(1)} %get-tuple-element.37.maps_ref, bf16[512,1024]{1,0:T(8,128)(2,1)} %z_ref.1, f32[16,512]{1,0:T(8,128)S(1)} %get-tuple-element.38.step_ref, ...), custom_call_target="tpu_custom_call" | custom-call | flops 8000000000 | bytes 6000000 | tf_op jit(solution)/shard_map/local_outputs/pallas_call | solution.py:390
  33.3 3.5 %all-to-all-done.got_ref = bf16[32,40,128]{2,1,0:T(8,128)(2,1)S(1)} async-done(((bf16[32,40,128]{2,1,0:T(8,128)(2,1)}), bf16[32,40,128]{2,1,0:T(8,128)(2,1)S(1)}, u32[]{:S(2)}, u32[]{:S(2)}) %all-to-all-start) | async-done | bytes 327712 | tf_op jit(solution)/shard_map/all_to_all | solution.py:620
  36.8 0.1 scan_blocks.1
  36.9 17.5 %all_to_all.10.carried_ref = bf16[32,32,128]{2,1,0:T(8,128)(2,1)S(1)} all-to-all(bf16[32,32,128]{2,1,0:T(8,128)(2,1)S(1)} %scan_blocks.1), channel_id=1, replica_groups=mesh['ctx'=32,'tp'=8] {'ctx'}, dimensions={0} | all-to-all | bytes 524288 | tf_op jit(solution)/shard_map/all_to_all | solution.py:632
  54.4 0.5 give_rows.1
  54.9 0.1 collective-permute-start.2
  55.0 3.8 %keep_rows.1 = (bf16[256,1024]{1,0:T(8,128)(2,1)S(1)}, bf16[1024,2048]{1,0:T(8,128)(2,1)S(1)}, bf16[1024,2048]{1,0:T(8,128)(2,1)S(1)}) custom-call(bf16[32,32,128]{2,1,0:T(8,128)(2,1)S(1)} %all_to_all.10.carried_ref, bf16[512,256]{1,0:T(8,128)(2,1)S(1)} %get-tuple-element.37.maps_ref, bf16[512,1024]{1,0:T(8,128)(2,1)S(1)} %get-tuple-element.43.shown_ref, ...), custom_call_target="tpu_custom_call" | custom-call | flops 1000000000 | bytes 3000000 | tf_op jit(solution)/shard_map/keep_rows/pallas_call | solution.py:474
  58.9 2.4 %left_half.1 = (bf16[64,2048]{1,0:T(8,128)(2,1)S(1)}, bf16[64,2048]{1,0:T(8,128)(2,1)S(1)}, bf16[64,2048]{1,0:T(8,128)(2,1)S(1)}, bf16[64,2048]{1,0:T(8,128)(2,1)S(1)}) custom-call(bf16[256,1024]{1,0:T(8,128)(2,1)S(1)} %get-tuple-element.46.own_ref, bf16[256,1024]{1,0:T(8,128)(2,1)S(1)} %collective-permute-done.2.other_ref, ...), custom_call_target="tpu_custom_call" | custom-call | flops 2147483648 | bytes 9000000 | tf_op jit(solution)/shard_map/left_half/pallas_call | solution.py:540
  61.2 1.7 %collective-permute-start.4 = (bf16[64,2048]{1,0:T(8,128)(2,1)S(1)}, bf16[64,2048]{1,0:T(8,128)(2,1)S(1)}, u32[]{:S(2)}, u32[]{:S(2)}) collective-permute-start(bf16[64,2048]{1,0:T(8,128)(2,1)S(1)} %get-tuple-element.52), channel_id=1, source_target_pairs={{0,2},{1,3},{2,4},{3,5},{4,6},{5,7},{6,0},{7,1},{8,10},{9,11},{10,... | collective-permute-start | bytes 786440 | tf_op jit(solution)/shard_map/ppermute | solution.py:589
  62.9 1.7 %collective-permute-start.3 = (bf16[64,2048]{1,0:T(8,128)(2,1)S(1)}, bf16[64,2048]{1,0:T(8,128)(2,1)S(1)}, u32[]{:S(2)}, u32[]{:S(2)}) collective-permute-start(bf16[64,2048]{1,0:T(8,128)(2,1)S(1)} %get-tuple-element.50), channel_id=1, source_target_pairs={{0,6},{1,7},{2,0},{3,1},{4,2},{5,3},{6,4},{7,5},{8,14},{9,15},{10,... | collective-permute-start | bytes 786440 | tf_op jit(solution)/shard_map/ppermute | solution.py:589
  64.5 4.7 %right_half.1 = (bf16[64,2048]{1,0:T(8,128)(2,1)S(1)}, bf16[64,2048]{1,0:T(8,128)(2,1)S(1)}, bf16[64,2048]{1,0:T(8,128)(2,1)S(1)}, bf16[64,2048]{1,0:T(8,128)(2,1)S(1)}) custom-call(bf16[256,1024]{1,0:T(8,128)(2,1)S(1)} %get-tuple-element.46.own_ref, bf16[256,1024]{1,0:T(8,128)(2,1)S(1)} %collective-permute-done.2.other_ref, ...), custom_call_target="tpu_custom_call" | custom-call | flops 2147483648 | bytes 9000000 | tf_op jit(solution)/shard_map/right_half/pallas_call | solution.py:540
  69.3 1.9 %collective-permute-start.6 = (bf16[64,2048]{1,0:T(8,128)(2,1)S(1)}, bf16[64,2048]{1,0:T(8,128)(2,1)S(1)}, u32[]{:S(2)}, u32[]{:S(2)}) collective-permute-start(bf16[64,2048]{1,0:T(8,128)(2,1)S(1)} %get-tuple-element.55), channel_id=1, source_target_pairs={{0,6},{1,7},{2,0},{3,1},{4,2},{5,3},{6,4},{7,5},{8,14},{9,15},{10,... | collective-permute-start | bytes 786440 | tf_op jit(solution)/shard_map/ppermute | solution.py:589
  71.1 0.2 collective-permute-start.8
  71.4 0.1 add_convert_fusion.3
  71.4 0.4 collective-permute-start.5
  71.9 5.7 %collective-permute-done.6 = bf16[64,2048]{1,0:T(8,128)(2,1)S(1)} collective-permute-done((bf16[64,2048]{1,0:T(8,128)(2,1)S(1)}, bf16[64,2048]{1,0:T(8,128)(2,1)S(1)}, u32[]{:S(2)}, u32[]{:S(2)}) %collective-permute-start.6) | collective-permute-done | bytes 262176 | tf_op jit(solution)/shard_map/ppermute | solution.py:589
  77.6 0.1 add_convert_fusion.1
  77.7 2.9 %collective-permute-start.7 = (bf16[64,2048]{1,0:T(8,128)(2,1)S(1)}, bf16[64,2048]{1,0:T(8,128)(2,1)S(1)}, u32[]{:S(2)}, u32[]{:S(2)}) collective-permute-start(bf16[64,2048]{1,0:T(8,128)(2,1)S(1)} %add_convert_fusion.1), channel_id=1, source_target_pairs={{0,6},{1,7},{2,0},{3,1},{4,2},{5,3},{6,4},{7,5},{8,14},{9,15},{10,... | collective-permute-start | bytes 786440 | tf_op jit(solution)/shard_map/ppermute | solution.py:589
  80.6 5.2 %collective-permute-done.5 = bf16[64,2048]{1,0:T(8,128)(2,1)S(1)} collective-permute-done((bf16[64,2048]{1,0:T(8,128)(2,1)S(1)}, bf16[64,2048]{1,0:T(8,128)(2,1)S(1)}, u32[]{:S(2)}, u32[]{:S(2)}) %collective-permute-start.5) | collective-permute-done | bytes 262176 | tf_op jit(solution)/shard_map/ppermute | solution.py:589
  85.8 0.1 add_convert_fusion.2
  85.9 0.1 add_convert_fusion
  86.0 0.8 pad_maximum_fusion
  (11 shorter events, 0.0 us)
Async XLA Ops:
  1.4 10.2 %collective-permute-start = (bf16[3,1280]{1,0:T(4,128)(2,1)S(1)}, bf16[3,1280]{1,0:T(4,128)(2,1)S(1)}, u32[]{:S(2)}, u32[]{:S(2)}) collective-permute-start(bf16[3,1280]{1,0:T(4,128)(2,1)S(1)} %pad_maximum_fusion.1), channel_id=1, source_target_pairs={{0,8},{8,16},{16,24},{24,32},{32,40},{40,48},{48,56},{56,64},{64,7... | collective-permute-start | bytes 23048 | tf_op jit(solution)/shard_map/ppermute | solution.py:27
  5.3 19.1 %copy-start.2 = (f32[16]{0:T(128)S(1)}, f32[16]{0:T(128)}, u32[]{:S(2)}) copy-start(f32[16]{0:T(128)} %skip_ref.1) | copy-start | bytes 196
  11.6 43.4 %collective-permute-start.1 = (bf16[1024,4096]{1,0:T(8,128)(2,1)}, bf16[1024,4096]{1,0:T(8,128)(2,1)}, u32[]{:S(2)}, u32[]{:S(2)}) collective-permute-start(bf16[1024,4096]{1,0:T(8,128)(2,1)} %own_weight_ref.1), channel_id=1, source_target_pairs={{0,1},{1,0},{2,3},{3,2},{4,5},{5,4},{6,7},{7,6},{8,9},{9,8},{10,11... | collective-permute-start | bytes 25165832 | tf_op jit(solution)/shard_map/ppermute | solution.py:583
  13.6 23.2 %all-to-all-start = ((bf16[32,40,128]{2,1,0:T(8,128)(2,1)}), bf16[32,40,128]{2,1,0:T(8,128)(2,1)S(1)}, u32[]{:S(2)}, u32[]{:S(2)}) async-start(bf16[32,40,128]{2,1,0:T(8,128)(2,1)} %get-tuple-element.35), calls=%async_computation | async-start | bytes 655360 | tf_op jit(solution)/shard_map/all_to_all | solution.py:620
  24.3 1.2 %copy-start = (bf16[512,1024]{1,0:T(8,128)(2,1)S(1)}, bf16[512,1024]{1,0:T(8,128)(2,1)}, u32[]{:S(2)}) copy-start(bf16[512,1024]{1,0:T(8,128)(2,1)} %get-tuple-element.36.x_ref) | copy-start | bytes 3145732
  25.5 28.8 %copy-start.1 = (f32[1024]{0:T(1024)S(1)}, f32[1024]{0:T(1024)}, u32[]{:S(2)}) copy-start(f32[1024]{0:T(1024)} %param.20) | copy-start | bytes 12292
  54.9 3.9 %collective-permute-start.2 = (bf16[256,1024]{1,0:T(8,128)(2,1)S(1)}, bf16[256,1024]{1,0:T(8,128)(2,1)S(1)}, u32[]{:S(2)}, u32[]{:S(2)}) collective-permute-start(bf16[256,1024]{1,0:T(8,128)(2,1)S(1)} %give_rows.1), channel_id=1, source_target_pairs={{0,1},{1,0},{2,3},{3,2},{4,5},{5,4},{6,7},{7,6},{8,9},{9,8},{10,11... | collective-permute-start | bytes 1572872 | tf_op jit(solution)/shard_map/ppermute | solution.py:583
  61.2 10.2 %collective-permute-start.4 = (bf16[64,2048]{1,0:T(8,128)(2,1)S(1)}, bf16[64,2048]{1,0:T(8,128)(2,1)S(1)}, u32[]{:S(2)}, u32[]{:S(2)}) collective-permute-start(bf16[64,2048]{1,0:T(8,128)(2,1)S(1)} %get-tuple-element.52), channel_id=1, source_target_pairs={{0,2},{1,3},{2,4},{3,5},{4,6},{5,7},{6,0},{7,1},{8,10},{9,11},{10,... | collective-permute-start | bytes 786440 | tf_op jit(solution)/shard_map/ppermute | solution.py:589
  62.9 17.8 %collective-permute-start.3 = (bf16[64,2048]{1,0:T(8,128)(2,1)S(1)}, bf16[64,2048]{1,0:T(8,128)(2,1)S(1)}, u32[]{:S(2)}, u32[]{:S(2)}) collective-permute-start(bf16[64,2048]{1,0:T(8,128)(2,1)S(1)} %get-tuple-element.50), channel_id=1, source_target_pairs={{0,6},{1,7},{2,0},{3,1},{4,2},{5,3},{6,4},{7,5},{8,14},{9,15},{10,... | collective-permute-start | bytes 786440 | tf_op jit(solution)/shard_map/ppermute | solution.py:589
  69.3 8.3 %collective-permute-start.6 = (bf16[64,2048]{1,0:T(8,128)(2,1)S(1)}, bf16[64,2048]{1,0:T(8,128)(2,1)S(1)}, u32[]{:S(2)}, u32[]{:S(2)}) collective-permute-start(bf16[64,2048]{1,0:T(8,128)(2,1)S(1)} %get-tuple-element.55), channel_id=1, source_target_pairs={{0,6},{1,7},{2,0},{3,1},{4,2},{5,3},{6,4},{7,5},{8,14},{9,15},{10,... | collective-permute-start | bytes 786440 | tf_op jit(solution)/shard_map/ppermute | solution.py:589
  71.1 14.8 %collective-permute-start.8 = (bf16[64,2048]{1,0:T(8,128)(2,1)S(1)}, bf16[64,2048]{1,0:T(8,128)(2,1)S(1)}, u32[]{:S(2)}, u32[]{:S(2)}) collective-permute-start(bf16[64,2048]{1,0:T(8,128)(2,1)S(1)} %get-tuple-element.56), channel_id=1, source_target_pairs={{0,2},{1,3},{2,4},{3,5},{4,6},{5,7},{6,0},{7,1},{8,10},{9,11},{10,... | collective-permute-start | bytes 786440 | tf_op jit(solution)/shard_map/ppermute | solution.py:589
  71.4 14.4 %collective-permute-start.5 = (bf16[64,2048]{1,0:T(8,128)(2,1)S(1)}, bf16[64,2048]{1,0:T(8,128)(2,1)S(1)}, u32[]{:S(2)}, u32[]{:S(2)}) collective-permute-start(bf16[64,2048]{1,0:T(8,128)(2,1)S(1)} %add_convert_fusion.3), channel_id=1, source_target_pairs={{0,2},{1,3},{2,4},{3,5},{4,6},{5,7},{6,0},{7,1},{8,10},{9,11},{10,... | collective-permute-start | bytes 786440 | tf_op jit(solution)/shard_map/ppermute | solution.py:589
  77.7 8.3 %collective-permute-start.7 = (bf16[64,2048]{1,0:T(8,128)(2,1)S(1)}, bf16[64,2048]{1,0:T(8,128)(2,1)S(1)}, u32[]{:S(2)}, u32[]{:S(2)}) collective-permute-start(bf16[64,2048]{1,0:T(8,128)(2,1)S(1)} %add_convert_fusion.1), channel_id=1, source_target_pairs={{0,6},{1,7},{2,0},{3,1},{4,2},{5,3},{6,4},{7,5},{8,14},{9,15},{10,... | collective-permute-start | bytes 786440 | tf_op jit(solution)/shard_map/ppermute | solution.py:589

commit v4 on v3

--- a/solution.py
+++ b/solution.py
@@ -59,12 +59,16 @@
 
 def conv_rows(padded, taps, start, rows):
     count = taps.shape[0]
-    total = None
-    for offset in range(count):
-        first = 8 - (count - 1) + offset + start
-        term = taps[offset : offset + 1] * padded[pl.ds(first, rows), :]
-        total = term if total is None else total + term
-    return total
+    columns = []
+    for column in range(taps.shape[1] // 128):
+        total = None
+        for offset in range(count):
+            first = 8 - (count - 1) + offset + start
+            weight = taps[offset : offset + 1, 128 * column : 128 * column + 128]
+            term = weight * padded[column, pl.ds(first, rows), :]
+            total = term if total is None else total + term
+        columns.append(total)
+    return columns[0] if len(columns) == 1 else jnp.concatenate(columns, axis=1)
 
 
 def state_kernel(
@@ -91,13 +95,16 @@
 ):
     column = pl.program_id(0)
     length, width = x_ref.shape
-    tile = 64
+    tile = 128
     state = maps_ref.shape[1] // 2
 
     def fill(source):
-        padded[pl.ds(0, 8), :] = jnp.zeros((8, padded.shape[1]), F32)
-        for start in range(0, length, tile):
-            padded[pl.ds(8 + start, tile), :] = source[pl.ds(start, tile), :].astype(F32)
+        for column in range(source.shape[1] // 128):
+            lanes = pl.ds(128 * column, 128)
+            padded[column, pl.ds(0, 8), :] = jnp.zeros((8, 128), F32)
+            for start in range(0, length, tile):
+                rows = pl.ds(8 + start, tile)
+                padded[column, rows, :] = source[pl.ds(start, tile), lanes].astype(F32)
 
     @pl.when(column == 0)
     def _():
@@ -166,7 +173,7 @@
     length, channels = x.shape
     heads = raw.shape[0]
     maps_width = maps.shape[1]
-    width = 256
+    width = 512
     columns = channels // width
     taps = x_taps.shape[0]
     state = maps_width // 2
@@ -201,7 +208,7 @@
             jax.ShapeDtypeStruct(reached, F32),
         ],
         scratch_shapes=[
-            pltpu.VMEM((length + 8, width), F32),
+            pltpu.VMEM((width // 128, length + 8, 128), F32),
             pltpu.VMEM((3 * heads, length), BF16),
             pltpu.VMEM((3 * heads, 128), BF16),
             pltpu.VMEM((length, width), BF16),
@@ -235,9 +242,12 @@
     leading = halo_ref.shape[0]
     state = maps_width // 2
     heads = first_tail_ref.shape[0] // 3
-    padded[pl.ds(8 - leading, leading), :] = halo_ref[...].astype(F32)
-    padded[pl.ds(8, held), :channels] = x_ref[...].astype(F32)
-    padded[pl.ds(8, held), channels:] = maps_ref[...].astype(F32)
+    for column in range(padded.shape[0]):
+        lanes = pl.ds(128 * column, 128)
+        padded[column, pl.ds(8 - leading, leading), :] = halo_ref[:, lanes].astype(F32)
+        source, first = (x_ref, 0) if 128 * column < channels else (maps_ref, channels)
+        lanes = pl.ds(128 * column - first, 128)
+        padded[column, pl.ds(8, held), :] = source[:, lanes].astype(F32)
     taps = jnp.concatenate([x_taps_ref[...].astype(F32), maps_taps_ref[...].astype(F32)], axis=1)
     rows = silu(conv_rows(padded, taps, 0, held)).astype(BF16)
     conv_ref[...] = rows[:, :channels]
@@ -292,7 +302,7 @@
             jax.ShapeDtypeStruct(maps_conv.shape, BF16),
             jax.ShapeDtypeStruct(reached.shape, BF16),
         ],
-        scratch_shapes=[pltpu.VMEM((held + 8, channels + maps_width), F32)],
+        scratch_shapes=[pltpu.VMEM(((channels + maps_width) // 128, held + 8, 128), F32)],
         input_output_aliases={7: 0, 8: 1},
         compiler_params=params(),
         name="first_rows",

time: 88.5 us -> 86.7 us (0.980)
  Pallas kernels: 27.6 us -> 25.8 us
  waiting for transfers between devices: 14.4 us -> 15.3 us
    pallas_call x1, Pallas kernels: 6.37 us -> 4.63 us  [local_states(): pl.pallas_call(functools.partial(state_kernel, heads, channels // heads,...]
    ppermute x1, waiting for transfers between devices: 0.01 us -> 0.9 us  [shifted(): lax.ppermute(value, axis, [(source, source + steps) for source in range(l...]
  transfers between devices with their start and end apart: 10 -> 10, of which waited for: 3 -> 4; matrix products, arithmetic and copies ran while one was open for 0% -> 0% of each run, Pallas kernels for 29% -> 28%
where the time goes in v4:
time: 86.7 us; the launch traced here: 85.1 us
  Pallas kernels  25.8 us (30%)
  starting transfers between devices  22.6 us (26%)
  blocking collectives  17.5 us (20%)
  waiting for transfers between devices  15.3 us (18%)
  local copies, waits for them, and re-layouts  2.64 us (3%)
  other arithmetic  1.17 us (1%)
    all_to_all x1, blocking collectives, on_device(): carried = lax.all_to_all(entering, 'ctx', 0, 0, tiled=True)  17.5 us
    ppermute x6, waiting for transfers between devices, along(): return lax.ppermute(value, 'tp', pairs)  10.9 us
    all_to_all x1, starting transfers between devices, on_device(): got = lax.all_to_all(sent, 'ctx', 0, 0, tiled=True)  9.84 us
    ppermute x6, starting transfers between devices, along(): return lax.ppermute(value, 'tp', pairs)  8.8 us
    pallas_call x1, Pallas kernels, local_outputs(): pl.pallas_call(functools.partial(local_kernel, head_dim), grid=(columns,)...  7.73 us
    pallas_call x2, Pallas kernels, project(): pl.pallas_call(project_far_kernel if far else project_near_kernel, in_spe...  7.08 us
    pallas_call x1, Pallas kernels, local_states(): pl.pallas_call(functools.partial(state_kernel, heads, channels // heads,...  4.63 us
    pallas_call x2, Pallas kernels, normed_rows(): pl.pallas_call(functools.partial(norm_kernel, other), in_specs=[near] * 5...  4.35 us
  transfers between devices with their start and end apart: 10, of which 4 were waited for; matrix products, arithmetic and copies ran while one was open for 0% of the time, Pallas kernels for 28%

profile of v4, /device:TPU:2, one launch (start us, length us, event | category | flops | bytes accessed | tf_op | source)
XLA Modules:
  0.0 85.1 jit_solution(15540879589710990361)
XLA Ops:
  0.0 0.7 slice.6
  0.7 0.7 slice.7
  1.4 3.8 %collective-permute-start = (bf16[3,1280]{1,0:T(4,128)(2,1)S(1)}, bf16[3,1280]{1,0:T(4,128)(2,1)S(1)}, u32[]{:S(2)}, u32[]{:S(2)}) collective-permute-start(bf16[3,1280]{1,0:T(4,128)(2,1)S(1)} %pad_maximum_fusion.1), channel_id=1, source_target_pairs={{0,8},{8,16},{16,24},{24,32},{32,40},{40,48},{48,56},{56,64},{64,7... | collective-permute-start | bytes 23048 | tf_op jit(solution)/shard_map/ppermute | solution.py:27
  5.3 0.0 copy-start.2
  5.3 4.6 %local_states.1 = (bf16[512,1024]{1,0:T(8,128)(2,1)}, bf16[512,256]{1,0:T(8,128)(2,1)S(1)}, f32[16,512]{1,0:T(8,128)S(1)}, f32[16,512]{1,0:T(8,128)S(1)}, bf16[4...) custom-call(bf16[512,1024]{1,0:T(8,128)(2,1)} %x_ref.3, bf16[4,1024]{1,0:T(4,128)(2,1)} %x_taps_ref.3, ...), custom_call_target="tpu_custom_call" | custom-call | flops 5000000000 | bytes 4000000 | tf_op jit(solution)/shard_map/local_states/pallas_call | solution.py:182
  9.9 0.9 %collective-permute-done.halo_ref = bf16[3,1280]{1,0:T(4,128)(2,1)S(1)} collective-permute-done((bf16[3,1280]{1,0:T(4,128)(2,1)S(1)}, bf16[3,1280]{1,0:T(4,128)(2,1)S(1)}, u32[]{:S(2)}, u32[]{:S(2)}) %collective-permute-start) | collective-permute-done | bytes 7712 | tf_op jit(solution)/shard_map/ppermute | solution.py:27
  10.8 0.0 collective-permute-start.1
  10.8 1.9 %first_rows.1 = (bf16[512,1024]{1,0:T(8,128)(2,1)}, bf16[512,256]{1,0:T(8,128)(2,1)S(1)}, bf16[32,40,128]{2,1,0:T(8,128)(2,1)}) custom-call(bf16[512,1024]{1,0:T(8,128)(2,1)} %x_ref.3, bf16[512,256]{1,0:T(8,128)(2,1)} %maps_ref.3, bf16[3,1280]{1,0:T(4,128)(2,1)S(1)} %collective-permute-done.halo_ref, ...), custom_call_target="tpu_custom_call", output_to_operand_aliasing={{0}: (7, {}), {1}: (8, {})} | custom-call | tf_op jit(solution)/shard_map/first_rows/pallas_call | solution.py:285
  12.7 9.8 %all-to-all-start = ((bf16[32,40,128]{2,1,0:T(8,128)(2,1)}), bf16[32,40,128]{2,1,0:T(8,128)(2,1)S(1)}, u32[]{:S(2)}, u32[]{:S(2)}) async-start(bf16[32,40,128]{2,1,0:T(8,128)(2,1)} %get-tuple-element.35), calls=%async_computation | async-start | bytes 655360 | tf_op jit(solution)/shard_map/all_to_all | solution.py:630
  22.6 1.2 %copy-done = bf16[512,1024]{1,0:T(8,128)(2,1)S(1)} copy-done((bf16[512,1024]{1,0:T(8,128)(2,1)S(1)}, bf16[512,1024]{1,0:T(8,128)(2,1)}, u32[]{:S(2)}) %copy-start) | copy-done | bytes 1048600
  23.8 7.7 %local_outputs.1 = (bf16[512,1024]{1,0:T(8,128)(2,1)S(1)}, bf16[512,1024]{1,0:T(8,128)(2,1)S(1)}) custom-call(bf16[512,1024]{1,0:T(8,128)(2,1)S(1)} %copy-done, bf16[512,256]{1,0:T(8,128)(2,1)S(1)} %get-tuple-element.37.maps_ref, bf16[512,1024]{1,0:T(8,128)(2,1)} %z_ref.1, f32[16,512]{1,0:T(8,128)S(1)} %get-tuple-element.38.step_ref, ...), custom_call_target="tpu_custom_call" | custom-call | flops 8000000000 | bytes 6000000 | tf_op jit(solution)/shard_map/local_outputs/pallas_call | solution.py:400
  31.5 3.5 %all-to-all-done.got_ref = bf16[32,40,128]{2,1,0:T(8,128)(2,1)S(1)} async-done(((bf16[32,40,128]{2,1,0:T(8,128)(2,1)}), bf16[32,40,128]{2,1,0:T(8,128)(2,1)S(1)}, u32[]{:S(2)}, u32[]{:S(2)}) %all-to-all-start) | async-done | bytes 327712 | tf_op jit(solution)/shard_map/all_to_all | solution.py:630
  35.0 0.1 scan_blocks.1
  35.1 17.5 %all_to_all.10.carried_ref = bf16[32,32,128]{2,1,0:T(8,128)(2,1)S(1)} all-to-all(bf16[32,32,128]{2,1,0:T(8,128)(2,1)S(1)} %scan_blocks.1), channel_id=1, replica_groups=mesh['ctx'=32,'tp'=8] {'ctx'}, dimensions={0} | all-to-all | bytes 524288 | tf_op jit(solution)/shard_map/all_to_all | solution.py:642
  52.6 0.5 give_rows.1
  53.1 0.1 collective-permute-start.2
  53.3 3.8 %keep_rows.1 = (bf16[256,1024]{1,0:T(8,128)(2,1)S(1)}, bf16[1024,2048]{1,0:T(8,128)(2,1)S(1)}, bf16[1024,2048]{1,0:T(8,128)(2,1)S(1)}) custom-call(bf16[32,32,128]{2,1,0:T(8,128)(2,1)S(1)} %all_to_all.10.carried_ref, bf16[512,256]{1,0:T(8,128)(2,1)S(1)} %get-tuple-element.37.maps_ref, bf16[512,1024]{1,0:T(8,128)(2,1)S(1)} %get-tuple-element.43.shown_ref, ...), custom_call_target="tpu_custom_call" | custom-call | flops 1000000000 | bytes 3000000 | tf_op jit(solution)/shard_map/keep_rows/pallas_call | solution.py:484
  57.1 2.4 %left_half.1 = (bf16[64,2048]{1,0:T(8,128)(2,1)S(1)}, bf16[64,2048]{1,0:T(8,128)(2,1)S(1)}, bf16[64,2048]{1,0:T(8,128)(2,1)S(1)}, bf16[64,2048]{1,0:T(8,128)(2,1)S(1)}) custom-call(bf16[256,1024]{1,0:T(8,128)(2,1)S(1)} %get-tuple-element.46.own_ref, bf16[256,1024]{1,0:T(8,128)(2,1)S(1)} %collective-permute-done.2.other_ref, ...), custom_call_target="tpu_custom_call" | custom-call | flops 2147483648 | bytes 9000000 | tf_op jit(solution)/shard_map/left_half/pallas_call | solution.py:550
  59.5 1.7 %collective-permute-start.4 = (bf16[64,2048]{1,0:T(8,128)(2,1)S(1)}, bf16[64,2048]{1,0:T(8,128)(2,1)S(1)}, u32[]{:S(2)}, u32[]{:S(2)}) collective-permute-start(bf16[64,2048]{1,0:T(8,128)(2,1)S(1)} %get-tuple-element.52), channel_id=1, source_target_pairs={{0,2},{1,3},{2,4},{3,5},{4,6},{5,7},{6,0},{7,1},{8,10},{9,11},{10,... | collective-permute-start | bytes 786440 | tf_op jit(solution)/shard_map/ppermute | solution.py:599
  61.1 1.7 %collective-permute-start.3 = (bf16[64,2048]{1,0:T(8,128)(2,1)S(1)}, bf16[64,2048]{1,0:T(8,128)(2,1)S(1)}, u32[]{:S(2)}, u32[]{:S(2)}) collective-permute-start(bf16[64,2048]{1,0:T(8,128)(2,1)S(1)} %get-tuple-element.50), channel_id=1, source_target_pairs={{0,6},{1,7},{2,0},{3,1},{4,2},{5,3},{6,4},{7,5},{8,14},{9,15},{10,... | collective-permute-start | bytes 786440 | tf_op jit(solution)/shard_map/ppermute | solution.py:599
  62.8 4.7 %right_half.1 = (bf16[64,2048]{1,0:T(8,128)(2,1)S(1)}, bf16[64,2048]{1,0:T(8,128)(2,1)S(1)}, bf16[64,2048]{1,0:T(8,128)(2,1)S(1)}, bf16[64,2048]{1,0:T(8,128)(2,1)S(1)}) custom-call(bf16[256,1024]{1,0:T(8,128)(2,1)S(1)} %get-tuple-element.46.own_ref, bf16[256,1024]{1,0:T(8,128)(2,1)S(1)} %collective-permute-done.2.other_ref, ...), custom_call_target="tpu_custom_call" | custom-call | flops 2147483648 | bytes 9000000 | tf_op jit(solution)/shard_map/right_half/pallas_call | solution.py:550
  67.5 1.9 %collective-permute-start.6 = (bf16[64,2048]{1,0:T(8,128)(2,1)S(1)}, bf16[64,2048]{1,0:T(8,128)(2,1)S(1)}, u32[]{:S(2)}, u32[]{:S(2)}) collective-permute-start(bf16[64,2048]{1,0:T(8,128)(2,1)S(1)} %get-tuple-element.55), channel_id=1, source_target_pairs={{0,6},{1,7},{2,0},{3,1},{4,2},{5,3},{6,4},{7,5},{8,14},{9,15},{10,... | collective-permute-start | bytes 786440 | tf_op jit(solution)/shard_map/ppermute | solution.py:599
  69.4 0.2 collective-permute-start.8
  69.6 0.1 add_convert_fusion.3
  69.7 0.4 collective-permute-start.5
  70.1 5.7 %collective-permute-done.6 = bf16[64,2048]{1,0:T(8,128)(2,1)S(1)} collective-permute-done((bf16[64,2048]{1,0:T(8,128)(2,1)S(1)}, bf16[64,2048]{1,0:T(8,128)(2,1)S(1)}, u32[]{:S(2)}, u32[]{:S(2)}) %collective-permute-start.6) | collective-permute-done | bytes 262176 | tf_op jit(solution)/shard_map/ppermute | solution.py:599
  75.9 0.1 add_convert_fusion.1
  75.9 2.9 %collective-permute-start.7 = (bf16[64,2048]{1,0:T(8,128)(2,1)S(1)}, bf16[64,2048]{1,0:T(8,128)(2,1)S(1)}, u32[]{:S(2)}, u32[]{:S(2)}) collective-permute-start(bf16[64,2048]{1,0:T(8,128)(2,1)S(1)} %add_convert_fusion.1), channel_id=1, source_target_pairs={{0,6},{1,7},{2,0},{3,1},{4,2},{5,3},{6,4},{7,5},{8,14},{9,15},{10,... | collective-permute-start | bytes 786440 | tf_op jit(solution)/shard_map/ppermute | solution.py:599
  78.9 5.2 %collective-permute-done.5 = bf16[64,2048]{1,0:T(8,128)(2,1)S(1)} collective-permute-done((bf16[64,2048]{1,0:T(8,128)(2,1)S(1)}, bf16[64,2048]{1,0:T(8,128)(2,1)S(1)}, u32[]{:S(2)}, u32[]{:S(2)}) %collective-permute-start.5) | collective-permute-done | bytes 262176 | tf_op jit(solution)/shard_map/ppermute | solution.py:599
  84.1 0.1 add_convert_fusion.2
  84.2 0.1 add_convert_fusion
  84.3 0.8 pad_maximum_fusion
  (11 shorter events, 0.0 us)
Async XLA Ops:
  1.4 9.4 %collective-permute-start = (bf16[3,1280]{1,0:T(4,128)(2,1)S(1)}, bf16[3,1280]{1,0:T(4,128)(2,1)S(1)}, u32[]{:S(2)}, u32[]{:S(2)}) collective-permute-start(bf16[3,1280]{1,0:T(4,128)(2,1)S(1)} %pad_maximum_fusion.1), channel_id=1, source_target_pairs={{0,8},{8,16},{16,24},{24,32},{32,40},{40,48},{48,56},{56,64},{64,7... | collective-permute-start | bytes 23048 | tf_op jit(solution)/shard_map/ppermute | solution.py:27
  5.3 17.3 %copy-start.2 = (f32[16]{0:T(128)S(1)}, f32[16]{0:T(128)}, u32[]{:S(2)}) copy-start(f32[16]{0:T(128)} %skip_ref.1) | copy-start | bytes 196
  10.8 42.4 %collective-permute-start.1 = (bf16[1024,4096]{1,0:T(8,128)(2,1)}, bf16[1024,4096]{1,0:T(8,128)(2,1)}, u32[]{:S(2)}, u32[]{:S(2)}) collective-permute-start(bf16[1024,4096]{1,0:T(8,128)(2,1)} %own_weight_ref.1), channel_id=1, source_target_pairs={{0,1},{1,0},{2,3},{3,2},{4,5},{5,4},{6,7},{7,6},{8,9},{9,8},{10,11... | collective-permute-start | bytes 25165832 | tf_op jit(solution)/shard_map/ppermute | solution.py:593
  12.7 22.3 %all-to-all-start = ((bf16[32,40,128]{2,1,0:T(8,128)(2,1)}), bf16[32,40,128]{2,1,0:T(8,128)(2,1)S(1)}, u32[]{:S(2)}, u32[]{:S(2)}) async-start(bf16[32,40,128]{2,1,0:T(8,128)(2,1)} %get-tuple-element.35), calls=%async_computation | async-start | bytes 655360 | tf_op jit(solution)/shard_map/all_to_all | solution.py:630
  22.6 1.2 %copy-start = (bf16[512,1024]{1,0:T(8,128)(2,1)S(1)}, bf16[512,1024]{1,0:T(8,128)(2,1)}, u32[]{:S(2)}) copy-start(bf16[512,1024]{1,0:T(8,128)(2,1)} %get-tuple-element.36.x_ref) | copy-start | bytes 3145732
  23.8 28.8 %copy-start.1 = (f32[1024]{0:T(1024)S(1)}, f32[1024]{0:T(1024)}, u32[]{:S(2)}) copy-start(f32[1024]{0:T(1024)} %param.20) | copy-start | bytes 12292
  53.1 3.9 %collective-permute-start.2 = (bf16[256,1024]{1,0:T(8,128)(2,1)S(1)}, bf16[256,1024]{1,0:T(8,128)(2,1)S(1)}, u32[]{:S(2)}, u32[]{:S(2)}) collective-permute-start(bf16[256,1024]{1,0:T(8,128)(2,1)S(1)} %give_rows.1), channel_id=1, source_target_pairs={{0,1},{1,0},{2,3},{3,2},{4,5},{5,4},{6,7},{7,6},{8,9},{9,8},{10,11... | collective-permute-start | bytes 1572872 | tf_op jit(solution)/shard_map/ppermute | solution.py:593
  59.5 10.2 %collective-permute-start.4 = (bf16[64,2048]{1,0:T(8,128)(2,1)S(1)}, bf16[64,2048]{1,0:T(8,128)(2,1)S(1)}, u32[]{:S(2)}, u32[]{:S(2)}) collective-permute-start(bf16[64,2048]{1,0:T(8,128)(2,1)S(1)} %get-tuple-element.52), channel_id=1, source_target_pairs={{0,2},{1,3},{2,4},{3,5},{4,6},{5,7},{6,0},{7,1},{8,10},{9,11},{10,... | collective-permute-start | bytes 786440 | tf_op jit(solution)/shard_map/ppermute | solution.py:599
  61.1 17.8 %collective-permute-start.3 = (bf16[64,2048]{1,0:T(8,128)(2,1)S(1)}, bf16[64,2048]{1,0:T(8,128)(2,1)S(1)}, u32[]{:S(2)}, u32[]{:S(2)}) collective-permute-start(bf16[64,2048]{1,0:T(8,128)(2,1)S(1)} %get-tuple-element.50), channel_id=1, source_target_pairs={{0,6},{1,7},{2,0},{3,1},{4,2},{5,3},{6,4},{7,5},{8,14},{9,15},{10,... | collective-permute-start | bytes 786440 | tf_op jit(solution)/shard_map/ppermute | solution.py:599
  67.5 8.4 %collective-permute-start.6 = (bf16[64,2048]{1,0:T(8,128)(2,1)S(1)}, bf16[64,2048]{1,0:T(8,128)(2,1)S(1)}, u32[]{:S(2)}, u32[]{:S(2)}) collective-permute-start(bf16[64,2048]{1,0:T(8,128)(2,1)S(1)} %get-tuple-element.55), channel_id=1, source_target_pairs={{0,6},{1,7},{2,0},{3,1},{4,2},{5,3},{6,4},{7,5},{8,14},{9,15},{10,... | collective-permute-start | bytes 786440 | tf_op jit(solution)/shard_map/ppermute | solution.py:599
  69.4 14.8 %collective-permute-start.8 = (bf16[64,2048]{1,0:T(8,128)(2,1)S(1)}, bf16[64,2048]{1,0:T(8,128)(2,1)S(1)}, u32[]{:S(2)}, u32[]{:S(2)}) collective-permute-start(bf16[64,2048]{1,0:T(8,128)(2,1)S(1)} %get-tuple-element.56), channel_id=1, source_target_pairs={{0,2},{1,3},{2,4},{3,5},{4,6},{5,7},{6,0},{7,1},{8,10},{9,11},{10,... | collective-permute-start | bytes 786440 | tf_op jit(solution)/shard_map/ppermute | solution.py:599
  69.7 14.4 %collective-permute-start.5 = (bf16[64,2048]{1,0:T(8,128)(2,1)S(1)}, bf16[64,2048]{1,0:T(8,128)(2,1)S(1)}, u32[]{:S(2)}, u32[]{:S(2)}) collective-permute-start(bf16[64,2048]{1,0:T(8,128)(2,1)S(1)} %add_convert_fusion.3), channel_id=1, source_target_pairs={{0,2},{1,3},{2,4},{3,5},{4,6},{5,7},{6,0},{7,1},{8,10},{9,11},{10,... | collective-permute-start | bytes 786440 | tf_op jit(solution)/shard_map/ppermute | solution.py:599
  75.9 8.3 %collective-permute-start.7 = (bf16[64,2048]{1,0:T(8,128)(2,1)S(1)}, bf16[64,2048]{1,0:T(8,128)(2,1)S(1)}, u32[]{:S(2)}, u32[]{:S(2)}) collective-permute-start(bf16[64,2048]{1,0:T(8,128)(2,1)S(1)} %add_convert_fusion.1), channel_id=1, source_target_pairs={{0,6},{1,7},{2,0},{3,1},{4,2},{5,3},{6,4},{7,5},{8,14},{9,15},{10,... | collective-permute-start | bytes 786440 | tf_op jit(solution)/shard_map/ppermute | solution.py:599

commit v5 on v4

--- a/solution.py
+++ b/solution.py
@@ -293,8 +293,8 @@
             whole(maps_taps),
             near,
             near,
-            head(conv),
-            head(maps_conv),
+            pl.BlockSpec(memory_space=pl.ANY),
+            pl.BlockSpec(memory_space=pl.ANY),
         ],
         out_specs=[head(conv), head(maps_conv), whole(reached)],
         out_shape=[
@@ -568,6 +568,29 @@
     )(own, other, *([far_memory(weight) for weight in weights] if far else weights))
 
 
+def last_rows_kernel(x_ref, maps_ref, out_ref):
+    count = out_ref.shape[0]
+    channels = x_ref.shape[1]
+    first = x_ref.shape[0] - count
+    out_ref[:, :channels] = x_ref[...].astype(F32)[first:].astype(BF16)
+    out_ref[:, channels:] = maps_ref[...].astype(F32)[first:].astype(BF16)
+
+
+def last_rows(x, maps, count, held):
+    last = x.shape[0] // held - 1
+    tail = lambda array: pl.BlockSpec((held, array.shape[1]), lambda i: (last, 0))
+    shape = (count, x.shape[1] + maps.shape[1])
+    return pl.pallas_call(
+        last_rows_kernel,
+        grid=(1,),
+        in_specs=[tail(x), tail(maps)],
+        out_specs=pl.BlockSpec(memory_space=pltpu.VMEM),
+        out_shape=jax.ShapeDtypeStruct(shape, BF16),
+        compiler_params=params(),
+        name="last_rows",
+    )(x, maps)
+
+
 def on_device(
     x_inputs,
     state_maps,
@@ -598,11 +621,10 @@
         ]
         return lax.ppermute(value, "tp", pairs)
 
-    ends = jnp.concatenate([x_inputs[length - leading :], state_maps[length - leading :]], axis=1)
-    halo = shifted(ends, "ctx", 1)
+    held = 16
     x_inputs, state_maps = far_memory(x_inputs), far_memory(state_maps)
+    halo = shifted(last_rows(x_inputs, state_maps, leading, held), "ctx", 1)
     x_filter, state_filter = far_memory(x_filter), far_memory(state_filter)
-    held = 16
     conv, maps_conv, step, total, first_tail, reached = local_states(
         x_inputs,
         x_filter,

time: 86.7 us -> 86 us (level)
  local copies, waits for them, and re-layouts: 2.64 us -> 1.23 us
    slice x2 -> x0, local copies, waits for them, and re-layouts: 1.41 us -> none  [the longest x1 0.72 us: on_device(): x_inputs[length - leading:]]
where the time goes in v5:
time: 86 us; the launch traced here: 84.5 us
  Pallas kernels  26.5 us (31%)
  starting transfers between devices  22.6 us (26%)
  blocking collectives  17.5 us (20%)
  waiting for transfers between devices  15.3 us (18%)
  local copies, waits for them, and re-layouts  1.23 us (1%)
  other arithmetic  1.16 us (1%)
    all_to_all x1, blocking collectives, on_device(): carried = lax.all_to_all(entering, 'ctx', 0, 0, tiled=True)  17.5 us
    ppermute x6, waiting for transfers between devices, along(): return lax.ppermute(value, 'tp', pairs)  10.9 us
    all_to_all x1, starting transfers between devices, on_device(): got = lax.all_to_all(sent, 'ctx', 0, 0, tiled=True)  9.84 us
    ppermute x6, starting transfers between devices, along(): return lax.ppermute(value, 'tp', pairs)  8.8 us
    pallas_call x1, Pallas kernels, local_outputs(): pl.pallas_call(functools.partial(local_kernel, head_dim), grid=(columns,)...  7.73 us
    pallas_call x2, Pallas kernels, project(): pl.pallas_call(project_far_kernel if far else project_near_kernel, in_spe...  7.08 us
    pallas_call x1, Pallas kernels, local_states(): pl.pallas_call(functools.partial(state_kernel, heads, channels // heads,...  4.63 us
    pallas_call x2, Pallas kernels, normed_rows(): pl.pallas_call(functools.partial(norm_kernel, other), in_specs=[near] * 5...  4.35 us
  transfers between devices with their start and end apart: 10, of which 4 were waited for; matrix products, arithmetic and copies ran while one was open for 0% of the time, Pallas kernels for 28%

profile of v5, /device:TPU:2, one launch (start us, length us, event | category | flops | bytes accessed | tf_op | source)
XLA Modules:
  0.0 84.5 jit_solution(1143187872791762426)
XLA Ops:
  0.0 0.8 last_rows.1
  0.8 3.8 %collective-permute-start = (bf16[3,1280]{1,0:T(4,128)(2,1)S(1)}, bf16[3,1280]{1,0:T(4,128)(2,1)S(1)}, u32[]{:S(2)}, u32[]{:S(2)}) collective-permute-start(bf16[3,1280]{1,0:T(4,128)(2,1)S(1)} %last_rows.1), channel_id=1, source_target_pairs={{0,8},{8,16},{16,24},{24,32},{32,40},{40,48},{48,56},{56,64},{64,7... | collective-permute-start | bytes 23048 | tf_op jit(solution)/shard_map/ppermute | solution.py:27
  4.6 0.0 copy-start.2
  4.6 4.6 %local_states.1 = (bf16[512,1024]{1,0:T(8,128)(2,1)}, bf16[512,256]{1,0:T(8,128)(2,1)S(1)}, f32[16,512]{1,0:T(8,128)S(1)}, f32[16,512]{1,0:T(8,128)S(1)}, bf16[4...) custom-call(bf16[512,1024]{1,0:T(8,128)(2,1)} %x_ref.5, bf16[4,1024]{1,0:T(4,128)(2,1)} %x_taps_ref.3, ...), custom_call_target="tpu_custom_call" | custom-call | flops 5000000000 | bytes 4000000 | tf_op jit(solution)/shard_map/local_states/pallas_call | solution.py:182
  9.3 0.9 %collective-permute-done.halo_ref = bf16[3,1280]{1,0:T(4,128)(2,1)S(1)} collective-permute-done((bf16[3,1280]{1,0:T(4,128)(2,1)S(1)}, bf16[3,1280]{1,0:T(4,128)(2,1)S(1)}, u32[]{:S(2)}, u32[]{:S(2)}) %collective-permute-start) | collective-permute-done | bytes 7712 | tf_op jit(solution)/shard_map/ppermute | solution.py:27
  10.2 0.0 collective-permute-start.1
  10.2 1.9 %first_rows.1 = (bf16[512,1024]{1,0:T(8,128)(2,1)}, bf16[512,256]{1,0:T(8,128)(2,1)S(1)}, bf16[32,40,128]{2,1,0:T(8,128)(2,1)}) custom-call(bf16[512,1024]{1,0:T(8,128)(2,1)} %x_ref.5, bf16[512,256]{1,0:T(8,128)(2,1)} %maps_ref.5, bf16[3,1280]{1,0:T(4,128)(2,1)S(1)} %collective-permute-done.halo_ref, ...), custom_call_target="tpu_custom_call", output_to_operand_aliasing={{0}: (7, {}), {1}: (8, {})} | custom-call | tf_op jit(solution)/shard_map/first_rows/pallas_call | solution.py:285
  12.0 9.8 %all-to-all-start = ((bf16[32,40,128]{2,1,0:T(8,128)(2,1)}), bf16[32,40,128]{2,1,0:T(8,128)(2,1)S(1)}, u32[]{:S(2)}, u32[]{:S(2)}) async-start(bf16[32,40,128]{2,1,0:T(8,128)(2,1)} %get-tuple-element.35), calls=%async_computation | async-start | bytes 655360 | tf_op jit(solution)/shard_map/all_to_all | solution.py:652
  21.9 1.2 %copy-done = bf16[512,1024]{1,0:T(8,128)(2,1)S(1)} copy-done((bf16[512,1024]{1,0:T(8,128)(2,1)S(1)}, bf16[512,1024]{1,0:T(8,128)(2,1)}, u32[]{:S(2)}) %copy-start) | copy-done | bytes 1048600
  23.1 7.7 %local_outputs.1 = (bf16[512,1024]{1,0:T(8,128)(2,1)S(1)}, bf16[512,1024]{1,0:T(8,128)(2,1)S(1)}) custom-call(bf16[512,1024]{1,0:T(8,128)(2,1)S(1)} %copy-done, bf16[512,256]{1,0:T(8,128)(2,1)S(1)} %get-tuple-element.37.maps_ref, bf16[512,1024]{1,0:T(8,128)(2,1)} %z_ref.1, f32[16,512]{1,0:T(8,128)S(1)} %get-tuple-element.38.step_ref, ...), custom_call_target="tpu_custom_call" | custom-call | flops 8000000000 | bytes 6000000 | tf_op jit(solution)/shard_map/local_outputs/pallas_call | solution.py:400
  30.9 3.5 %all-to-all-done.got_ref = bf16[32,40,128]{2,1,0:T(8,128)(2,1)S(1)} async-done(((bf16[32,40,128]{2,1,0:T(8,128)(2,1)}), bf16[32,40,128]{2,1,0:T(8,128)(2,1)S(1)}, u32[]{:S(2)}, u32[]{:S(2)}) %all-to-all-start) | async-done | bytes 327712 | tf_op jit(solution)/shard_map/all_to_all | solution.py:652
  34.3 0.1 scan_blocks.1
  34.4 17.5 %all_to_all.10.carried_ref = bf16[32,32,128]{2,1,0:T(8,128)(2,1)S(1)} all-to-all(bf16[32,32,128]{2,1,0:T(8,128)(2,1)S(1)} %scan_blocks.1), channel_id=1, replica_groups=mesh['ctx'=32,'tp'=8] {'ctx'}, dimensions={0} | all-to-all | bytes 524288 | tf_op jit(solution)/shard_map/all_to_all | solution.py:664
  51.9 0.5 give_rows.1
  52.5 0.1 collective-permute-start.2
  52.6 3.8 %keep_rows.1 = (bf16[256,1024]{1,0:T(8,128)(2,1)S(1)}, bf16[1024,2048]{1,0:T(8,128)(2,1)S(1)}, bf16[1024,2048]{1,0:T(8,128)(2,1)S(1)}) custom-call(bf16[32,32,128]{2,1,0:T(8,128)(2,1)S(1)} %all_to_all.10.carried_ref, bf16[512,256]{1,0:T(8,128)(2,1)S(1)} %get-tuple-element.37.maps_ref, bf16[512,1024]{1,0:T(8,128)(2,1)S(1)} %get-tuple-element.43.shown_ref, ...), custom_call_target="tpu_custom_call" | custom-call | flops 1000000000 | bytes 3000000 | tf_op jit(solution)/shard_map/keep_rows/pallas_call | solution.py:484
  56.4 2.4 %left_half.1 = (bf16[64,2048]{1,0:T(8,128)(2,1)S(1)}, bf16[64,2048]{1,0:T(8,128)(2,1)S(1)}, bf16[64,2048]{1,0:T(8,128)(2,1)S(1)}, bf16[64,2048]{1,0:T(8,128)(2,1)S(1)}) custom-call(bf16[256,1024]{1,0:T(8,128)(2,1)S(1)} %get-tuple-element.46.own_ref, bf16[256,1024]{1,0:T(8,128)(2,1)S(1)} %collective-permute-done.2.other_ref, ...), custom_call_target="tpu_custom_call" | custom-call | flops 2147483648 | bytes 9000000 | tf_op jit(solution)/shard_map/left_half/pallas_call | solution.py:550
  58.8 1.7 %collective-permute-start.4 = (bf16[64,2048]{1,0:T(8,128)(2,1)S(1)}, bf16[64,2048]{1,0:T(8,128)(2,1)S(1)}, u32[]{:S(2)}, u32[]{:S(2)}) collective-permute-start(bf16[64,2048]{1,0:T(8,128)(2,1)S(1)} %get-tuple-element.52), channel_id=1, source_target_pairs={{0,2},{1,3},{2,4},{3,5},{4,6},{5,7},{6,0},{7,1},{8,10},{9,11},{10,... | collective-permute-start | bytes 786440 | tf_op jit(solution)/shard_map/ppermute | solution.py:622
  60.4 1.7 %collective-permute-start.3 = (bf16[64,2048]{1,0:T(8,128)(2,1)S(1)}, bf16[64,2048]{1,0:T(8,128)(2,1)S(1)}, u32[]{:S(2)}, u32[]{:S(2)}) collective-permute-start(bf16[64,2048]{1,0:T(8,128)(2,1)S(1)} %get-tuple-element.50), channel_id=1, source_target_pairs={{0,6},{1,7},{2,0},{3,1},{4,2},{5,3},{6,4},{7,5},{8,14},{9,15},{10,... | collective-permute-start | bytes 786440 | tf_op jit(solution)/shard_map/ppermute | solution.py:622
  62.1 4.7 %right_half.1 = (bf16[64,2048]{1,0:T(8,128)(2,1)S(1)}, bf16[64,2048]{1,0:T(8,128)(2,1)S(1)}, bf16[64,2048]{1,0:T(8,128)(2,1)S(1)}, bf16[64,2048]{1,0:T(8,128)(2,1)S(1)}) custom-call(bf16[256,1024]{1,0:T(8,128)(2,1)S(1)} %get-tuple-element.46.own_ref, bf16[256,1024]{1,0:T(8,128)(2,1)S(1)} %collective-permute-done.2.other_ref, ...), custom_call_target="tpu_custom_call" | custom-call | flops 2147483648 | bytes 9000000 | tf_op jit(solution)/shard_map/right_half/pallas_call | solution.py:550
  66.8 1.9 %collective-permute-start.6 = (bf16[64,2048]{1,0:T(8,128)(2,1)S(1)}, bf16[64,2048]{1,0:T(8,128)(2,1)S(1)}, u32[]{:S(2)}, u32[]{:S(2)}) collective-permute-start(bf16[64,2048]{1,0:T(8,128)(2,1)S(1)} %get-tuple-element.55), channel_id=1, source_target_pairs={{0,6},{1,7},{2,0},{3,1},{4,2},{5,3},{6,4},{7,5},{8,14},{9,15},{10,... | collective-permute-start | bytes 786440 | tf_op jit(solution)/shard_map/ppermute | solution.py:622
  68.7 0.2 collective-permute-start.8
  68.9 0.1 add_convert_fusion.3
  69.0 0.4 collective-permute-start.5
  69.4 5.7 %collective-permute-done.6 = bf16[64,2048]{1,0:T(8,128)(2,1)S(1)} collective-permute-done((bf16[64,2048]{1,0:T(8,128)(2,1)S(1)}, bf16[64,2048]{1,0:T(8,128)(2,1)S(1)}, u32[]{:S(2)}, u32[]{:S(2)}) %collective-permute-start.6) | collective-permute-done | bytes 262176 | tf_op jit(solution)/shard_map/ppermute | solution.py:622
  75.2 0.1 add_convert_fusion.1
  75.3 2.9 %collective-permute-start.7 = (bf16[64,2048]{1,0:T(8,128)(2,1)S(1)}, bf16[64,2048]{1,0:T(8,128)(2,1)S(1)}, u32[]{:S(2)}, u32[]{:S(2)}) collective-permute-start(bf16[64,2048]{1,0:T(8,128)(2,1)S(1)} %add_convert_fusion.1), channel_id=1, source_target_pairs={{0,6},{1,7},{2,0},{3,1},{4,2},{5,3},{6,4},{7,5},{8,14},{9,15},{10,... | collective-permute-start | bytes 786440 | tf_op jit(solution)/shard_map/ppermute | solution.py:622
  78.2 5.2 %collective-permute-done.5 = bf16[64,2048]{1,0:T(8,128)(2,1)S(1)} collective-permute-done((bf16[64,2048]{1,0:T(8,128)(2,1)S(1)}, bf16[64,2048]{1,0:T(8,128)(2,1)S(1)}, u32[]{:S(2)}, u32[]{:S(2)}) %collective-permute-start.5) | collective-permute-done | bytes 262176 | tf_op jit(solution)/shard_map/ppermute | solution.py:622
  83.4 0.1 add_convert_fusion.2
  83.5 0.0 collective-permute-done.8
  83.5 0.1 add_convert_fusion
  83.6 0.8 pad_maximum_fusion
  (9 shorter events, 0.0 us)
Async XLA Ops:
  0.8 9.4 %collective-permute-start = (bf16[3,1280]{1,0:T(4,128)(2,1)S(1)}, bf16[3,1280]{1,0:T(4,128)(2,1)S(1)}, u32[]{:S(2)}, u32[]{:S(2)}) collective-permute-start(bf16[3,1280]{1,0:T(4,128)(2,1)S(1)} %last_rows.1), channel_id=1, source_target_pairs={{0,8},{8,16},{16,24},{24,32},{32,40},{40,48},{48,56},{56,64},{64,7... | collective-permute-start | bytes 23048 | tf_op jit(solution)/shard_map/ppermute | solution.py:27
  4.6 17.3 %copy-start.2 = (f32[16]{0:T(128)S(1)}, f32[16]{0:T(128)}, u32[]{:S(2)}) copy-start(f32[16]{0:T(128)} %skip_ref.1) | copy-start | bytes 196
  10.2 42.4 %collective-permute-start.1 = (bf16[1024,4096]{1,0:T(8,128)(2,1)}, bf16[1024,4096]{1,0:T(8,128)(2,1)}, u32[]{:S(2)}, u32[]{:S(2)}) collective-permute-start(bf16[1024,4096]{1,0:T(8,128)(2,1)} %own_weight_ref.1), channel_id=1, source_target_pairs={{0,1},{1,0},{2,3},{3,2},{4,5},{5,4},{6,7},{7,6},{8,9},{9,8},{10,11... | collective-permute-start | bytes 25165832 | tf_op jit(solution)/shard_map/ppermute | solution.py:616
  12.0 22.3 %all-to-all-start = ((bf16[32,40,128]{2,1,0:T(8,128)(2,1)}), bf16[32,40,128]{2,1,0:T(8,128)(2,1)S(1)}, u32[]{:S(2)}, u32[]{:S(2)}) async-start(bf16[32,40,128]{2,1,0:T(8,128)(2,1)} %get-tuple-element.35), calls=%async_computation | async-start | bytes 655360 | tf_op jit(solution)/shard_map/all_to_all | solution.py:652
  21.9 1.2 %copy-start = (bf16[512,1024]{1,0:T(8,128)(2,1)S(1)}, bf16[512,1024]{1,0:T(8,128)(2,1)}, u32[]{:S(2)}) copy-start(bf16[512,1024]{1,0:T(8,128)(2,1)} %get-tuple-element.36.x_ref) | copy-start | bytes 3145732
  23.1 28.8 %copy-start.1 = (f32[1024]{0:T(1024)S(1)}, f32[1024]{0:T(1024)}, u32[]{:S(2)}) copy-start(f32[1024]{0:T(1024)} %param.20) | copy-start | bytes 12292
  52.5 3.9 %collective-permute-start.2 = (bf16[256,1024]{1,0:T(8,128)(2,1)S(1)}, bf16[256,1024]{1,0:T(8,128)(2,1)S(1)}, u32[]{:S(2)}, u32[]{:S(2)}) collective-permute-start(bf16[256,1024]{1,0:T(8,128)(2,1)S(1)} %give_rows.1), channel_id=1, source_target_pairs={{0,1},{1,0},{2,3},{3,2},{4,5},{5,4},{6,7},{7,6},{8,9},{9,8},{10,11... | collective-permute-start | bytes 1572872 | tf_op jit(solution)/shard_map/ppermute | solution.py:616
  58.8 10.2 %collective-permute-start.4 = (bf16[64,2048]{1,0:T(8,128)(2,1)S(1)}, bf16[64,2048]{1,0:T(8,128)(2,1)S(1)}, u32[]{:S(2)}, u32[]{:S(2)}) collective-permute-start(bf16[64,2048]{1,0:T(8,128)(2,1)S(1)} %get-tuple-element.52), channel_id=1, source_target_pairs={{0,2},{1,3},{2,4},{3,5},{4,6},{5,7},{6,0},{7,1},{8,10},{9,11},{10,... | collective-permute-start | bytes 786440 | tf_op jit(solution)/shard_map/ppermute | solution.py:622
  60.4 17.8 %collective-permute-start.3 = (bf16[64,2048]{1,0:T(8,128)(2,1)S(1)}, bf16[64,2048]{1,0:T(8,128)(2,1)S(1)}, u32[]{:S(2)}, u32[]{:S(2)}) collective-permute-start(bf16[64,2048]{1,0:T(8,128)(2,1)S(1)} %get-tuple-element.50), channel_id=1, source_target_pairs={{0,6},{1,7},{2,0},{3,1},{4,2},{5,3},{6,4},{7,5},{8,14},{9,15},{10,... | collective-permute-start | bytes 786440 | tf_op jit(solution)/shard_map/ppermute | solution.py:622
  66.8 8.4 %collective-permute-start.6 = (bf16[64,2048]{1,0:T(8,128)(2,1)S(1)}, bf16[64,2048]{1,0:T(8,128)(2,1)S(1)}, u32[]{:S(2)}, u32[]{:S(2)}) collective-permute-start(bf16[64,2048]{1,0:T(8,128)(2,1)S(1)} %get-tuple-element.55), channel_id=1, source_target_pairs={{0,6},{1,7},{2,0},{3,1},{4,2},{5,3},{6,4},{7,5},{8,14},{9,15},{10,... | collective-permute-start | bytes 786440 | tf_op jit(solution)/shard_map/ppermute | solution.py:622
  68.7 14.8 %collective-permute-start.8 = (bf16[64,2048]{1,0:T(8,128)(2,1)S(1)}, bf16[64,2048]{1,0:T(8,128)(2,1)S(1)}, u32[]{:S(2)}, u32[]{:S(2)}) collective-permute-start(bf16[64,2048]{1,0:T(8,128)(2,1)S(1)} %get-tuple-element.56), channel_id=1, source_target_pairs={{0,2},{1,3},{2,4},{3,5},{4,6},{5,7},{6,0},{7,1},{8,10},{9,11},{10,... | collective-permute-start | bytes 786440 | tf_op jit(solution)/shard_map/ppermute | solution.py:622
  69.0 14.4 %collective-permute-start.5 = (bf16[64,2048]{1,0:T(8,128)(2,1)S(1)}, bf16[64,2048]{1,0:T(8,128)(2,1)S(1)}, u32[]{:S(2)}, u32[]{:S(2)}) collective-permute-start(bf16[64,2048]{1,0:T(8,128)(2,1)S(1)} %add_convert_fusion.3), channel_id=1, source_target_pairs={{0,2},{1,3},{2,4},{3,5},{4,6},{5,7},{6,0},{7,1},{8,10},{9,11},{10,... | collective-permute-start | bytes 786440 | tf_op jit(solution)/shard_map/ppermute | solution.py:622
  75.3 8.3 %collective-permute-start.7 = (bf16[64,2048]{1,0:T(8,128)(2,1)S(1)}, bf16[64,2048]{1,0:T(8,128)(2,1)S(1)}, u32[]{:S(2)}, u32[]{:S(2)}) collective-permute-start(bf16[64,2048]{1,0:T(8,128)(2,1)S(1)} %add_convert_fusion.1), channel_id=1, source_target_pairs={{0,6},{1,7},{2,0},{3,1},{4,2},{5,3},{6,4},{7,5},{8,14},{9,15},{10,... | collective-permute-start | bytes 786440 | tf_op jit(solution)/shard_map/ppermute | solution.py:622

commit v6 on v5

--- a/solution.py
+++ b/solution.py
@@ -510,30 +510,30 @@
 
 
 def project_far_kernel(own_ref, other_ref, own_weight_ref, other_weight_ref, *rest):
-    out_refs, (own_near, other_near, total, arrived) = rest[:4], rest[4:]
+    out_refs, (own_near, other_near, arrived) = rest[:4], rest[4:]
     rows, columns = out_refs[0].shape
     width = 512
-    copies = fetches(
-        (own_weight_ref, other_weight_ref),
-        (own_near, other_near),
-        pl.ds(columns, columns),
-        arrived,
-    )
-    half = len(copies) // 2
+    first = own_weight_ref.shape[1] - columns
+    copies = []
+    for tile in range(columns // width):
+        for index, (source, target) in enumerate(
+            ((own_weight_ref, own_near), (other_weight_ref, other_near))
+        ):
+            copies.append(
+                pltpu.make_async_copy(
+                    source.at[:, pl.ds(first + tile * width, width)],
+                    target.at[:, pl.ds(tile * width, width)],
+                    arrived.at[2 * tile + index],
+                )
+            )
     for copy in copies:
         copy.start()
-    for copy in copies[:half]:
-        copy.wait()
-    for start in range(0, columns, width):
-        lanes = pl.ds(start, width)
-        total[:, lanes] = jnp.dot(
-            own_ref[...], own_near[:, lanes], preferred_element_type=F32
-        )
-    for copy in copies[half:]:
-        copy.wait()
-    for start in range(0, columns, width):
-        lanes = pl.ds(start, width)
-        product = total[:, lanes] + jnp.dot(
+    for tile in range(columns // width):
+        lanes = pl.ds(tile * width, width)
+        copies[2 * tile].wait()
+        copies[2 * tile + 1].wait()
+        product = jnp.dot(own_ref[...], own_near[:, lanes], preferred_element_type=F32)
+        product = product + jnp.dot(
             other_ref[...], other_near[:, lanes], preferred_element_type=F32
         )
         for index, out_ref in enumerate(out_refs):
@@ -555,7 +555,6 @@
         scratch_shapes=[
             pltpu.VMEM((depth, columns), BF16),
             pltpu.VMEM((depth, columns), BF16),
-            pltpu.VMEM((count, columns), F32),
             pltpu.SemaphoreType.DMA((8,)),
         ]
         if far

time: 86 us -> 85.8 us (level)
  transfers between devices with their start and end apart: 10 -> 10, of which waited for: 4 -> 5; matrix products, arithmetic and copies ran while one was open for 0% -> 0% of each run, Pallas kernels for 28% -> 28%
where the time goes in v6:
time: 85.8 us; the launch traced here: 84.2 us
  Pallas kernels  26.3 us (31%)
  starting transfers between devices  22.5 us (26%)
  blocking collectives  17.5 us (20%)
  waiting for transfers between devices  15.4 us (18%)
  local copies, waits for them, and re-layouts  1.23 us (1%)
  other arithmetic  1.16 us (1%)
    all_to_all x1, blocking collectives, on_device(): carried = lax.all_to_all(entering, 'ctx', 0, 0, tiled=True)  17.5 us
    ppermute x6, waiting for transfers between devices, along(): return lax.ppermute(value, 'tp', pairs)  11 us
    all_to_all x1, starting transfers between devices, on_device(): got = lax.all_to_all(sent, 'ctx', 0, 0, tiled=True)  9.84 us
    ppermute x6, starting transfers between devices, along(): return lax.ppermute(value, 'tp', pairs)  8.76 us
    pallas_call x1, Pallas kernels, local_outputs(): pl.pallas_call(functools.partial(local_kernel, head_dim), grid=(columns,)...  7.73 us
    pallas_call x2, Pallas kernels, project(): pl.pallas_call(project_far_kernel if far else project_near_kernel, in_spe...  6.84 us
    pallas_call x1, Pallas kernels, local_states(): pl.pallas_call(functools.partial(state_kernel, heads, channels // heads,...  4.63 us
    pallas_call x2, Pallas kernels, normed_rows(): pl.pallas_call(functools.partial(norm_kernel, other), in_specs=[near] * 5...  4.35 us
  transfers between devices with their start and end apart: 10, of which 5 were waited for; matrix products, arithmetic and copies ran while one was open for 0% of the time, Pallas kernels for 28%

profile of v6, /device:TPU:2, one launch (start us, length us, event | category | flops | bytes accessed | tf_op | source)
XLA Modules:
  0.0 84.2 jit_solution(10031337484234501295)
XLA Ops:
  0.0 0.8 last_rows.1
  0.8 3.8 %collective-permute-start = (bf16[3,1280]{1,0:T(4,128)(2,1)S(1)}, bf16[3,1280]{1,0:T(4,128)(2,1)S(1)}, u32[]{:S(2)}, u32[]{:S(2)}) collective-permute-start(bf16[3,1280]{1,0:T(4,128)(2,1)S(1)} %last_rows.1), channel_id=1, source_target_pairs={{0,8},{8,16},{16,24},{24,32},{32,40},{40,48},{48,56},{56,64},{64,7... | collective-permute-start | bytes 23048 | tf_op jit(solution)/shard_map/ppermute | solution.py:27
  4.6 0.0 copy-start.2
  4.6 4.6 %local_states.1 = (bf16[512,1024]{1,0:T(8,128)(2,1)}, bf16[512,256]{1,0:T(8,128)(2,1)S(1)}, f32[16,512]{1,0:T(8,128)S(1)}, f32[16,512]{1,0:T(8,128)S(1)}, bf16[4...) custom-call(bf16[512,1024]{1,0:T(8,128)(2,1)} %x_ref.5, bf16[4,1024]{1,0:T(4,128)(2,1)} %x_taps_ref.3, ...), custom_call_target="tpu_custom_call" | custom-call | flops 5000000000 | bytes 4000000 | tf_op jit(solution)/shard_map/local_states/pallas_call | solution.py:182
  9.3 0.9 %collective-permute-done.halo_ref = bf16[3,1280]{1,0:T(4,128)(2,1)S(1)} collective-permute-done((bf16[3,1280]{1,0:T(4,128)(2,1)S(1)}, bf16[3,1280]{1,0:T(4,128)(2,1)S(1)}, u32[]{:S(2)}, u32[]{:S(2)}) %collective-permute-start) | collective-permute-done | bytes 7712 | tf_op jit(solution)/shard_map/ppermute | solution.py:27
  10.2 0.0 collective-permute-start.1
  10.2 1.9 %first_rows.1 = (bf16[512,1024]{1,0:T(8,128)(2,1)}, bf16[512,256]{1,0:T(8,128)(2,1)S(1)}, bf16[32,40,128]{2,1,0:T(8,128)(2,1)}) custom-call(bf16[512,1024]{1,0:T(8,128)(2,1)} %x_ref.5, bf16[512,256]{1,0:T(8,128)(2,1)} %maps_ref.5, bf16[3,1280]{1,0:T(4,128)(2,1)S(1)} %collective-permute-done.halo_ref, ...), custom_call_target="tpu_custom_call", output_to_operand_aliasing={{0}: (7, {}), {1}: (8, {})} | custom-call | tf_op jit(solution)/shard_map/first_rows/pallas_call | solution.py:285
  12.0 9.8 %all-to-all-start = ((bf16[32,40,128]{2,1,0:T(8,128)(2,1)}), bf16[32,40,128]{2,1,0:T(8,128)(2,1)S(1)}, u32[]{:S(2)}, u32[]{:S(2)}) async-start(bf16[32,40,128]{2,1,0:T(8,128)(2,1)} %get-tuple-element.35), calls=%async_computation | async-start | bytes 655360 | tf_op jit(solution)/shard_map/all_to_all | solution.py:651
  21.9 1.2 %copy-done = bf16[512,1024]{1,0:T(8,128)(2,1)S(1)} copy-done((bf16[512,1024]{1,0:T(8,128)(2,1)S(1)}, bf16[512,1024]{1,0:T(8,128)(2,1)}, u32[]{:S(2)}) %copy-start) | copy-done | bytes 1048600
  23.1 7.7 %local_outputs.1 = (bf16[512,1024]{1,0:T(8,128)(2,1)S(1)}, bf16[512,1024]{1,0:T(8,128)(2,1)S(1)}) custom-call(bf16[512,1024]{1,0:T(8,128)(2,1)S(1)} %copy-done, bf16[512,256]{1,0:T(8,128)(2,1)S(1)} %get-tuple-element.37.maps_ref, bf16[512,1024]{1,0:T(8,128)(2,1)} %z_ref.1, f32[16,512]{1,0:T(8,128)S(1)} %get-tuple-element.38.step_ref, ...), custom_call_target="tpu_custom_call" | custom-call | flops 8000000000 | bytes 6000000 | tf_op jit(solution)/shard_map/local_outputs/pallas_call | solution.py:400
  30.9 3.5 %all-to-all-done.got_ref = bf16[32,40,128]{2,1,0:T(8,128)(2,1)S(1)} async-done(((bf16[32,40,128]{2,1,0:T(8,128)(2,1)}), bf16[32,40,128]{2,1,0:T(8,128)(2,1)S(1)}, u32[]{:S(2)}, u32[]{:S(2)}) %all-to-all-start) | async-done | bytes 327712 | tf_op jit(solution)/shard_map/all_to_all | solution.py:651
  34.3 0.1 scan_blocks.1
  34.4 17.5 %all_to_all.10.carried_ref = bf16[32,32,128]{2,1,0:T(8,128)(2,1)S(1)} all-to-all(bf16[32,32,128]{2,1,0:T(8,128)(2,1)S(1)} %scan_blocks.1), channel_id=1, replica_groups=mesh['ctx'=32,'tp'=8] {'ctx'}, dimensions={0} | all-to-all | bytes 524288 | tf_op jit(solution)/shard_map/all_to_all | solution.py:663
  51.9 0.5 give_rows.1
  52.5 0.1 collective-permute-start.2
  52.6 3.8 %keep_rows.1 = (bf16[256,1024]{1,0:T(8,128)(2,1)S(1)}, bf16[1024,2048]{1,0:T(8,128)(2,1)S(1)}, bf16[1024,2048]{1,0:T(8,128)(2,1)S(1)}) custom-call(bf16[32,32,128]{2,1,0:T(8,128)(2,1)S(1)} %all_to_all.10.carried_ref, bf16[512,256]{1,0:T(8,128)(2,1)S(1)} %get-tuple-element.37.maps_ref, bf16[512,1024]{1,0:T(8,128)(2,1)S(1)} %get-tuple-element.43.shown_ref, ...), custom_call_target="tpu_custom_call" | custom-call | flops 1000000000 | bytes 3000000 | tf_op jit(solution)/shard_map/keep_rows/pallas_call | solution.py:484
  56.4 2.4 %left_half.1 = (bf16[64,2048]{1,0:T(8,128)(2,1)S(1)}, bf16[64,2048]{1,0:T(8,128)(2,1)S(1)}, bf16[64,2048]{1,0:T(8,128)(2,1)S(1)}, bf16[64,2048]{1,0:T(8,128)(2,1)S(1)}) custom-call(bf16[256,1024]{1,0:T(8,128)(2,1)S(1)} %get-tuple-element.46.own_ref, bf16[256,1024]{1,0:T(8,128)(2,1)S(1)} %collective-permute-done.2.other_ref, ...), custom_call_target="tpu_custom_call" | custom-call | flops 2147483648 | bytes 9000000 | tf_op jit(solution)/shard_map/left_half/pallas_call | solution.py:550
  58.8 1.7 %collective-permute-start.4 = (bf16[64,2048]{1,0:T(8,128)(2,1)S(1)}, bf16[64,2048]{1,0:T(8,128)(2,1)S(1)}, u32[]{:S(2)}, u32[]{:S(2)}) collective-permute-start(bf16[64,2048]{1,0:T(8,128)(2,1)S(1)} %get-tuple-element.52), channel_id=1, source_target_pairs={{0,2},{1,3},{2,4},{3,5},{4,6},{5,7},{6,0},{7,1},{8,10},{9,11},{10,... | collective-permute-start | bytes 786440 | tf_op jit(solution)/shard_map/ppermute | solution.py:621
  60.4 1.7 %collective-permute-start.3 = (bf16[64,2048]{1,0:T(8,128)(2,1)S(1)}, bf16[64,2048]{1,0:T(8,128)(2,1)S(1)}, u32[]{:S(2)}, u32[]{:S(2)}) collective-permute-start(bf16[64,2048]{1,0:T(8,128)(2,1)S(1)} %get-tuple-element.50), channel_id=1, source_target_pairs={{0,6},{1,7},{2,0},{3,1},{4,2},{5,3},{6,4},{7,5},{8,14},{9,15},{10,... | collective-permute-start | bytes 786440 | tf_op jit(solution)/shard_map/ppermute | solution.py:621
  62.1 4.5 %right_half.1 = (bf16[64,2048]{1,0:T(8,128)(2,1)S(1)}, bf16[64,2048]{1,0:T(8,128)(2,1)S(1)}, bf16[64,2048]{1,0:T(8,128)(2,1)S(1)}, bf16[64,2048]{1,0:T(8,128)(2,1)S(1)}) custom-call(bf16[256,1024]{1,0:T(8,128)(2,1)S(1)} %get-tuple-element.46.own_ref, bf16[256,1024]{1,0:T(8,128)(2,1)S(1)} %collective-permute-done.2.other_ref, ...), custom_call_target="tpu_custom_call" | custom-call | flops 2147483648 | bytes 9000000 | tf_op jit(solution)/shard_map/right_half/pallas_call | solution.py:550
  66.6 1.9 %collective-permute-start.6 = (bf16[64,2048]{1,0:T(8,128)(2,1)S(1)}, bf16[64,2048]{1,0:T(8,128)(2,1)S(1)}, u32[]{:S(2)}, u32[]{:S(2)}) collective-permute-start(bf16[64,2048]{1,0:T(8,128)(2,1)S(1)} %get-tuple-element.55), channel_id=1, source_target_pairs={{0,6},{1,7},{2,0},{3,1},{4,2},{5,3},{6,4},{7,5},{8,14},{9,15},{10,... | collective-permute-start | bytes 786440 | tf_op jit(solution)/shard_map/ppermute | solution.py:621
  68.5 0.2 collective-permute-start.8
  68.7 0.1 collective-permute-done.4
  68.8 0.1 add_convert_fusion.3
  68.9 0.4 collective-permute-start.5
  69.3 5.7 %collective-permute-done.6 = bf16[64,2048]{1,0:T(8,128)(2,1)S(1)} collective-permute-done((bf16[64,2048]{1,0:T(8,128)(2,1)S(1)}, bf16[64,2048]{1,0:T(8,128)(2,1)S(1)}, u32[]{:S(2)}, u32[]{:S(2)}) %collective-permute-start.6) | collective-permute-done | bytes 262176 | tf_op jit(solution)/shard_map/ppermute | solution.py:621
  75.0 0.1 add_convert_fusion.1
  75.0 2.9 %collective-permute-start.7 = (bf16[64,2048]{1,0:T(8,128)(2,1)S(1)}, bf16[64,2048]{1,0:T(8,128)(2,1)S(1)}, u32[]{:S(2)}, u32[]{:S(2)}) collective-permute-start(bf16[64,2048]{1,0:T(8,128)(2,1)S(1)} %add_convert_fusion.1), channel_id=1, source_target_pairs={{0,6},{1,7},{2,0},{3,1},{4,2},{5,3},{6,4},{7,5},{8,14},{9,15},{10,... | collective-permute-start | bytes 786440 | tf_op jit(solution)/shard_map/ppermute | solution.py:621
  78.0 5.2 %collective-permute-done.5 = bf16[64,2048]{1,0:T(8,128)(2,1)S(1)} collective-permute-done((bf16[64,2048]{1,0:T(8,128)(2,1)S(1)}, bf16[64,2048]{1,0:T(8,128)(2,1)S(1)}, u32[]{:S(2)}, u32[]{:S(2)}) %collective-permute-start.5) | collective-permute-done | bytes 262176 | tf_op jit(solution)/shard_map/ppermute | solution.py:621
  83.2 0.1 add_convert_fusion.2
  83.3 0.1 add_convert_fusion
  83.4 0.8 pad_maximum_fusion
  (9 shorter events, 0.0 us)
Async XLA Ops:
  0.8 9.4 %collective-permute-start = (bf16[3,1280]{1,0:T(4,128)(2,1)S(1)}, bf16[3,1280]{1,0:T(4,128)(2,1)S(1)}, u32[]{:S(2)}, u32[]{:S(2)}) collective-permute-start(bf16[3,1280]{1,0:T(4,128)(2,1)S(1)} %last_rows.1), channel_id=1, source_target_pairs={{0,8},{8,16},{16,24},{24,32},{32,40},{40,48},{48,56},{56,64},{64,7... | collective-permute-start | bytes 23048 | tf_op jit(solution)/shard_map/ppermute | solution.py:27
  4.6 17.3 %copy-start.2 = (f32[16]{0:T(128)S(1)}, f32[16]{0:T(128)}, u32[]{:S(2)}) copy-start(f32[16]{0:T(128)} %skip_ref.1) | copy-start | bytes 196
  10.2 42.4 %collective-permute-start.1 = (bf16[1024,4096]{1,0:T(8,128)(2,1)}, bf16[1024,4096]{1,0:T(8,128)(2,1)}, u32[]{:S(2)}, u32[]{:S(2)}) collective-permute-start(bf16[1024,4096]{1,0:T(8,128)(2,1)} %own_weight_ref.1), channel_id=1, source_target_pairs={{0,1},{1,0},{2,3},{3,2},{4,5},{5,4},{6,7},{7,6},{8,9},{9,8},{10,11... | collective-permute-start | bytes 25165832 | tf_op jit(solution)/shard_map/ppermute | solution.py:615
  12.0 22.3 %all-to-all-start = ((bf16[32,40,128]{2,1,0:T(8,128)(2,1)}), bf16[32,40,128]{2,1,0:T(8,128)(2,1)S(1)}, u32[]{:S(2)}, u32[]{:S(2)}) async-start(bf16[32,40,128]{2,1,0:T(8,128)(2,1)} %get-tuple-element.35), calls=%async_computation | async-start | bytes 655360 | tf_op jit(solution)/shard_map/all_to_all | solution.py:651
  21.9 1.2 %copy-start = (bf16[512,1024]{1,0:T(8,128)(2,1)S(1)}, bf16[512,1024]{1,0:T(8,128)(2,1)}, u32[]{:S(2)}) copy-start(bf16[512,1024]{1,0:T(8,128)(2,1)} %get-tuple-element.36.x_ref) | copy-start | bytes 3145732
  23.1 28.8 %copy-start.1 = (f32[1024]{0:T(1024)S(1)}, f32[1024]{0:T(1024)}, u32[]{:S(2)}) copy-start(f32[1024]{0:T(1024)} %param.20) | copy-start | bytes 12292
  52.5 3.9 %collective-permute-start.2 = (bf16[256,1024]{1,0:T(8,128)(2,1)S(1)}, bf16[256,1024]{1,0:T(8,128)(2,1)S(1)}, u32[]{:S(2)}, u32[]{:S(2)}) collective-permute-start(bf16[256,1024]{1,0:T(8,128)(2,1)S(1)} %give_rows.1), channel_id=1, source_target_pairs={{0,1},{1,0},{2,3},{3,2},{4,5},{5,4},{6,7},{7,6},{8,9},{9,8},{10,11... | collective-permute-start | bytes 1572872 | tf_op jit(solution)/shard_map/ppermute | solution.py:615
  58.8 10.1 %collective-permute-start.4 = (bf16[64,2048]{1,0:T(8,128)(2,1)S(1)}, bf16[64,2048]{1,0:T(8,128)(2,1)S(1)}, u32[]{:S(2)}, u32[]{:S(2)}) collective-permute-start(bf16[64,2048]{1,0:T(8,128)(2,1)S(1)} %get-tuple-element.52), channel_id=1, source_target_pairs={{0,2},{1,3},{2,4},{3,5},{4,6},{5,7},{6,0},{7,1},{8,10},{9,11},{10,... | collective-permute-start | bytes 786440 | tf_op jit(solution)/shard_map/ppermute | solution.py:621
  60.4 17.5 %collective-permute-start.3 = (bf16[64,2048]{1,0:T(8,128)(2,1)S(1)}, bf16[64,2048]{1,0:T(8,128)(2,1)S(1)}, u32[]{:S(2)}, u32[]{:S(2)}) collective-permute-start(bf16[64,2048]{1,0:T(8,128)(2,1)S(1)} %get-tuple-element.50), channel_id=1, source_target_pairs={{0,6},{1,7},{2,0},{3,1},{4,2},{5,3},{6,4},{7,5},{8,14},{9,15},{10,... | collective-permute-start | bytes 786440 | tf_op jit(solution)/shard_map/ppermute | solution.py:621
  66.6 8.4 %collective-permute-start.6 = (bf16[64,2048]{1,0:T(8,128)(2,1)S(1)}, bf16[64,2048]{1,0:T(8,128)(2,1)S(1)}, u32[]{:S(2)}, u32[]{:S(2)}) collective-permute-start(bf16[64,2048]{1,0:T(8,128)(2,1)S(1)} %get-tuple-element.55), channel_id=1, source_target_pairs={{0,6},{1,7},{2,0},{3,1},{4,2},{5,3},{6,4},{7,5},{8,14},{9,15},{10,... | collective-permute-start | bytes 786440 | tf_op jit(solution)/shard_map/ppermute | solution.py:621
  68.5 14.8 %collective-permute-start.8 = (bf16[64,2048]{1,0:T(8,128)(2,1)S(1)}, bf16[64,2048]{1,0:T(8,128)(2,1)S(1)}, u32[]{:S(2)}, u32[]{:S(2)}) collective-permute-start(bf16[64,2048]{1,0:T(8,128)(2,1)S(1)} %get-tuple-element.56), channel_id=1, source_target_pairs={{0,2},{1,3},{2,4},{3,5},{4,6},{5,7},{6,0},{7,1},{8,10},{9,11},{10,... | collective-permute-start | bytes 786440 | tf_op jit(solution)/shard_map/ppermute | solution.py:621
  68.9 14.3 %collective-permute-start.5 = (bf16[64,2048]{1,0:T(8,128)(2,1)S(1)}, bf16[64,2048]{1,0:T(8,128)(2,1)S(1)}, u32[]{:S(2)}, u32[]{:S(2)}) collective-permute-start(bf16[64,2048]{1,0:T(8,128)(2,1)S(1)} %add_convert_fusion.3), channel_id=1, source_target_pairs={{0,2},{1,3},{2,4},{3,5},{4,6},{5,7},{6,0},{7,1},{8,10},{9,11},{10,... | collective-permute-start | bytes 786440 | tf_op jit(solution)/shard_map/ppermute | solution.py:621
  75.0 8.3 %collective-permute-start.7 = (bf16[64,2048]{1,0:T(8,128)(2,1)S(1)}, bf16[64,2048]{1,0:T(8,128)(2,1)S(1)}, u32[]{:S(2)}, u32[]{:S(2)}) collective-permute-start(bf16[64,2048]{1,0:T(8,128)(2,1)S(1)} %add_convert_fusion.1), channel_id=1, source_target_pairs={{0,6},{1,7},{2,0},{3,1},{4,2},{5,3},{6,4},{7,5},{8,14},{9,15},{10,... | collective-permute-start | bytes 786440 | tf_op jit(solution)/shard_map/ppermute | solution.py:621
